TPU v7x, 128 devices: a whole 4x4x4 slice. The times are simulated.
128 devices in a mesh: seq: 16 (over z, y), head: 8 (over x, core).
Axes of the slice: x: 4, y: 4, z: 4, core: 2. Of those that a mesh axis runs over, the one named last changes fastest.
Arguments:
- normed: bfloat16 [32, 8192], P(None, 'seq'), may hold values from -6 to 6
- qkv_weight: bfloat16 [8192, 10240], P('seq', 'head'), may hold values from -0.0625 to 0.0625
- out_weight: bfloat16 [8192, 8192], P('head', 'seq'), may hold values from -0.0625 to 0.0625
- kv_cache: bfloat16 [1024, 2, 128, 1024], P('seq', None, None, 'head'), may hold values from -160 to 160
- lengths: int32 [8], replicated, may hold values from 1 to 9344, as said below
- slot_request: int32 [1024], P('seq'), may hold values from 0 to 8, as said below
- slot_block: int32 [1024], P('seq'), may hold values from 0 to 72, as said below
- send_list: int32 [16, 16, 4], P('seq'), may hold values from 0 to 64, as said below
- recv_list: int32 [16, 16, 4], P('seq'), may hold values from 0 to 64, as said below
Outputs:
- projected: bfloat16 [32, 8192], P('head', 'seq')
- moved_cache: bfloat16 [1024, 2, 128, 1024], P('seq', None, None, 'head')
Inputs may be any that keep to these rules, and one draw needn't show every extreme that they name: `lengths`: every request has at least one block; a request with n blocks has each of the block numbers 0 to n - 1 in exactly one slot, and its length lies in ((n - 1) * 128, n * 128]. `slot_request`: 8 marks an empty slot. `slot_block`: 0 in empty slots. 64 marks an unused entry, and send_list[s, e, c] is unused exactly where recv_list[e, s, c] is; every owned slot is sent exactly once and no empty slot is sent; at most 4 blocks go from one device to another, and some device receives exactly 4 from every device; after the scale-in only half of the seq devices hold blocks. `recv_list`: 64 marks an unused entry; each slot of a device is filled at most once.
All inputs are finite; a program needn't handle non-finite values.
Results may differ from a plain program's by a relative error of at most 0.025.
Values may be sent and summed in bfloat16 or wider, within the bound.
A program may use at most 128 MiB of HBM per device.

v0:
```python
import functools

import jax
import jax.numpy as jnp
from jax import lax
from jax.experimental import pallas as pl
from jax.experimental.pallas import tpu as pltpu
from jax.sharding import PartitionSpec as P

HEADS = 64
KV_HEADS = 8
HEAD = 128
POS = 4
BLOCK = 128

MESH = pl.DeviceIdType.MESH

rope_base = 500000.0
neg_large = -1e30


def _barrier(peers):
    barrier = pltpu.get_barrier_semaphore()
    for device in peers:
        pl.semaphore_signal(barrier, inc=1, device_id=device, device_id_type=MESH)
    pl.semaphore_wait(barrier, len(peers))


def _send_all(axis, n, me, src_of, land, send_sem, recv_sem):
    copies = []
    for i in range(1, n):
        peer = lax.rem(me + i, n)
        copy = pltpu.make_async_remote_copy(
            src_ref=src_of(peer),
            dst_ref=land.at[me],
            send_sem=send_sem.at[peer],
            recv_sem=recv_sem.at[me],
            device_id={axis: peer},
            device_id_type=MESH,
        )
        copy.start()
        copies.append(copy)
    return copies


def _wait_all(axis, n, me, land, send_sem, recv_sem):
    for i in range(1, n):
        src = lax.rem(me + n - i, n)
        pltpu.make_async_remote_copy(
            src_ref=land.at[src],
            dst_ref=land.at[src],
            send_sem=send_sem.at[src],
            recv_sem=recv_sem.at[src],
            device_id={axis: src},
            device_id_type=MESH,
        ).wait_recv()


def _qkv_kernel(n, part_ref, cos_ref, sin_ref, out_ref, land_a, mine, land_b, sems):
    me = lax.axis_index("seq")
    land_a[me] = part_ref[me]
    _barrier([{"seq": lax.rem(me + i, n)} for i in range(1, n)])
    sent_a = _send_all("seq", n, me, lambda p: part_ref.at[p], land_a, sems.at[0], sems.at[1])
    _wait_all("seq", n, me, land_a, sems.at[0], sems.at[1])
    total = land_a[0]
    for i in range(1, n):
        total = total + land_a[i]
    turned = pltpu.roll(total, HEAD // 2, 1)
    rotated = (total * cos_ref[...] + turned * sin_ref[...]).astype(mine.dtype)
    mine[...] = rotated
    land_b[me] = rotated
    sent_b = _send_all("seq", n, me, lambda p: mine, land_b, sems.at[2], sems.at[3])
    _wait_all("seq", n, me, land_b, sems.at[2], sems.at[3])
    for copy in sent_a + sent_b:
        copy.wait_send()
    out_ref[...] = land_b[...]


def qkv_exchange(partial, cos_table, sin_table):
    n = partial.shape[0]
    return pl.pallas_call(
        functools.partial(_qkv_kernel, n),
        out_shape=jax.ShapeDtypeStruct(partial.shape, jnp.bfloat16),
        in_specs=[pl.BlockSpec(memory_space=pltpu.VMEM)] * 3,
        out_specs=pl.BlockSpec(memory_space=pltpu.VMEM),
        scratch_shapes=[
            pltpu.VMEM(partial.shape, jnp.float32),
            pltpu.VMEM(partial.shape[1:], jnp.bfloat16),
            pltpu.VMEM(partial.shape, jnp.bfloat16),
            pltpu.SemaphoreType.DMA((4, n)),
        ],
        compiler_params=pltpu.CompilerParams(collective_id=0, has_side_effects=True),
        cost_estimate=pl.CostEstimate(
            flops=0, bytes_accessed=partial.size * 12, transcendentals=0
        ),
    )(partial, cos_table, sin_table)


def _attend_kernel(
    n, m, rows, packed_ref, w_ref, out_ref, land_p, mine, land_a, part_c, land_c, sems
):
    me = lax.axis_index("seq")
    me_h = lax.axis_index("head")
    land_p[me] = packed_ref[me]
    _barrier(
        [{"seq": lax.rem(me + i, n)} for i in range(1, n)]
        + [{"head": lax.rem(me_h + i, m)} for i in range(1, m)]
    )
    sent_p = _send_all("seq", n, me, lambda p: packed_ref.at[p], land_p, sems.at[0], sems.at[1])
    _wait_all("seq", n, me, land_p, sems.at[0], sems.at[1])
    top = land_p[0, rows : 2 * rows]
    for i in range(1, n):
        top = jnp.maximum(top, land_p[i, rows : 2 * rows])
    numerator = jnp.zeros((rows, HEAD), jnp.float32)
    denominator = jnp.zeros((rows, HEAD), jnp.float32)
    for i in range(n):
        scale = jnp.exp(land_p[i, rows : 2 * rows] - top)
        denominator = denominator + land_p[i, 2 * rows : 3 * rows] * scale
        numerator = numerator + land_p[i, :rows] * scale
    attended = (numerator / denominator).astype(mine.dtype)
    mine[...] = attended
    land_a[me] = attended
    sent_a = _send_all("seq", n, me, lambda p: mine, land_a, sems.at[2], sems.at[3])
    _wait_all("seq", n, me, land_a, sems.at[2], sems.at[3])
    heads = n // 2
    projected = None
    for g in range(heads):
        lhs = land_a[2 * g : 2 * g + 2].reshape(2 * rows, HEAD)
        term = jnp.dot(lhs, w_ref[g * HEAD : (g + 1) * HEAD, :], preferred_element_type=jnp.float32)
        projected = term if projected is None else projected + term
    per = part_c.shape[1]
    for j in range(m):
        part_c[j] = projected[j * per : (j + 1) * per]
    land_c[me_h] = part_c[me_h]
    sent_c = _send_all("head", m, me_h, lambda p: part_c.at[p], land_c, sems.at[4], sems.at[5])
    _wait_all("head", m, me_h, land_c, sems.at[4], sems.at[5])
    total = land_c[0]
    for j in range(1, m):
        total = total + land_c[j]
    for copy in sent_p + sent_a + sent_c:
        copy.wait_send()
    out_ref[...] = total.astype(out_ref.dtype)


def attend_exchange(packed, out_weight, m):
    n, three_rows, _ = packed.shape
    rows = three_rows // 3
    width = out_weight.shape[1]
    per = 2 * rows // m
    return pl.pallas_call(
        functools.partial(_attend_kernel, n, m, rows),
        out_shape=jax.ShapeDtypeStruct((per, width), jnp.bfloat16),
        in_specs=[pl.BlockSpec(memory_space=pltpu.VMEM)] * 2,
        out_specs=pl.BlockSpec(memory_space=pltpu.VMEM),
        scratch_shapes=[
            pltpu.VMEM(packed.shape, jnp.float32),
            pltpu.VMEM((rows, HEAD), jnp.bfloat16),
            pltpu.VMEM((n, rows, HEAD), jnp.bfloat16),
            pltpu.VMEM((m, per, width), jnp.float32),
            pltpu.VMEM((m, per, width), jnp.float32),
            pltpu.SemaphoreType.DMA((6, max(n, m))),
        ],
        compiler_params=pltpu.CompilerParams(collective_id=1, has_side_effects=True),
        cost_estimate=pl.CostEstimate(
            flops=2 * 2 * rows * out_weight.shape[0] * width,
            bytes_accessed=packed.size * 8 + out_weight.size * 2,
            transcendentals=n * rows * HEAD,
        ),
    )(packed, out_weight)


def rotate(values, positions):
    half_width = values.shape[-1] // 2
    frequencies = rope_base ** (
        -(jnp.arange(half_width, dtype=jnp.float32) * 2.0 / values.shape[-1])
    )
    angles = positions[..., None] * frequencies
    cosine_table = jnp.cos(angles)
    sine_table = jnp.sin(angles)
    lower_half = values[..., :half_width]
    upper_half = values[..., half_width:]
    return jnp.concatenate(
        [
            lower_half * cosine_table - upper_half * sine_table,
            upper_half * cosine_table + lower_half * sine_table,
        ],
        axis=-1,
    )


def body(
    normed,
    qkv_weight,
    out_weight,
    kv_cache,
    lengths,
    slot_request,
    slot_block,
    send_list,
    recv_list,
):
    group_size = HEADS // KV_HEADS
    scale_factor = HEAD ** (-0.5)
    requests = lengths.shape[0]
    slot_count = kv_cache.shape[0]
    n_seq = lax.axis_size("seq")
    n_head = lax.axis_size("head")
    me_seq = lax.axis_index("seq")
    rows = normed.shape[0]
    rows_per = rows // n_seq
    groups = qkv_weight.shape[1] // HEAD

    partial = jnp.dot(normed, qkv_weight, preferred_element_type=jnp.float32)
    partial = partial.reshape(n_seq, rows_per * groups, HEAD)
    row_ids = me_seq * rows_per + jnp.arange(rows_per, dtype=jnp.int32)
    row_pos = (lengths[row_ids // POS] + row_ids % POS).astype(jnp.float32)
    half_width = HEAD // 2
    frequencies = rope_base ** (-(jnp.arange(half_width, dtype=jnp.float32) * 2.0 / HEAD))
    angles = row_pos[:, None] * frequencies
    cosine, sine = jnp.cos(angles), jnp.sin(angles)
    turned_groups = (jnp.arange(groups) <= group_size)[None, :, None]
    cos_table = jnp.where(
        turned_groups, jnp.concatenate([cosine, cosine], axis=-1)[:, None, :], 1.0
    ).reshape(rows_per * groups, HEAD)
    sin_table = jnp.where(
        turned_groups, jnp.concatenate([-sine, sine], axis=-1)[:, None, :], 0.0
    ).reshape(rows_per * groups, HEAD)
    qkv = qkv_exchange(partial, cos_table, sin_table).reshape(requests, POS, 1, groups, HEAD)
    local_kv = 1

    flat_send = send_list.reshape(-1)
    outgoing = kv_cache[jnp.minimum(flat_send, slot_count - 1)]
    outgoing = outgoing.reshape((lax.axis_size("seq"), -1) + kv_cache.shape[1:])
    outgoing, qkv = lax.optimization_barrier((outgoing, qkv))
    incoming = lax.all_to_all(outgoing, "seq", split_axis=0, concat_axis=0, tiled=True)
    incoming = incoming.reshape((-1,) + kv_cache.shape[1:])
    arrivals = incoming.shape[0]
    source_of = (
        jnp.full((slot_count + 1,), arrivals, jnp.int32)
        .at[recv_list.reshape(-1)]
        .set(jnp.arange(arrivals, dtype=jnp.int32), mode="drop")[:slot_count]
    )
    moved_cache = jnp.where(
        (source_of < arrivals)[:, None, None, None],
        incoming[jnp.minimum(source_of, arrivals - 1)],
        jnp.zeros((), kv_cache.dtype),
    )
    queries = qkv[:, :, :, :group_size]
    keys_new = qkv[:, :, :, group_size]
    values_new = qkv[:, :, :, group_size + 1]

    slot_clip = jnp.minimum(slot_request, requests - 1)
    live_slot = slot_request < requests
    token_pos = slot_block[:, None] * BLOCK + jnp.arange(BLOCK, dtype=jnp.int32)[None, :]
    token_valid = (token_pos < lengths[slot_clip][:, None]) & live_slot[:, None]
    cache_view = kv_cache.reshape(slot_count, 2, BLOCK, local_kv, HEAD)
    gathered = queries[slot_clip]
    scores = (
        jnp.einsum(
            "sptgd,sbtd->stgpb", gathered, cache_view[:, 0], preferred_element_type=jnp.float32
        )
        * scale_factor
    )
    scores = jnp.where(token_valid[:, None, None, None, :], scores, neg_large)
    slot_max = jnp.max(scores, axis=-1)
    weights = jnp.where(
        token_valid[:, None, None, None, :], jnp.exp(scores - slot_max[..., None]), 0.0
    )
    slot_sum = jnp.sum(weights, axis=-1)
    slot_acc = jnp.einsum(
        "stgpb,sbtd->stgpd",
        weights.astype(jnp.bfloat16),
        cache_view[:, 1],
        preferred_element_type=jnp.float32,
    )
    flat_width = local_kv * group_size * POS
    slot_max_flat = slot_max.reshape(slot_count, flat_width)
    member = slot_request[:, None] == jnp.arange(requests, dtype=jnp.int32)[None, :]
    request_max = jnp.max(
        jnp.where(member[:, None, :], slot_max_flat[:, :, None], neg_large), axis=0
    ).T
    rescale = jnp.exp(slot_max_flat - request_max[slot_clip])
    member_float = member.astype(jnp.float32).T
    request_sum = jnp.dot(
        member_float,
        slot_sum.reshape(slot_count, flat_width) * rescale,
        precision=lax.Precision.HIGHEST,
    )
    scaled_acc = (slot_acc.reshape(slot_count, flat_width, HEAD) * rescale[:, :, None]).reshape(
        slot_count, flat_width * HEAD
    )
    request_acc = jnp.dot(member_float, scaled_acc, precision=lax.Precision.HIGHEST).reshape(
        requests, flat_width, HEAD
    )

    new_scores = (
        jnp.einsum("rptgd,rqtd->rtgpq", queries, keys_new, preferred_element_type=jnp.float32)
        * scale_factor
    )
    causal = jnp.arange(POS)[:, None] >= jnp.arange(POS)[None, :]
    new_scores = jnp.where(causal, new_scores, neg_large)
    new_max = jnp.max(new_scores, axis=-1)
    new_weights = jnp.where(causal, jnp.exp(new_scores - new_max[..., None]), 0.0)
    new_sum = jnp.sum(new_weights, axis=-1).reshape(requests, flat_width)
    new_acc = jnp.einsum(
        "rtgpq,rqtd->rtgpd",
        new_weights.astype(jnp.bfloat16),
        values_new,
        preferred_element_type=jnp.float32,
    ).reshape(requests, flat_width, HEAD)
    first = me_seq == 0
    new_max = jnp.where(first, new_max.reshape(requests, flat_width), neg_large)
    new_sum = jnp.where(first, new_sum, 0.0)
    new_acc = jnp.where(first, new_acc, 0.0)
    part_max = jnp.maximum(request_max, new_max)
    keep_old = jnp.exp(request_max - part_max)
    keep_new = jnp.exp(new_max - part_max)
    part_sum = request_sum * keep_old + new_sum * keep_new
    part_acc = request_acc * keep_old[..., None] + new_acc * keep_new[..., None]

    def by_chunk(values):
        lead = values.reshape(2, requests // 2, group_size, POS, -1).transpose(2, 0, 1, 3, 4)
        return lead.reshape(n_seq, requests * group_size * POS // n_seq, -1)

    chunk_rows = requests * flat_width // n_seq
    packed = jnp.concatenate(
        [
            by_chunk(part_acc),
            jnp.broadcast_to(by_chunk(part_max), (n_seq, chunk_rows, HEAD)),
            jnp.broadcast_to(by_chunk(part_sum), (n_seq, chunk_rows, HEAD)),
        ],
        axis=1,
    )
    projected = attend_exchange(packed, out_weight, n_head)
    return (projected, moved_cache)


def solution(mesh):
    placed = (
        P(None, "seq"),
        P("seq", "head"),
        P("head", "seq"),
        P("seq", None, None, "head"),
        P(),
        P("seq"),
        P("seq"),
        P("seq", None, None),
        P("seq", None, None),
    )
    return jax.shard_map(
        body,
        mesh=mesh,
        in_specs=placed,
        out_specs=(P("head", "seq"), P("seq", None, None, "head")),
        check_vma=False,
    )
```

profile of v0, /device:TPU:1, one launch (start us, length us, event | category | flops | bytes accessed | tf_op | source)
XLA Modules:
  0.0 122.9 jit_solution(9955489730531515780)
XLA Ops:
  0.7 1.4 %gather_fusion.1 = s32[2]{0:T(128)S(1)} fusion(s32[8]{0:T(128)} %param.13, s32[1024]{0:T(1024)S(1)} %pad_clamp_fusion.2), kind=kCustom, calls=%fused_computation.1 | custom fusion | bytes 24 | tf_op jit(solution)/shard_map/gather | solution.py:216
  2.1 0.1 fusion.40
  2.3 0.1 broadcast_in_dim.176
  2.4 1.1 fusion.45
  3.5 0.7 reshape.339.part_ref
  4.2 0.7 broadcast_select_fusion.3
  4.9 17.9 %shard_map.104 = bf16[16,20,128]{2,1,0:T(8,128)(2,1)} custom-call(f32[16,20,128]{2,1,0:T(8,128)} %reshape.339.part_ref, f32[20,128]{1,0:T(8,128)} %get-tuple-element.27.cos_ref, f32[20,128]{1,0:T(8,128)} %get-tuple-element.26.sin_ref), custom_call_target="tpu_custom_call" | custom-call | bytes 491520 | tf_op jit(solution)/shard_map/pallas_call | solution.py:81
  22.8 0.9 reshape.340
  23.7 0.7 broadcast_minimum_fusion
  24.4 0.1 copy.74
  24.5 0.1 min.25
  24.6 5.3 %gather_fusion = bf16[64,2,128,128]{3,2,1,0:T(8,128)(2,1)} fusion(bf16[64,2,128,128]{3,2,1,0:T(8,128)(2,1)} %param.12, s32[1024]{0:T(1024)S(1)} %pad_clamp_fusion.3), kind=kCustom, calls=%fused_computation | custom fusion | bytes 8388864 | tf_op jit(solution)/shard_map/gather | solution.py:232
  29.9 4.7 %all-to-all-start = ((bf16[16,4,2,128,128]{4,3,2,1,0:T(8,128)(2,1)}), bf16[16,4,2,128,128]{4,3,2,1,0:T(8,128)(2,1)}, u32[]{:S(2)}, u32[]{:S(2)}) async-start(bf16[16,4,2,128,128]{4,3,2,1,0:T(8,128)(2,1)} %bitcast.124), calls=%async_computation | async-start | bytes 8388608 | tf_op jit(solution)/shard_map/all_to_all | solution.py:235
  34.6 0.7 fusion.42
  35.2 4.8 %copy.129 = bf16[64,2,128,128]{3,2,0,1:T(8,128)(2,1)} copy(bf16[64,2,128,128]{3,2,1,0:T(8,128)(2,1)} %param.12) | data formatting | bytes 8388608 | tf_op args[3]
  40.1 4.8 %compare_select_fusion.7 = (s32[64]{0:T(128)S(1)}, s32[64]{0:T(128)S(1)}, s32[64]{0:T(128)S(1)}) fusion(s32[]{:T(128)} %bitcast.1, s32[]{:T(128)} %bitcast.2, s32[]{:T(128)} %bitcast.3, s32[]{:T(128)} %bitcast.4, s32[]{:T(128)} %bitcast.5, s32[]{:T(128)} %bitcast.6, s32[]{:T(128)} %bitcast.7, s32[]{:T(128)} %bitcast.8, s32[64]{0:T(128)S(1)} %copy-done.6, ...), kind=kLoop, calls=%fused_computation.74 | loop fusion | flops 1216 | bytes 1312 | tf_op jit(solution)/shard_map/gather | solution.py:255
  44.9 0.7 gather_fusion.2
  45.6 0.1 fusion.24
  45.7 3.1 %fusion.44 = (f32[64,8,4]{1,2,0:T(4,128)S(1)}, f32[64,1,8,4,128]{4,2,3,0,1:T(8,128)S(1)}) fusion(bf16[64,4,8,128]{3,2,1,0:T(8,128)(2,1)S(1)} %gather_fusion.2, bf16[64,2,128,1,128]{4,2,0,3,1:T(8,128)(2,1)} %bitcast.125, pred[64,128]{1,0:T(8,128)(4,1)S(1)} %fusion.24), kind=kOutput, calls=%fused_computation.110 | convolution fusion | flops 67893248 | bytes 3686400 | tf_op jit(solution)/shard_map/sptgd,sbtd->stgpb/dot_general | solution.py:259
  48.8 0.8 fusion.15
  49.6 0.7 fusion
  50.2 0.1 copy.77
  50.3 0.4 reshape.346
  50.9 0.7 iota_compare_fusion
  51.5 0.1 select_reduce_fusion
  51.7 0.7 gather_fusion.3
  52.4 0.9 fusion.41
  53.4 1.3 %fusion.43 = (f32[8,8,4]{1,2,0:T(4,128)S(1)}, f32[8,1,8,4,4]{2,4,3,0,1:T(4,128)S(1)}) fusion(bf16[8,4,1,10,128]{4,3,1,0,2:T(8,128)(2,1)} %copy-done.3, bf16[8,4,128,1]{2,0,1,3:T(8,128)(2,1)S(1)} %bitcast.137, pred[4,4]{1,0:T(4,128)(4,1)S(1)} %iota_compare_fusion.3), kind=kOutput, calls=%fused_computation.109 | convolution fusion | flops 264960 | bytes 78864 | tf_op jit(solution)/shard_map/rptgd,rqtd->rtgpq/dot_general | solution.py:297
  54.7 0.3 convolution_select_fusion
  55.1 0.1 copy.83
  55.4 0.1 bitcast_multiply_fusion.1
  55.5 0.3 mul.97
  55.9 1.7 %fusion.6 = f32[8,32,128]{2,0,1:T(8,128)S(1)} fusion(f32[8,32,128]{2,0,1:T(8,128)S(1)} %bitcast_multiply_fusion.1, f32[8,32]{0,1:T(8,128)S(1)} %copy.85, s32[64]{0:T(128)} %param.14, f32[64,4096]{1,0:T(8,128)S(1)} %reshape.346, f32[8,8,32,128]{3,2,1,0:T(8,128)S(1)} %bitcast.127), kind=kOutput, calls=%fused_computation.17 | convolution fusion | flops 25494016 | bytes 2360576 | tf_op jit(solution)/shard_map/dot_general | solution.py:292
  57.6 0.1 copy.93
  57.7 0.1 copy.94
  57.8 0.1 fusion.17
  58.0 0.1 copy.95
  58.1 0.1 fusion.8
  58.6 0.1 broadcast_in_dim.198
  58.7 0.1 broadcast_in_dim.195
  58.8 0.8 pad_maximum_fusion.packed_ref
  59.6 51.8 %shard_map.105 = bf16[4,512]{1,0:T(4,128)(2,1)} custom-call(f32[16,48,128]{2,1,0:T(8,128)} %pad_maximum_fusion.packed_ref, bf16[1024,512]{1,0:T(8,128)(2,1)} %w_ref.1), custom_call_target="tpu_custom_call" | custom-call | flops 33554432 | bytes 1835008 | tf_op jit(solution)/shard_map/pallas_call | solution.py:150
  111.4 0.1 copy.98
  111.5 0.1 reshape.357
  111.6 0.8 scatter_custom_fusion
  112.5 5.3 %gather_fusion.4 = bf16[64,2,128,128]{3,2,1,0:T(8,128)(2,1)} fusion(bf16[64,2,128,128]{3,2,1,0:T(8,128)(2,1)} %bitcast.44, s32[1024]{0:T(1024)S(1)} %pad_clamp_fusion), kind=kCustom, calls=%fused_computation.4 | custom fusion | bytes 8388864 | tf_op jit(solution)/shard_map/gather | solution.py:245
  117.7 4.5 %broadcast_select_fusion = bf16[64,2,128,128]{3,2,1,0:T(8,128)(2,1)} fusion(bf16[64,2,128,128]{3,2,1,0:T(8,128)(2,1)} %gather_fusion.4, pred[64]{0:T(512)(128)(4,1)S(1)} %slice_compare_fusion), kind=kLoop, calls=%fused_computation.7 | loop fusion | flops 2097152 | bytes 8388672 | tf_op jit(solution)/shard_map/jit(_where)/select_n | solution.py:243
  122.3 0.6 copy.133
  (63 shorter events, 1.2 us)
Async XLA Ops:
  0.6 1.8 %copy-start = (bf16[512,1280]{1,0:T(8,128)(2,1)S(1)}, bf16[512,1280]{1,0:T(8,128)(2,1)}, u32[]{:S(2)}) copy-start(bf16[512,1280]{1,0:T(8,128)(2,1)} %param.10) | copy-start | bytes 3932164
  23.7 16.3 %copy-start.3 = (bf16[8,4,1,10,128]{4,3,1,0,2:T(8,128)(2,1)}, bf16[8,4,1,10,128]{4,3,1,0,2:T(8,128)(2,1)S(1)}, u32[]{:S(2)}) copy-start(bf16[8,4,1,10,128]{4,3,1,0,2:T(8,128)(2,1)S(1)} %reshape.340) | copy-start | bytes 245764
  29.9 4.7 %copy-start.1 = (s32[8]{0:T(128)S(1)}, s32[8]{0:T(128)}, u32[]{:S(2)}) copy-start(s32[8]{0:T(128)} %param.13) | copy-start | bytes 100
  29.9 82.6 %all-to-all-start = ((bf16[16,4,2,128,128]{4,3,2,1,0:T(8,128)(2,1)}), bf16[16,4,2,128,128]{4,3,2,1,0:T(8,128)(2,1)}, u32[]{:S(2)}, u32[]{:S(2)}) async-start(bf16[16,4,2,128,128]{4,3,2,1,0:T(8,128)(2,1)} %bitcast.124), calls=%async_computation | async-start | bytes 8388608 | tf_op jit(solution)/shard_map/all_to_all | solution.py:235
  35.2 4.8 %copy-start.6 = (s32[64]{0:T(128)S(1)}, s32[64]{0:T(128)}, u32[]{:S(2)}) copy-start(s32[64]{0:T(128)} %param.14) | copy-start | bytes 772
  35.2 4.9 %copy-start.9 = (s32[64]{0:T(128)S(1)}, s32[64]{0:T(128)}, u32[]{:S(2)}) copy-start(s32[64]{0:T(128)} %param.15) | copy-start | bytes 772
  44.9 0.7 copy-start.5
  45.6 4.0 %copy-start.2 = (bf16[64,2,128,128]{3,2,0,1:T(8,128)(2,1)S(1)}, bf16[64,2,128,128]{3,2,0,1:T(8,128)(2,1)}, u32[]{:S(2)}) copy-start(bf16[64,2,128,128]{3,2,0,1:T(8,128)(2,1)} %copy.129) | copy-start | bytes 12582916
  50.8 7.4 %copy-start.7 = (s32[64]{0:T(128)S(1)}, s32[64]{0:T(128)}, u32[]{:S(2)}) copy-start(s32[64]{0:T(128)} %param.14) | copy-start | bytes 772
  52.4 59.0 %copy-start.8 = (s32[1,16,4]{1,2,0:T(4,128)S(1)}, s32[1,16,4]{1,2,0:T(4,128)}, u32[]{:S(2)}) copy-start(s32[1,16,4]{1,2,0:T(4,128)} %param.17) | copy-start | bytes 772
  117.7 4.6 %copy-start.4 = (bf16[4,512]{1,0:T(4,128)(2,1)S(1)}, bf16[4,512]{1,0:T(4,128)(2,1)}, u32[]{:S(2)}) copy-start(bf16[4,512]{1,0:T(4,128)(2,1)} %shard_map.105) | copy-start | bytes 12292
where the time goes:
time: 124 us; the launch traced here: 123 us
  Pallas kernels  69.7 us (56%)
  local copies, waits for them, and re-layouts  25.5 us (21%)
  other arithmetic  13.7 us (11%)
  matrix products  8.21 us (7%)
  starting transfers between devices  4.67 us (4%)
    pallas_call x1, Pallas kernels, attend_exchange(): pl.pallas_call(functools.partial(_attend_kernel, n, m, rows), out_shape=j...  51.8 us
    pallas_call x1, Pallas kernels, qkv_exchange(): pl.pallas_call(functools.partial(_qkv_kernel, n), out_shape=jax.ShapeDtyp...  17.9 us
    unnamed x23, local copies, waits for them, and re-layouts  5.54 us
    gather x1, local copies, waits for them, and re-layouts, body(): incoming[jnp.minimum(source_of, arrivals - 1)]  5.29 us
    gather x1, local copies, waits for them, and re-layouts, body(): outgoing = kv_cache[jnp.minimum(flat_send, slot_count - 1)]  5.25 us
    gather x1, other arithmetic, body(): token_valid = (token_pos < lengths[slot_clip][:, None]) & live_slot[:, None]  4.81 us
    all_to_all x1, starting transfers between devices, body(): lax.all_to_all(outgoing, 'seq', split_axis=0, concat_axis=0, tiled=True)  4.67 us
    select_n x1, other arithmetic, body(): jnp.where((source_of < arrivals)[:, None, None, None], incoming[jnp.minim...  4.55 us
  transfers between devices with their start and end apart: 1, of which 0 were waited for; matrix products, arithmetic and copies ran while one was open for 21% of the time, Pallas kernels for 42%

commit v1 on v0

--- a/solution.py
+++ b/solution.py
@@ -108,14 +108,14 @@
     )
     sent_p = _send_all("seq", n, me, lambda p: packed_ref.at[p], land_p, sems.at[0], sems.at[1])
     _wait_all("seq", n, me, land_p, sems.at[0], sems.at[1])
-    top = land_p[0, rows : 2 * rows]
+    top = land_p[0, rows:, 0:1]
     for i in range(1, n):
-        top = jnp.maximum(top, land_p[i, rows : 2 * rows])
+        top = jnp.maximum(top, land_p[i, rows:, 0:1])
     numerator = jnp.zeros((rows, HEAD), jnp.float32)
-    denominator = jnp.zeros((rows, HEAD), jnp.float32)
+    denominator = jnp.zeros((rows, 1), jnp.float32)
     for i in range(n):
-        scale = jnp.exp(land_p[i, rows : 2 * rows] - top)
-        denominator = denominator + land_p[i, 2 * rows : 3 * rows] * scale
+        scale = jnp.exp(land_p[i, rows:, 0:1] - top)
+        denominator = denominator + land_p[i, rows:, 1:2] * scale
         numerator = numerator + land_p[i, :rows] * scale
     attended = (numerator / denominator).astype(mine.dtype)
     mine[...] = attended
@@ -143,8 +143,8 @@
 
 
 def attend_exchange(packed, out_weight, m):
-    n, three_rows, _ = packed.shape
-    rows = three_rows // 3
+    n, two_rows, _ = packed.shape
+    rows = two_rows // 2
     width = out_weight.shape[1]
     per = 2 * rows // m
     return pl.pallas_call(
@@ -229,22 +229,24 @@
     local_kv = 1
 
     flat_send = send_list.reshape(-1)
-    outgoing = kv_cache[jnp.minimum(flat_send, slot_count - 1)]
+    outgoing = jnp.where(
+        (flat_send < slot_count)[:, None, None, None],
+        kv_cache[jnp.minimum(flat_send, slot_count - 1)],
+        jnp.zeros((), kv_cache.dtype),
+    )
     outgoing = outgoing.reshape((lax.axis_size("seq"), -1) + kv_cache.shape[1:])
     outgoing, qkv = lax.optimization_barrier((outgoing, qkv))
     incoming = lax.all_to_all(outgoing, "seq", split_axis=0, concat_axis=0, tiled=True)
     incoming = incoming.reshape((-1,) + kv_cache.shape[1:])
     arrivals = incoming.shape[0]
+    recv_flat = recv_list.reshape(-1)
     source_of = (
         jnp.full((slot_count + 1,), arrivals, jnp.int32)
-        .at[recv_list.reshape(-1)]
+        .at[recv_flat]
         .set(jnp.arange(arrivals, dtype=jnp.int32), mode="drop")[:slot_count]
     )
-    moved_cache = jnp.where(
-        (source_of < arrivals)[:, None, None, None],
-        incoming[jnp.minimum(source_of, arrivals - 1)],
-        jnp.zeros((), kv_cache.dtype),
-    )
+    zero_entry = jnp.argmax(recv_flat >= slot_count).astype(jnp.int32)
+    moved_cache = incoming[jnp.where(source_of < arrivals, source_of, zero_entry)]
     queries = qkv[:, :, :, :group_size]
     keys_new = qkv[:, :, :, group_size]
     values_new = qkv[:, :, :, group_size + 1]
@@ -323,14 +325,15 @@
         return lead.reshape(n_seq, requests * group_size * POS // n_seq, -1)
 
     chunk_rows = requests * flat_width // n_seq
-    packed = jnp.concatenate(
+    stats = jnp.concatenate(
         [
-            by_chunk(part_acc),
-            jnp.broadcast_to(by_chunk(part_max), (n_seq, chunk_rows, HEAD)),
-            jnp.broadcast_to(by_chunk(part_sum), (n_seq, chunk_rows, HEAD)),
+            by_chunk(part_max),
+            by_chunk(part_sum),
+            jnp.zeros((n_seq, chunk_rows, HEAD - 2), jnp.float32),
         ],
-        axis=1,
-    )
+        axis=-1,
+    )
+    packed = jnp.concatenate([by_chunk(part_acc), stats], axis=1)
     projected = attend_exchange(packed, out_weight, n_head)
     return (projected, moved_cache)
 

time: 124 us -> 125 us (level)
  other arithmetic: 13.7 us -> 16.7 us
  Pallas kernels: 69.7 us -> 67.3 us
    pallas_call x1, Pallas kernels: 51.8 us -> 49.5 us  [attend_exchange(): pl.pallas_call(functools.partial(_attend_kernel, n, m, rows), out_shape=j...]
  transfers between devices with their start and end apart: 1 -> 1, of which waited for: 0 -> 0; matrix products, arithmetic and copies ran while one was open for 21% -> 23% of each run, Pallas kernels for 42% -> 40%
where the time goes in v1:
time: 125 us; the launch traced here: 124 us
  Pallas kernels  67.3 us (54%)
  local copies, waits for them, and re-layouts  25.9 us (21%)
  other arithmetic  16.7 us (13%)
  matrix products  8.2 us (7%)
  starting transfers between devices  4.66 us (4%)
    pallas_call x1, Pallas kernels, attend_exchange(): pl.pallas_call(functools.partial(_attend_kernel, n, m, rows), out_shape=j...  49.5 us
    pallas_call x1, Pallas kernels, qkv_exchange(): pl.pallas_call(functools.partial(_qkv_kernel, n), out_shape=jax.ShapeDtyp...  17.9 us
    unnamed x23, local copies, waits for them, and re-layouts  5.56 us
    gather x1, local copies, waits for them, and re-layouts, body(): incoming[jnp.where(source_of < arrivals, source_of, zero_entry)]  5.29 us
    gather x1, local copies, waits for them, and re-layouts, body(): kv_cache[jnp.minimum(flat_send, slot_count - 1)]  5.28 us
    gather x1, other arithmetic, body(): token_valid = (token_pos < lengths[slot_clip][:, None]) & live_slot[:, None]  5.13 us
    all_to_all x1, starting transfers between devices, body(): lax.all_to_all(outgoing, 'seq', split_axis=0, concat_axis=0, tiled=True)  4.66 us
    select_n x1, other arithmetic, body(): jnp.where((flat_send < slot_count)[:, None, None, None], kv_cache[jnp.min...  4.5 us
  transfers between devices with their start and end apart: 1, of which 0 were waited for; matrix products, arithmetic and copies ran while one was open for 23% of the time, Pallas kernels for 40%

profile of v1, /device:TPU:1, one launch (start us, length us, event | category | flops | bytes accessed | tf_op | source)
XLA Modules:
  0.0 123.8 jit_solution(5548417342120320403)
XLA Ops:
  0.7 0.8 broadcast_minimum_fusion
  1.5 0.7 compare_bitcast_fusion
  2.2 1.3 %gather_fusion.1 = s32[2]{0:T(128)S(1)} fusion(s32[8]{0:T(128)} %param.13, s32[1024]{0:T(1024)S(1)} %pad_clamp_fusion.2), kind=kCustom, calls=%fused_computation.1 | custom fusion | bytes 24 | tf_op jit(solution)/shard_map/gather | solution.py:216
  3.5 0.1 fusion.40
  3.7 0.1 broadcast_in_dim.171
  3.8 1.1 fusion.45
  4.9 0.7 reshape.349.part_ref
  5.6 0.7 broadcast_select_fusion.3
  6.3 17.9 %shard_map.104 = bf16[16,20,128]{2,1,0:T(8,128)(2,1)} custom-call(f32[16,20,128]{2,1,0:T(8,128)} %reshape.349.part_ref, f32[20,128]{1,0:T(8,128)} %get-tuple-element.29.cos_ref, f32[20,128]{1,0:T(8,128)} %get-tuple-element.28.sin_ref), custom_call_target="tpu_custom_call" | custom-call | bytes 491520 | tf_op jit(solution)/shard_map/pallas_call | solution.py:81
  24.2 0.9 reshape.350
  25.2 0.1 min.26
  25.3 0.1 copy.84
  25.4 5.3 %gather_fusion = bf16[64,2,128,128]{3,2,1,0:T(8,128)(2,1)} fusion(bf16[64,2,128,128]{3,2,1,0:T(8,128)(2,1)} %param.12, s32[1024]{0:T(1024)S(1)} %pad_clamp_fusion.3), kind=kCustom, calls=%fused_computation | custom fusion | bytes 8388864 | tf_op jit(solution)/shard_map/gather | solution.py:234
  30.7 4.5 %broadcast_select_fusion = bf16[16,4,2,128,128]{4,3,2,1,0:T(8,128)(2,1)} fusion(bf16[16,4,2,128,128]{4,3,2,1,0:T(8,128)(2,1)} %bitcast.126, pred[16,4]{1,0:T(8,128)(4,1)S(1)} %copy.84), kind=kLoop, calls=%fused_computation.7 | loop fusion | flops 2097152 | bytes 8388672 | tf_op jit(solution)/shard_map/jit(_where)/select_n | solution.py:232
  35.2 4.7 %all-to-all-start = ((bf16[16,4,2,128,128]{4,3,2,1,0:T(8,128)(2,1)}), bf16[16,4,2,128,128]{4,3,2,1,0:T(8,128)(2,1)}, u32[]{:S(2)}, u32[]{:S(2)}) async-start(bf16[16,4,2,128,128]{4,3,2,1,0:T(8,128)(2,1)} %broadcast_select_fusion), calls=%async_computation | async-start | bytes 8388608 | tf_op jit(solution)/shard_map/all_to_all | solution.py:239
  39.9 0.7 fusion.42
  40.5 4.8 %copy.143 = bf16[64,2,128,128]{3,2,0,1:T(8,128)(2,1)} copy(bf16[64,2,128,128]{3,2,1,0:T(8,128)(2,1)} %param.12) | data formatting | bytes 8388608 | tf_op args[3]
  45.4 5.1 %compare_select_fusion.8 = (s32[64]{0:T(128)S(1)}, s32[64]{0:T(128)S(1)}, s32[64]{0:T(128)S(1)}) fusion(s32[]{:T(128)} %bitcast.1, s32[]{:T(128)} %bitcast.2, s32[]{:T(128)} %bitcast.3, s32[]{:T(128)} %bitcast.4, s32[]{:T(128)} %bitcast.5, s32[]{:T(128)} %bitcast.6, s32[]{:T(128)} %bitcast.7, s32[]{:T(128)} %bitcast.8, s32[64]{0:T(128)S(1)} %copy-done.7, ...), kind=kLoop, calls=%fused_computation.75 | loop fusion | flops 1216 | bytes 1312 | tf_op jit(solution)/shard_map/gather | solution.py:257
  50.6 0.7 gather_fusion.2
  51.3 0.1 fusion.24
  51.4 3.1 %fusion.44 = (f32[64,8,4]{1,2,0:T(4,128)S(1)}, f32[64,1,8,4,128]{4,2,3,0,1:T(8,128)S(1)}) fusion(bf16[64,4,8,128]{3,2,1,0:T(8,128)(2,1)S(1)} %gather_fusion.2, bf16[64,2,128,1,128]{4,2,0,3,1:T(8,128)(2,1)} %bitcast.127, pred[64,128]{1,0:T(8,128)(4,1)S(1)} %fusion.24), kind=kOutput, calls=%fused_computation.113 | convolution fusion | flops 67893248 | bytes 3686400 | tf_op jit(solution)/shard_map/sptgd,sbtd->stgpb/dot_general | solution.py:261
  54.4 0.8 fusion.15
  55.2 0.7 fusion
  55.9 0.6 iota_compare_fusion
  56.5 0.4 reshape.356
  57.1 0.8 select_reduce_fusion
  57.9 0.9 gather_fusion.3
  58.8 0.9 fusion.41
  59.8 1.3 %fusion.43 = (f32[8,8,4]{1,2,0:T(4,128)S(1)}, f32[8,1,8,4,4]{2,4,3,0,1:T(4,128)S(1)}) fusion(bf16[8,4,1,10,128]{4,3,1,0,2:T(8,128)(2,1)} %copy-done.3, bf16[8,4,128,1]{2,0,1,3:T(8,128)(2,1)S(1)} %bitcast.139, pred[4,4]{1,0:T(4,128)(4,1)S(1)} %iota_compare_fusion.3), kind=kOutput, calls=%fused_computation.112 | convolution fusion | flops 264960 | bytes 78864 | tf_op jit(solution)/shard_map/rptgd,rqtd->rtgpq/dot_general | solution.py:299
  61.0 0.3 convolution_select_fusion
  61.8 0.1 bitcast_multiply_fusion.1
  61.9 0.3 mul.97
  62.2 1.7 %fusion.6 = f32[8,32,128]{2,0,1:T(8,128)S(1)} fusion(f32[8,32,128]{2,0,1:T(8,128)S(1)} %bitcast_multiply_fusion.1, f32[8,32]{0,1:T(8,128)S(1)} %copy.96, s32[64]{0:T(128)} %param.14, f32[64,4096]{1,0:T(8,128)S(1)} %reshape.356, f32[8,8,32,128]{3,2,1,0:T(8,128)S(1)} %bitcast.129), kind=kOutput, calls=%fused_computation.17 | convolution fusion | flops 25494016 | bytes 2360576 | tf_op jit(solution)/shard_map/dot_general | solution.py:294
  64.0 0.1 fusion.17
  64.3 0.1 copy.104
  64.5 0.1 fusion.8
  64.7 0.1 reshape.447
  64.9 0.1 reshape.446
  65.1 0.8 maximum_maximum_fusion.packed_ref
  65.9 49.5 %shard_map.105 = bf16[4,512]{1,0:T(4,128)(2,1)} custom-call(f32[16,32,128]{2,1,0:T(8,128)} %maximum_maximum_fusion.packed_ref, bf16[1024,512]{1,0:T(8,128)(2,1)} %w_ref.1), custom_call_target="tpu_custom_call" | custom-call | flops 33554432 | bytes 1572864 | tf_op jit(solution)/shard_map/pallas_call | solution.py:150
  115.5 0.1 reshape.370
  115.6 0.1 copy.112
  115.7 0.1 ge.29
  115.8 0.8 scatter_custom_fusion
  116.6 0.7 iota_reduce_fusion
  117.2 0.6 compare_select_fusion
  117.9 5.3 %gather_fusion.4 = bf16[64,2,128,128]{3,2,1,0:T(8,128)(2,1)} fusion(bf16[64,2,128,128]{3,2,1,0:T(8,128)(2,1)} %bitcast.44, s32[1024]{0:T(1024)S(1)} %pad_clamp_fusion), kind=kCustom, calls=%fused_computation.4 | custom fusion | bytes 8388864 | tf_op jit(solution)/shard_map/gather | solution.py:249
  123.2 0.6 copy.147
  (68 shorter events, 1.6 us)
Async XLA Ops:
  0.6 3.2 %copy-start = (bf16[512,1280]{1,0:T(8,128)(2,1)S(1)}, bf16[512,1280]{1,0:T(8,128)(2,1)}, u32[]{:S(2)}) copy-start(bf16[512,1280]{1,0:T(8,128)(2,1)} %param.10) | copy-start | bytes 3932164
  25.1 20.3 %copy-start.3 = (bf16[8,4,1,10,128]{4,3,1,0,2:T(8,128)(2,1)}, bf16[8,4,1,10,128]{4,3,1,0,2:T(8,128)(2,1)S(1)}, u32[]{:S(2)}) copy-start(bf16[8,4,1,10,128]{4,3,1,0,2:T(8,128)(2,1)S(1)} %reshape.350) | copy-start | bytes 245764
  35.2 4.7 %copy-start.1 = (s32[8]{0:T(128)S(1)}, s32[8]{0:T(128)}, u32[]{:S(2)}) copy-start(s32[8]{0:T(128)} %param.13) | copy-start | bytes 100
  35.2 82.7 %all-to-all-start = ((bf16[16,4,2,128,128]{4,3,2,1,0:T(8,128)(2,1)}), bf16[16,4,2,128,128]{4,3,2,1,0:T(8,128)(2,1)}, u32[]{:S(2)}, u32[]{:S(2)}) async-start(bf16[16,4,2,128,128]{4,3,2,1,0:T(8,128)(2,1)} %broadcast_select_fusion), calls=%async_computation | async-start | bytes 8388608 | tf_op jit(solution)/shard_map/all_to_all | solution.py:239
  40.5 4.8 %copy-start.7 = (s32[64]{0:T(128)S(1)}, s32[64]{0:T(128)}, u32[]{:S(2)}) copy-start(s32[64]{0:T(128)} %param.14) | copy-start | bytes 772
  40.5 4.9 %copy-start.9 = (s32[64]{0:T(128)S(1)}, s32[64]{0:T(128)}, u32[]{:S(2)}) copy-start(s32[64]{0:T(128)} %param.15) | copy-start | bytes 772
  50.6 0.7 copy-start.6
  51.2 4.0 %copy-start.2 = (bf16[64,2,128,128]{3,2,0,1:T(8,128)(2,1)S(1)}, bf16[64,2,128,128]{3,2,0,1:T(8,128)(2,1)}, u32[]{:S(2)}) copy-start(bf16[64,2,128,128]{3,2,0,1:T(8,128)(2,1)} %copy.143) | copy-start | bytes 12582916
  57.0 7.5 %copy-start.8 = (s32[64]{0:T(128)S(1)}, s32[64]{0:T(128)}, u32[]{:S(2)}) copy-start(s32[64]{0:T(128)} %param.14) | copy-start | bytes 772
  57.9 57.5 %copy-start.5 = (s32[1,16,4]{1,2,0:T(4,128)S(1)}, s32[1,16,4]{1,2,0:T(4,128)}, u32[]{:S(2)}) copy-start(s32[1,16,4]{1,2,0:T(4,128)} %param.17) | copy-start | bytes 772
  117.9 5.3 %copy-start.4 = (bf16[4,512]{1,0:T(4,128)(2,1)S(1)}, bf16[4,512]{1,0:T(4,128)(2,1)}, u32[]{:S(2)}) copy-start(bf16[4,512]{1,0:T(4,128)(2,1)} %shard_map.105) | copy-start | bytes 12292

commit v2 on v1

--- a/solution.py
+++ b/solution.py
@@ -169,6 +169,59 @@
     )(packed, out_weight)
 
 
+def _pick_kernel(limit, index_ref, src_hbm, out_hbm, buf, sems, out_sem):
+    count = buf.shape[0]
+
+    def start(j, carry):
+        k = index_ref[j]
+
+        @pl.when(k < limit)
+        def _():
+            pltpu.make_async_copy(src_hbm.at[jnp.minimum(k, limit - 1)], buf.at[j], sems.at[j]).start()
+
+        @pl.when(k >= limit)
+        def _():
+            buf[j] = jnp.zeros(buf.shape[1:], buf.dtype)
+
+        return carry
+
+    def finish(j, carry):
+        k = index_ref[j]
+
+        @pl.when(k < limit)
+        def _():
+            pltpu.make_async_copy(src_hbm.at[0], buf.at[j], sems.at[j]).wait()
+
+        return carry
+
+    lax.fori_loop(0, count, start, 0)
+    lax.fori_loop(0, count, finish, 0)
+    out = pltpu.make_async_copy(buf, out_hbm, out_sem)
+    out.start()
+    out.wait()
+
+
+def pick_blocks(index, source, limit):
+    count = index.shape[0]
+    shape = (count,) + source.shape[1:]
+    nbytes = count * source[0].size * source.dtype.itemsize
+    return pl.pallas_call(
+        functools.partial(_pick_kernel, limit),
+        out_shape=jax.ShapeDtypeStruct(shape, source.dtype),
+        in_specs=[
+            pl.BlockSpec(memory_space=pltpu.SMEM),
+            pl.BlockSpec(memory_space=pl.ANY),
+        ],
+        out_specs=pl.BlockSpec(memory_space=pl.ANY),
+        scratch_shapes=[
+            pltpu.VMEM(shape, source.dtype),
+            pltpu.SemaphoreType.DMA((count,)),
+            pltpu.SemaphoreType.DMA(()),
+        ],
+        cost_estimate=pl.CostEstimate(flops=0, bytes_accessed=2 * nbytes, transcendentals=0),
+    )(index, source)
+
+
 def rotate(values, positions):
     half_width = values.shape[-1] // 2
     frequencies = rope_base ** (
@@ -229,24 +282,18 @@
     local_kv = 1
 
     flat_send = send_list.reshape(-1)
-    outgoing = jnp.where(
-        (flat_send < slot_count)[:, None, None, None],
-        kv_cache[jnp.minimum(flat_send, slot_count - 1)],
-        jnp.zeros((), kv_cache.dtype),
-    )
+    outgoing = pick_blocks(jnp.minimum(flat_send, slot_count - 1), kv_cache, slot_count)
     outgoing = outgoing.reshape((lax.axis_size("seq"), -1) + kv_cache.shape[1:])
     outgoing, qkv = lax.optimization_barrier((outgoing, qkv))
     incoming = lax.all_to_all(outgoing, "seq", split_axis=0, concat_axis=0, tiled=True)
     incoming = incoming.reshape((-1,) + kv_cache.shape[1:])
     arrivals = incoming.shape[0]
-    recv_flat = recv_list.reshape(-1)
     source_of = (
         jnp.full((slot_count + 1,), arrivals, jnp.int32)
-        .at[recv_flat]
+        .at[recv_list.reshape(-1)]
         .set(jnp.arange(arrivals, dtype=jnp.int32), mode="drop")[:slot_count]
     )
-    zero_entry = jnp.argmax(recv_flat >= slot_count).astype(jnp.int32)
-    moved_cache = incoming[jnp.where(source_of < arrivals, source_of, zero_entry)]
+    moved_cache = pick_blocks(source_of, incoming, arrivals)
     queries = qkv[:, :, :, :group_size]
     keys_new = qkv[:, :, :, group_size]
     values_new = qkv[:, :, :, group_size + 1]

time: 125 us -> 121 us (0.968)
  Pallas kernels: 67.3 us -> 79.5 us
  local copies, waits for them, and re-layouts: 25.9 us -> 16 us
  other arithmetic: 16.7 us -> 9.23 us
  matrix products: 8.2 us -> 9.65 us
    pallas_call x0 -> x2, Pallas kernels: none -> 12.7 us  [pick_blocks(): pl.pallas_call(functools.partial(_pick_kernel, limit), out_shape=jax.Shap...]
    gather x2 -> x0, local copies, waits for them, and re-layouts: 10.6 us -> none  [the longest x1 5.29 us: body(): incoming[jnp.where(source_of < arrivals, source_of, zero_entry)]]
    select_n x4 -> x1, other arithmetic: 5.16 us -> 0.01 us  [body(): source_of = jnp.full((slot_count + 1,), arrivals, jnp.int32).at[recv_list...]
    dot_general x1, matrix products: 0.67 us -> 2.27 us  [body(): jnp.einsum('stgpb,sbtd->stgpd', weights.astype(jnp.bfloat16), cache_view[...]
    unnamed x23 -> x21, local copies, waits for them, and re-layouts: 5.56 us -> 5.54 us
  transfers between devices with their start and end apart: 1 -> 1, of which waited for: 0 -> 0; matrix products, arithmetic and copies ran while one was open for 23% -> 23% of each run, Pallas kernels for 40% -> 41%
where the time goes in v2:
time: 121 us; the launch traced here: 120 us
  Pallas kernels  79.5 us (66%)
  local copies, waits for them, and re-layouts  16 us (13%)
  matrix products  9.65 us (8%)
  other arithmetic  9.23 us (8%)
  starting transfers between devices  4.54 us (4%)
    pallas_call x1, Pallas kernels, attend_exchange(): pl.pallas_call(functools.partial(_attend_kernel, n, m, rows), out_shape=j...  48.9 us
    pallas_call x1, Pallas kernels, qkv_exchange(): pl.pallas_call(functools.partial(_qkv_kernel, n), out_shape=jax.ShapeDtyp...  17.9 us
    pallas_call x2, Pallas kernels, pick_blocks(): pl.pallas_call(functools.partial(_pick_kernel, limit), out_shape=jax.Shap...  12.7 us
    unnamed x21, local copies, waits for them, and re-layouts  5.54 us
    gather x1, other arithmetic, body(): token_valid = (token_pos < lengths[slot_clip][:, None]) & live_slot[:, None]  4.87 us
    all_to_all x1, starting transfers between devices, body(): lax.all_to_all(outgoing, 'seq', split_axis=0, concat_axis=0, tiled=True)  4.54 us
    dot_general x1, matrix products, body(): jnp.einsum('sptgd,sbtd->stgpb', gathered, cache_view[:, 0], preferred_ele...  2.91 us
  transfers between devices with their start and end apart: 1, of which 0 were waited for; matrix products, arithmetic and copies ran while one was open for 23% of the time, Pallas kernels for 41%

profile of v2, /device:TPU:1, one launch (start us, length us, event | category | flops | bytes accessed | tf_op | source)
XLA Modules:
  0.0 120.1 jit_solution(4858427676282141581)
XLA Ops:
  0.7 1.4 %gather_fusion = s32[2]{0:T(128)S(1)} fusion(s32[8]{0:T(128)} %param.13, s32[1024]{0:T(1024)S(1)} %pad_clamp_fusion.1), kind=kCustom, calls=%fused_computation | custom fusion | bytes 24 | tf_op jit(solution)/shard_map/gather | solution.py:269
  2.1 0.1 fusion.39
  2.3 0.1 broadcast_in_dim.148
  2.4 1.1 fusion.44
  3.5 0.7 reshape.321.part_ref
  4.2 0.7 broadcast_select_fusion.2
  4.9 17.9 %shard_map.105 = bf16[16,20,128]{2,1,0:T(8,128)(2,1)} custom-call(f32[16,20,128]{2,1,0:T(8,128)} %reshape.321.part_ref, f32[20,128]{1,0:T(8,128)} %get-tuple-element.27.cos_ref, f32[20,128]{1,0:T(8,128)} %get-tuple-element.26.sin_ref), custom_call_target="tpu_custom_call" | custom-call | bytes 491520 | tf_op jit(solution)/shard_map/pallas_call | solution.py:81
  22.8 0.9 reshape.322
  23.7 0.7 broadcast_minimum_fusion
  24.4 0.1 copy.78
  24.5 0.6 min.18.index_ref
  25.1 7.2 %shard_map.104 = bf16[64,2,128,128]{3,2,1,0:T(8,128)(2,1)} custom-call(s32[64]{0:T(128)} %min.18.index_ref, bf16[64,2,128,128]{3,2,1,0:T(8,128)(2,1)} %src_hbm.1), custom_call_target="tpu_custom_call" | custom-call | bytes 8388608 | tf_op jit(solution)/shard_map/pallas_call | solution.py:208
  32.4 4.5 %all-to-all-start = ((bf16[16,4,2,128,128]{4,3,2,1,0:T(8,128)(2,1)}), bf16[16,4,2,128,128]{4,3,2,1,0:T(8,128)(2,1)}, u32[]{:S(2)}, u32[]{:S(2)}) async-start(bf16[16,4,2,128,128]{4,3,2,1,0:T(8,128)(2,1)} %bitcast.123), calls=%async_computation | async-start | bytes 8388608 | tf_op jit(solution)/shard_map/all_to_all | solution.py:288
  36.9 0.7 fusion.41
  37.6 4.8 %copy.135 = bf16[64,2,128,128]{3,2,0,1:T(8,128)(2,1)} copy(bf16[64,2,128,128]{3,2,1,0:T(8,128)(2,1)} %src_hbm.1) | data formatting | bytes 8388608 | tf_op args[3]
  42.5 4.9 %compare_select_fusion.5 = (s32[64]{0:T(128)S(1)}, s32[64]{0:T(128)S(1)}, s32[64]{0:T(128)S(1)}) fusion(s32[]{:T(128)} %bitcast.1, s32[]{:T(128)} %bitcast.2, s32[]{:T(128)} %bitcast.3, s32[]{:T(128)} %bitcast.4, s32[]{:T(128)} %bitcast.5, s32[]{:T(128)} %bitcast.6, s32[]{:T(128)} %bitcast.7, s32[]{:T(128)} %bitcast.8, s32[64]{0:T(128)S(1)} %copy-done.5, ...), kind=kLoop, calls=%fused_computation.67 | loop fusion | flops 1216 | bytes 1312 | tf_op jit(solution)/shard_map/gather | solution.py:304
  47.4 0.7 gather_fusion.1
  48.0 0.1 fusion.24
  48.1 2.9 %fusion.43 = (f32[64,8,4]{1,2,0:T(4,128)S(1)}, f32[64,1,8,4,128]{4,2,3,0,1:T(8,128)S(1)}) fusion(bf16[64,4,8,128]{3,2,1,0:T(8,128)(2,1)S(1)} %gather_fusion.1, bf16[64,2,128,1,128]{4,2,0,3,1:T(8,128)(2,1)} %bitcast.124, pred[64,128]{1,0:T(8,128)(4,1)S(1)} %fusion.24), kind=kOutput, calls=%fused_computation.101 | convolution fusion | flops 67893248 | bytes 3686400 | tf_op jit(solution)/shard_map/sptgd,sbtd->stgpb/dot_general | solution.py:308
  51.0 0.1 copy.81
  51.1 0.8 fusion.15
  51.9 2.3 %fusion = f32[64,8,4,128]{3,2,1,0:T(4,128)S(1)} fusion(bf16[64,2,128,1,128]{4,2,0,3,1:T(8,128)(2,1)} %bitcast.125, bf16[64,8,4,128]{3,1,2,0:T(8,128)(2,1)S(1)} %get-tuple-element.6), kind=kOutput, calls=%fused_computation.6 | convolution fusion | flops 67108864 | bytes 3670016 | tf_op jit(solution)/shard_map/stgpb,sbtd->stgpd/dot_general | solution.py:319
  54.2 0.4 reshape.328
  54.7 0.7 iota_compare_fusion
  55.4 0.1 select_reduce_fusion
  55.5 0.9 gather_fusion.2
  56.4 0.9 fusion.40
  57.4 1.3 %fusion.42 = (f32[8,8,4]{1,2,0:T(4,128)S(1)}, f32[8,1,8,4,4]{2,4,3,0,1:T(4,128)S(1)}) fusion(bf16[8,4,1,10,128]{4,3,1,0,2:T(8,128)(2,1)} %copy-done.2, bf16[8,4,128,1]{2,0,1,3:T(8,128)(2,1)S(1)} %bitcast.136, pred[4,4]{1,0:T(4,128)(4,1)S(1)} %iota_compare_fusion.3), kind=kOutput, calls=%fused_computation.100 | convolution fusion | flops 264960 | bytes 78864 | tf_op jit(solution)/shard_map/rptgd,rqtd->rtgpq/dot_general | solution.py:346
  58.6 0.3 convolution_select_fusion
  58.9 0.1 copy.92
  59.0 0.1 copy.87
  59.4 0.1 bitcast_multiply_fusion.1
  59.5 0.3 mul.97
  59.8 1.7 %fusion.6 = f32[8,32,128]{2,0,1:T(8,128)S(1)} fusion(f32[8,32,128]{2,0,1:T(8,128)S(1)} %bitcast_multiply_fusion.1, f32[8,32]{0,1:T(8,128)S(1)} %copy.89, s32[64]{0:T(128)} %param.14, f32[64,4096]{1,0:T(8,128)S(1)} %reshape.328, f32[8,8,32,128]{3,2,1,0:T(8,128)S(1)} %bitcast.126), kind=kOutput, calls=%fused_computation.14 | convolution fusion | flops 25494016 | bytes 2360576 | tf_op jit(solution)/shard_map/dot_general | solution.py:341
  61.6 0.1 copy.97
  61.7 0.1 copy.98
  61.8 0.1 fusion.17
  61.9 0.1 copy.99
  62.1 0.1 fusion.8
  62.3 0.1 reshape.402
  62.5 0.1 reshape.401
  62.7 0.8 maximum_maximum_fusion.packed_ref
  63.5 48.9 %shard_map.106 = bf16[4,512]{1,0:T(4,128)(2,1)} custom-call(f32[16,32,128]{2,1,0:T(8,128)} %maximum_maximum_fusion.packed_ref, bf16[1024,512]{1,0:T(8,128)(2,1)} %w_ref.1), custom_call_target="tpu_custom_call" | custom-call | flops 33554432 | bytes 1572864 | tf_op jit(solution)/shard_map/pallas_call | solution.py:150
  112.5 0.1 copy.104
  112.5 0.1 reshape.341
  112.6 1.3 %scatter_custom_fusion = s32[65]{0:T(128)} fusion(s32[64]{0:T(128)S(1)} %fusion.34, s32[64]{0:T(128)S(1)} %iota.50, s32[]{:T(128)} %constant.69.clone.1), kind=kCustom, calls=%fused_computation.91 | custom fusion | bytes 264 | tf_op jit(solution)/shard_map/scatter | solution.py:294
  113.9 5.5 %shard_map.107 = bf16[64,2,128,128]{3,2,1,0:T(8,128)(2,1)} custom-call(s32[64]{0:T(128)} %bitcast.138, bf16[64,2,128,128]{3,2,1,0:T(8,128)(2,1)} %bitcast.43.src_hbm), custom_call_target="tpu_custom_call" | custom-call | bytes 8388608 | tf_op jit(solution)/shard_map/pallas_call | solution.py:208
  119.5 0.6 copy.139
  (55 shorter events, 1.0 us)
Async XLA Ops:
  0.6 1.8 %copy-start = (bf16[512,1280]{1,0:T(8,128)(2,1)S(1)}, bf16[512,1280]{1,0:T(8,128)(2,1)}, u32[]{:S(2)}) copy-start(bf16[512,1280]{1,0:T(8,128)(2,1)} %param.10) | copy-start | bytes 3932164
  23.7 18.7 %copy-start.2 = (bf16[8,4,1,10,128]{4,3,1,0,2:T(8,128)(2,1)}, bf16[8,4,1,10,128]{4,3,1,0,2:T(8,128)(2,1)S(1)}, u32[]{:S(2)}) copy-start(bf16[8,4,1,10,128]{4,3,1,0,2:T(8,128)(2,1)S(1)} %reshape.322) | copy-start | bytes 245764
  32.3 4.6 %copy-start.1 = (s32[8]{0:T(128)S(1)}, s32[8]{0:T(128)}, u32[]{:S(2)}) copy-start(s32[8]{0:T(128)} %param.13) | copy-start | bytes 100
  32.4 81.6 %all-to-all-start = ((bf16[16,4,2,128,128]{4,3,2,1,0:T(8,128)(2,1)}), bf16[16,4,2,128,128]{4,3,2,1,0:T(8,128)(2,1)}, u32[]{:S(2)}, u32[]{:S(2)}) async-start(bf16[16,4,2,128,128]{4,3,2,1,0:T(8,128)(2,1)} %bitcast.123), calls=%async_computation | async-start | bytes 8388608 | tf_op jit(solution)/shard_map/all_to_all | solution.py:288
  37.6 4.8 %copy-start.5 = (s32[64]{0:T(128)S(1)}, s32[64]{0:T(128)}, u32[]{:S(2)}) copy-start(s32[64]{0:T(128)} %param.14) | copy-start | bytes 772
  37.6 4.9 %copy-start.8 = (s32[64]{0:T(128)S(1)}, s32[64]{0:T(128)}, u32[]{:S(2)}) copy-start(s32[64]{0:T(128)} %param.15) | copy-start | bytes 772
  47.4 0.8 copy-start.4
  54.6 7.5 %copy-start.6 = (s32[64]{0:T(128)S(1)}, s32[64]{0:T(128)}, u32[]{:S(2)}) copy-start(s32[64]{0:T(128)} %param.14) | copy-start | bytes 772
  55.5 56.9 %copy-start.7 = (s32[1,16,4]{1,2,0:T(4,128)S(1)}, s32[1,16,4]{1,2,0:T(4,128)}, u32[]{:S(2)}) copy-start(s32[1,16,4]{1,2,0:T(4,128)} %param.17) | copy-start | bytes 772
  113.9 5.5 %copy-start.3 = (bf16[4,512]{1,0:T(4,128)(2,1)S(1)}, bf16[4,512]{1,0:T(4,128)(2,1)}, u32[]{:S(2)}) copy-start(bf16[4,512]{1,0:T(4,128)(2,1)} %shard_map.106) | copy-start | bytes 12292

commit v3 on v2

--- a/solution.py
+++ b/solution.py
@@ -56,11 +56,25 @@
         ).wait_recv()
 
 
-def _qkv_kernel(n, part_ref, cos_ref, sin_ref, out_ref, land_a, mine, land_b, sems):
+def _qkv_kernel(
+    n, limit, part_ref, cos_ref, sin_ref, pick_ref, kv_hbm, out_ref, sent_hbm,
+    land_a, mine, land_b, sems, kv_vmem, sent_vmem, local_sems,
+):
     me = lax.axis_index("seq")
+    kv_in = pltpu.make_async_copy(kv_hbm, kv_vmem, local_sems.at[0])
+    kv_in.start()
     land_a[me] = part_ref[me]
     _barrier([{"seq": lax.rem(me + i, n)} for i in range(1, n)])
     sent_a = _send_all("seq", n, me, lambda p: part_ref.at[p], land_a, sems.at[0], sems.at[1])
+    kv_in.wait()
+
+    def pick(j, carry):
+        sent_vmem[j] = kv_vmem[jnp.minimum(pick_ref[j], limit - 1)]
+        return carry
+
+    lax.fori_loop(0, sent_vmem.shape[0], pick, 0)
+    kv_out = pltpu.make_async_copy(sent_vmem, sent_hbm, local_sems.at[1])
+    kv_out.start()
     _wait_all("seq", n, me, land_a, sems.at[0], sems.at[1])
     total = land_a[0]
     for i in range(1, n):
@@ -74,26 +88,37 @@
     for copy in sent_a + sent_b:
         copy.wait_send()
     out_ref[...] = land_b[...]
-
-
-def qkv_exchange(partial, cos_table, sin_table):
+    kv_out.wait()
+
+
+def qkv_exchange(partial, cos_table, sin_table, pick, kv_cache):
     n = partial.shape[0]
+    picked = (pick.shape[0],) + kv_cache.shape[1:]
     return pl.pallas_call(
-        functools.partial(_qkv_kernel, n),
-        out_shape=jax.ShapeDtypeStruct(partial.shape, jnp.bfloat16),
-        in_specs=[pl.BlockSpec(memory_space=pltpu.VMEM)] * 3,
-        out_specs=pl.BlockSpec(memory_space=pltpu.VMEM),
+        functools.partial(_qkv_kernel, n, kv_cache.shape[0]),
+        out_shape=(
+            jax.ShapeDtypeStruct(partial.shape, jnp.bfloat16),
+            jax.ShapeDtypeStruct(picked, kv_cache.dtype),
+        ),
+        in_specs=[pl.BlockSpec(memory_space=pltpu.VMEM)] * 3
+        + [pl.BlockSpec(memory_space=pltpu.SMEM), pl.BlockSpec(memory_space=pl.ANY)],
+        out_specs=(pl.BlockSpec(memory_space=pltpu.VMEM), pl.BlockSpec(memory_space=pl.ANY)),
         scratch_shapes=[
             pltpu.VMEM(partial.shape, jnp.float32),
             pltpu.VMEM(partial.shape[1:], jnp.bfloat16),
             pltpu.VMEM(partial.shape, jnp.bfloat16),
             pltpu.SemaphoreType.DMA((4, n)),
+            pltpu.VMEM(kv_cache.shape, kv_cache.dtype),
+            pltpu.VMEM(picked, kv_cache.dtype),
+            pltpu.SemaphoreType.DMA((2,)),
         ],
         compiler_params=pltpu.CompilerParams(collective_id=0, has_side_effects=True),
         cost_estimate=pl.CostEstimate(
-            flops=0, bytes_accessed=partial.size * 12, transcendentals=0
+            flops=0,
+            bytes_accessed=partial.size * 12 + 2 * kv_cache.size * kv_cache.dtype.itemsize,
+            transcendentals=0,
         ),
-    )(partial, cos_table, sin_table)
+    )(partial, cos_table, sin_table, pick, kv_cache)
 
 
 def _attend_kernel(
@@ -185,20 +210,23 @@
 
         return carry
 
-    def finish(j, carry):
+    def send(j, carry):
         k = index_ref[j]
 
         @pl.when(k < limit)
         def _():
             pltpu.make_async_copy(src_hbm.at[0], buf.at[j], sems.at[j]).wait()
 
+        pltpu.make_async_copy(buf.at[j], out_hbm.at[j], out_sem.at[j]).start()
         return carry
 
+    def finish(j, carry):
+        pltpu.make_async_copy(buf.at[j], out_hbm.at[j], out_sem.at[j]).wait()
+        return carry
+
     lax.fori_loop(0, count, start, 0)
+    lax.fori_loop(0, count, send, 0)
     lax.fori_loop(0, count, finish, 0)
-    out = pltpu.make_async_copy(buf, out_hbm, out_sem)
-    out.start()
-    out.wait()
 
 
 def pick_blocks(index, source, limit):
@@ -216,7 +244,7 @@
         scratch_shapes=[
             pltpu.VMEM(shape, source.dtype),
             pltpu.SemaphoreType.DMA((count,)),
-            pltpu.SemaphoreType.DMA(()),
+            pltpu.SemaphoreType.DMA((count,)),
         ],
         cost_estimate=pl.CostEstimate(flops=0, bytes_accessed=2 * nbytes, transcendentals=0),
     )(index, source)
@@ -278,13 +306,11 @@
     sin_table = jnp.where(
         turned_groups, jnp.concatenate([-sine, sine], axis=-1)[:, None, :], 0.0
     ).reshape(rows_per * groups, HEAD)
-    qkv = qkv_exchange(partial, cos_table, sin_table).reshape(requests, POS, 1, groups, HEAD)
+    qkv, outgoing = qkv_exchange(partial, cos_table, sin_table, send_list.reshape(-1), kv_cache)
+    qkv = qkv.reshape(requests, POS, 1, groups, HEAD)
     local_kv = 1
 
-    flat_send = send_list.reshape(-1)
-    outgoing = pick_blocks(jnp.minimum(flat_send, slot_count - 1), kv_cache, slot_count)
     outgoing = outgoing.reshape((lax.axis_size("seq"), -1) + kv_cache.shape[1:])
-    outgoing, qkv = lax.optimization_barrier((outgoing, qkv))
     incoming = lax.all_to_all(outgoing, "seq", split_axis=0, concat_axis=0, tiled=True)
     incoming = incoming.reshape((-1,) + kv_cache.shape[1:])
     arrivals = incoming.shape[0]

time: 121 us -> 112 us (0.926)
  Pallas kernels: 79.5 us -> 72.1 us
    pallas_call x2 -> x1, Pallas kernels: 12.7 us -> 5.21 us  [pick_blocks(): pl.pallas_call(functools.partial(_pick_kernel, limit), out_shape=jax.Shap...]
    unnamed x21 -> x24, local copies, waits for them, and re-layouts: 5.54 us -> 6.31 us
  transfers between devices with their start and end apart: 1 -> 1, of which waited for: 0 -> 0; matrix products, arithmetic and copies ran while one was open for 23% -> 25% of each run, Pallas kernels for 41% -> 44%
where the time goes in v3:
time: 112 us
  Pallas kernels  72.1 us (64%)
  local copies, waits for them, and re-layouts  15.8 us (14%)
  matrix products  9.65 us (9%)
  other arithmetic  8.47 us (8%)
  starting transfers between devices  4.56 us (4%)
    pallas_call x1, Pallas kernels, attend_exchange(): pl.pallas_call(functools.partial(_attend_kernel, n, m, rows), out_shape=j...  48.9 us
    pallas_call x1, Pallas kernels, qkv_exchange(): pl.pallas_call(functools.partial(_qkv_kernel, n, kv_cache.shape[0]), out_...  18 us
    unnamed x24, local copies, waits for them, and re-layouts  6.31 us
    pallas_call x1, Pallas kernels, pick_blocks(): pl.pallas_call(functools.partial(_pick_kernel, limit), out_shape=jax.Shap...  5.21 us
    gather x1, other arithmetic, body(): token_valid = (token_pos < lengths[slot_clip][:, None]) & live_slot[:, None]  4.81 us
    all_to_all x1, starting transfers between devices, body(): lax.all_to_all(outgoing, 'seq', split_axis=0, concat_axis=0, tiled=True)  4.56 us
    dot_general x1, matrix products, body(): jnp.einsum('sptgd,sbtd->stgpb', gathered, cache_view[:, 0], preferred_ele...  2.91 us
    dot_general x1, matrix products, body(): jnp.einsum('stgpb,sbtd->stgpd', weights.astype(jnp.bfloat16), cache_view[...  2.27 us
  transfers between devices with their start and end apart: 1, of which 0 were waited for; matrix products, arithmetic and copies ran while one was open for 25% of the time, Pallas kernels for 44%

profile of v3, /device:TPU:1, one launch (start us, length us, event | category | flops | bytes accessed | tf_op | source)
XLA Modules:
  0.0 111.7 jit_solution(665600755243581571)
XLA Ops:
  0.7 1.4 %gather_fusion = s32[2]{0:T(128)S(1)} fusion(s32[8]{0:T(128)} %param.13, s32[1024]{0:T(1024)S(1)} %pad_clamp_fusion.1), kind=kCustom, calls=%fused_computation | custom fusion | bytes 24 | tf_op jit(solution)/shard_map/gather | solution.py:297
  2.1 0.1 fusion.39
  2.2 0.1 pad_maximum_fusion
  2.3 0.1 broadcast_in_dim.148
  2.4 1.1 fusion.44
  3.5 0.7 reshape.320.part_ref
  4.2 0.8 copy.78
  5.0 0.6 reshape.321.pick_ref
  5.6 0.7 broadcast_select_fusion.2
  6.3 18.0 %shard_map.104 = (bf16[16,20,128]{2,1,0:T(8,128)(2,1)}, bf16[64,2,128,128]{3,2,1,0:T(8,128)(2,1)}) custom-call(f32[16,20,128]{2,1,0:T(8,128)} %reshape.320.part_ref, f32[20,128]{1,0:T(8,128)} %get-tuple-element.27.cos_ref, f32[20,128]{1,0:T(8,128)} %get-tuple-element.26.sin_ref, s32[64]{0:T(128)} %reshape.321.pick_ref, bf16[64,2,128,128]{3,2,1,0:T(8,128)(2,1)} %kv_hbm.1), custom_call_target="tpu_custom_call" | custom-call | bytes 8880128 | tf_op jit(solution)/shard_map/pallas_call | solution.py:97
  24.3 4.6 %all-to-all-start = ((bf16[16,4,2,128,128]{4,3,2,1,0:T(8,128)(2,1)}), bf16[16,4,2,128,128]{4,3,2,1,0:T(8,128)(2,1)}, u32[]{:S(2)}, u32[]{:S(2)}) async-start(bf16[16,4,2,128,128]{4,3,2,1,0:T(8,128)(2,1)} %bitcast.125), calls=%async_computation | async-start | bytes 8388608 | tf_op jit(solution)/shard_map/all_to_all | solution.py:314
  28.8 0.7 fusion.41
  29.5 4.8 %copy.135 = bf16[64,2,128,128]{3,2,0,1:T(8,128)(2,1)} copy(bf16[64,2,128,128]{3,2,1,0:T(8,128)(2,1)} %kv_hbm.1) | data formatting | bytes 8388608 | tf_op args[3]
  34.4 4.8 %compare_select_fusion.5 = (s32[64]{0:T(128)S(1)}, s32[64]{0:T(128)S(1)}, s32[64]{0:T(128)S(1)}) fusion(s32[]{:T(128)} %bitcast.1, s32[]{:T(128)} %bitcast.2, s32[]{:T(128)} %bitcast.3, s32[]{:T(128)} %bitcast.4, s32[]{:T(128)} %bitcast.5, s32[]{:T(128)} %bitcast.6, s32[]{:T(128)} %bitcast.7, s32[]{:T(128)} %bitcast.8, s32[64]{0:T(128)S(1)} %copy-done.6, ...), kind=kLoop, calls=%fused_computation.67 | loop fusion | flops 1216 | bytes 1312 | tf_op jit(solution)/shard_map/gather | solution.py:330
  39.3 0.7 gather_fusion.1
  40.0 0.1 fusion.24
  40.1 2.9 %fusion.43 = (f32[64,8,4]{1,2,0:T(4,128)S(1)}, f32[64,1,8,4,128]{4,2,3,0,1:T(8,128)S(1)}) fusion(bf16[64,4,8,128]{3,2,1,0:T(8,128)(2,1)S(1)} %gather_fusion.1, bf16[64,2,128,1,128]{4,2,0,3,1:T(8,128)(2,1)} %bitcast.123, pred[64,128]{1,0:T(8,128)(4,1)S(1)} %fusion.24), kind=kOutput, calls=%fused_computation.100 | convolution fusion | flops 67893248 | bytes 3686400 | tf_op jit(solution)/shard_map/sptgd,sbtd->stgpb/dot_general | solution.py:334
  43.0 0.1 copy.81
  43.1 0.8 fusion.15
  43.8 2.3 %fusion = f32[64,8,4,128]{3,2,1,0:T(4,128)S(1)} fusion(bf16[64,2,128,1,128]{4,2,0,3,1:T(8,128)(2,1)} %bitcast.124, bf16[64,8,4,128]{3,1,2,0:T(8,128)(2,1)S(1)} %get-tuple-element.6), kind=kOutput, calls=%fused_computation.6 | convolution fusion | flops 67108864 | bytes 3670016 | tf_op jit(solution)/shard_map/stgpb,sbtd->stgpd/dot_general | solution.py:345
  46.1 0.4 reshape.328
  46.5 0.1 copy.83
  46.6 0.7 iota_compare_fusion
  47.3 0.1 select_reduce_fusion
  47.5 0.9 gather_fusion.2
  48.3 0.9 fusion.40
  49.3 1.3 %fusion.42 = (f32[8,8,4]{1,2,0:T(4,128)S(1)}, f32[8,1,8,4,4]{2,4,3,0,1:T(4,128)S(1)}) fusion(bf16[8,4,1,10,128]{4,3,1,0,2:T(8,128)(2,1)} %copy-done.2, bf16[8,4,128,1]{2,0,1,3:T(8,128)(2,1)S(1)} %bitcast.136, pred[4,4]{1,0:T(4,128)(4,1)S(1)} %iota_compare_fusion.3), kind=kOutput, calls=%fused_computation.99 | convolution fusion | flops 264960 | bytes 78864 | tf_op jit(solution)/shard_map/rptgd,rqtd->rtgpq/dot_general | solution.py:372
  50.6 0.3 convolution_select_fusion
  50.9 0.1 copy.92
  51.0 0.1 copy.87
  51.1 0.1 copy.94
  51.3 0.1 bitcast_multiply_fusion.1
  51.4 0.3 mul.97
  51.8 1.7 %fusion.6 = f32[8,32,128]{2,0,1:T(8,128)S(1)} fusion(f32[8,32,128]{2,0,1:T(8,128)S(1)} %bitcast_multiply_fusion.1, f32[8,32]{0,1:T(8,128)S(1)} %copy.89, s32[64]{0:T(128)} %param.14, f32[64,4096]{1,0:T(8,128)S(1)} %reshape.328, f32[8,8,32,128]{3,2,1,0:T(8,128)S(1)} %bitcast.126), kind=kOutput, calls=%fused_computation.14 | convolution fusion | flops 25494016 | bytes 2360576 | tf_op jit(solution)/shard_map/dot_general | solution.py:367
  53.5 0.1 copy.97
  53.6 0.1 copy.98
  53.7 0.1 fusion.17
  53.9 0.1 copy.99
  54.0 0.1 fusion.8
  54.3 0.1 reshape.403
  54.4 0.1 reshape.402
  54.6 0.8 maximum_maximum_fusion.packed_ref
  55.4 48.9 %shard_map.105 = bf16[4,512]{1,0:T(4,128)(2,1)} custom-call(f32[16,32,128]{2,1,0:T(8,128)} %maximum_maximum_fusion.packed_ref, bf16[1024,512]{1,0:T(8,128)(2,1)} %w_ref.1), custom_call_target="tpu_custom_call" | custom-call | flops 33554432 | bytes 1572864 | tf_op jit(solution)/shard_map/pallas_call | solution.py:175
  104.4 0.1 copy.104
  104.5 0.1 reshape.341
  104.6 1.3 %scatter_custom_fusion = s32[65]{0:T(128)} fusion(s32[64]{0:T(128)S(1)} %fusion.34, s32[64]{0:T(128)S(1)} %iota.50, s32[]{:T(128)} %constant.67.clone.1), kind=kCustom, calls=%fused_computation.90 | custom fusion | bytes 264 | tf_op jit(solution)/shard_map/scatter | solution.py:320
  105.9 5.2 %shard_map.106 = bf16[64,2,128,128]{3,2,1,0:T(8,128)(2,1)} custom-call(s32[64]{0:T(128)} %bitcast.138, bf16[64,2,128,128]{3,2,1,0:T(8,128)(2,1)} %bitcast.43.src_hbm), custom_call_target="tpu_custom_call" | custom-call | bytes 8388608 | tf_op jit(solution)/shard_map/pallas_call | solution.py:236
  111.1 0.6 copy.139
  (55 shorter events, 0.8 us)
Async XLA Ops:
  0.6 1.8 %copy-start = (bf16[512,1280]{1,0:T(8,128)(2,1)S(1)}, bf16[512,1280]{1,0:T(8,128)(2,1)}, u32[]{:S(2)}) copy-start(bf16[512,1280]{1,0:T(8,128)(2,1)} %param.10) | copy-start | bytes 3932164
  24.2 4.6 %copy-start.1 = (s32[8]{0:T(128)S(1)}, s32[8]{0:T(128)}, u32[]{:S(2)}) copy-start(s32[8]{0:T(128)} %param.13) | copy-start | bytes 100
  24.3 81.6 %all-to-all-start = ((bf16[16,4,2,128,128]{4,3,2,1,0:T(8,128)(2,1)}), bf16[16,4,2,128,128]{4,3,2,1,0:T(8,128)(2,1)}, u32[]{:S(2)}, u32[]{:S(2)}) async-start(bf16[16,4,2,128,128]{4,3,2,1,0:T(8,128)(2,1)} %bitcast.125), calls=%async_computation | async-start | bytes 8388608 | tf_op jit(solution)/shard_map/all_to_all | solution.py:314
  29.5 4.8 %copy-start.3 = (bf16[16,20,128]{2,1,0:T(8,128)(2,1)S(1)}, bf16[16,20,128]{2,1,0:T(8,128)(2,1)}, u32[]{:S(2)}) copy-start(bf16[16,20,128]{2,1,0:T(8,128)(2,1)} %get-tuple-element.4) | copy-start | bytes 245764
  29.5 4.9 %copy-start.6 = (s32[64]{0:T(128)S(1)}, s32[64]{0:T(128)}, u32[]{:S(2)}) copy-start(s32[64]{0:T(128)} %param.14) | copy-start | bytes 772
  29.5 4.9 %copy-start.9 = (s32[64]{0:T(128)S(1)}, s32[64]{0:T(128)}, u32[]{:S(2)}) copy-start(s32[64]{0:T(128)} %param.15) | copy-start | bytes 772
  34.4 4.9 %copy-start.2 = (bf16[8,4,1,10,128]{4,3,1,0,2:T(8,128)(2,1)}, bf16[8,4,1,10,128]{4,3,1,0,2:T(8,128)(2,1)S(1)}, u32[]{:S(2)}) copy-start(bf16[8,4,1,10,128]{4,3,1,0,2:T(8,128)(2,1)S(1)} %reshape.322) | copy-start | bytes 245764
  39.3 0.8 copy-start.5
  46.5 7.5 %copy-start.7 = (s32[64]{0:T(128)S(1)}, s32[64]{0:T(128)}, u32[]{:S(2)}) copy-start(s32[64]{0:T(128)} %param.14) | copy-start | bytes 772
  47.5 56.9 %copy-start.8 = (s32[1,16,4]{1,2,0:T(4,128)S(1)}, s32[1,16,4]{1,2,0:T(4,128)}, u32[]{:S(2)}) copy-start(s32[1,16,4]{1,2,0:T(4,128)} %param.17) | copy-start | bytes 772
  105.9 5.2 %copy-start.4 = (bf16[4,512]{1,0:T(4,128)(2,1)S(1)}, bf16[4,512]{1,0:T(4,128)(2,1)}, u32[]{:S(2)}) copy-start(bf16[4,512]{1,0:T(4,128)(2,1)} %shard_map.105) | copy-start | bytes 12292

commit v4 on v3

--- a/solution.py
+++ b/solution.py
@@ -57,7 +57,7 @@
 
 
 def _qkv_kernel(
-    n, limit, part_ref, cos_ref, sin_ref, pick_ref, kv_hbm, out_ref, sent_hbm,
+    n, limit, part_ref, freq_ref, lengths_ref, pick_ref, kv_hbm, out_ref, sent_hbm,
     land_a, mine, land_b, sems, kv_vmem, sent_vmem, local_sems,
 ):
     me = lax.axis_index("seq")
@@ -69,7 +69,8 @@
     kv_in.wait()
 
     def pick(j, carry):
-        sent_vmem[j] = kv_vmem[jnp.minimum(pick_ref[j], limit - 1)]
+        per = pick_ref.shape[2]
+        sent_vmem[j] = kv_vmem[jnp.minimum(pick_ref[0, j // per, j % per], limit - 1)]
         return carry
 
     lax.fori_loop(0, sent_vmem.shape[0], pick, 0)
@@ -79,8 +80,19 @@
     total = land_a[0]
     for i in range(1, n):
         total = total + land_a[i]
+    g = total.shape[0] // 2
+    first_row = 2 * me
+    second_row = first_row + 1
+    pos_a = (lengths_ref[first_row // POS] + first_row % POS).astype(jnp.float32)
+    pos_b = (lengths_ref[second_row // POS] + second_row % POS).astype(jnp.float32)
+    row = lax.broadcasted_iota(jnp.int32, total.shape, 0)
+    lane = lax.broadcasted_iota(jnp.int32, total.shape, 1)
+    angle = jnp.where(row < g, pos_a, pos_b) * freq_ref[...]
+    value_row = (row == g - 1) | (row == 2 * g - 1)
+    cosine = jnp.where(value_row, 1.0, jnp.cos(angle))
+    sine = jnp.where(value_row, 0.0, jnp.where(lane < HEAD // 2, -jnp.sin(angle), jnp.sin(angle)))
     turned = pltpu.roll(total, HEAD // 2, 1)
-    rotated = (total * cos_ref[...] + turned * sin_ref[...]).astype(mine.dtype)
+    rotated = (total * cosine + turned * sine).astype(mine.dtype)
     mine[...] = rotated
     land_b[me] = rotated
     sent_b = _send_all("seq", n, me, lambda p: mine, land_b, sems.at[2], sems.at[3])
@@ -91,17 +103,18 @@
     kv_out.wait()
 
 
-def qkv_exchange(partial, cos_table, sin_table, pick, kv_cache):
+def qkv_exchange(partial, freq, lengths, pick, kv_cache):
     n = partial.shape[0]
-    picked = (pick.shape[0],) + kv_cache.shape[1:]
+    picked = (pick.size,) + kv_cache.shape[1:]
     return pl.pallas_call(
         functools.partial(_qkv_kernel, n, kv_cache.shape[0]),
         out_shape=(
             jax.ShapeDtypeStruct(partial.shape, jnp.bfloat16),
             jax.ShapeDtypeStruct(picked, kv_cache.dtype),
         ),
-        in_specs=[pl.BlockSpec(memory_space=pltpu.VMEM)] * 3
-        + [pl.BlockSpec(memory_space=pltpu.SMEM), pl.BlockSpec(memory_space=pl.ANY)],
+        in_specs=[pl.BlockSpec(memory_space=pltpu.VMEM)] * 2
+        + [pl.BlockSpec(memory_space=pltpu.SMEM)] * 2
+        + [pl.BlockSpec(memory_space=pl.ANY)],
         out_specs=(pl.BlockSpec(memory_space=pltpu.VMEM), pl.BlockSpec(memory_space=pl.ANY)),
         scratch_shapes=[
             pltpu.VMEM(partial.shape, jnp.float32),
@@ -118,7 +131,7 @@
             bytes_accessed=partial.size * 12 + 2 * kv_cache.size * kv_cache.dtype.itemsize,
             transcendentals=0,
         ),
-    )(partial, cos_table, sin_table, pick, kv_cache)
+    )(partial, freq, lengths, pick, kv_cache)
 
 
 def _attend_kernel(
@@ -293,20 +306,10 @@
 
     partial = jnp.dot(normed, qkv_weight, preferred_element_type=jnp.float32)
     partial = partial.reshape(n_seq, rows_per * groups, HEAD)
-    row_ids = me_seq * rows_per + jnp.arange(rows_per, dtype=jnp.int32)
-    row_pos = (lengths[row_ids // POS] + row_ids % POS).astype(jnp.float32)
     half_width = HEAD // 2
     frequencies = rope_base ** (-(jnp.arange(half_width, dtype=jnp.float32) * 2.0 / HEAD))
-    angles = row_pos[:, None] * frequencies
-    cosine, sine = jnp.cos(angles), jnp.sin(angles)
-    turned_groups = (jnp.arange(groups) <= group_size)[None, :, None]
-    cos_table = jnp.where(
-        turned_groups, jnp.concatenate([cosine, cosine], axis=-1)[:, None, :], 1.0
-    ).reshape(rows_per * groups, HEAD)
-    sin_table = jnp.where(
-        turned_groups, jnp.concatenate([-sine, sine], axis=-1)[:, None, :], 0.0
-    ).reshape(rows_per * groups, HEAD)
-    qkv, outgoing = qkv_exchange(partial, cos_table, sin_table, send_list.reshape(-1), kv_cache)
+    freq_row = jnp.concatenate([frequencies, frequencies])[None, :]
+    qkv, outgoing = qkv_exchange(partial, freq_row, lengths, send_list, kv_cache)
     qkv = qkv.reshape(requests, POS, 1, groups, HEAD)
     local_kv = 1
 
@@ -319,7 +322,6 @@
         .at[recv_list.reshape(-1)]
         .set(jnp.arange(arrivals, dtype=jnp.int32), mode="drop")[:slot_count]
     )
-    moved_cache = pick_blocks(source_of, incoming, arrivals)
     queries = qkv[:, :, :, :group_size]
     keys_new = qkv[:, :, :, group_size]
     values_new = qkv[:, :, :, group_size + 1]
@@ -407,7 +409,9 @@
         axis=-1,
     )
     packed = jnp.concatenate([by_chunk(part_acc), stats], axis=1)
+    source_of, packed = lax.optimization_barrier((source_of, packed))
     projected = attend_exchange(packed, out_weight, n_head)
+    moved_cache = pick_blocks(source_of, incoming, arrivals)
     return (projected, moved_cache)
 
 

time: 112 us -> 110 us (0.982)
  Pallas kernels: 72.1 us -> 70 us
    unnamed x24, local copies, waits for them, and re-layouts: 6.31 us -> 8.84 us
    pallas_call x1, Pallas kernels: 48.9 us -> 46.9 us  [attend_exchange(): pl.pallas_call(functools.partial(_attend_kernel, n, m, rows), out_shape=j...]
    gather x1 -> x0, local copies, waits for them, and re-layouts: 1.38 us -> none  [body(): row_pos = (lengths[row_ids // POS] + row_ids % POS).astype(jnp.float32)]
  transfers between devices with their start and end apart: 1 -> 1, of which waited for: 0 -> 0; matrix products, arithmetic and copies ran while one was open for 25% -> 25% of each run, Pallas kernels for 44% -> 43%
where the time goes in v4:
time: 110 us
  Pallas kernels  70 us (64%)
  local copies, waits for them, and re-layouts  16.2 us (15%)
  matrix products  9.65 us (9%)
  other arithmetic  8.21 us (7%)
  starting transfers between devices  4.55 us (4%)
    pallas_call x1, Pallas kernels, attend_exchange(): pl.pallas_call(functools.partial(_attend_kernel, n, m, rows), out_shape=j...  46.9 us
    pallas_call x1, Pallas kernels, qkv_exchange(): pl.pallas_call(functools.partial(_qkv_kernel, n, kv_cache.shape[0]), out_...  18 us
    unnamed x24, local copies, waits for them, and re-layouts  8.84 us
    pallas_call x1, Pallas kernels, pick_blocks(): pl.pallas_call(functools.partial(_pick_kernel, limit), out_shape=jax.Shap...  5.08 us
    gather x1, other arithmetic, body(): token_valid = (token_pos < lengths[slot_clip][:, None]) & live_slot[:, None]  4.89 us
    all_to_all x1, starting transfers between devices, body(): lax.all_to_all(outgoing, 'seq', split_axis=0, concat_axis=0, tiled=True)  4.55 us
    dot_general x1, matrix products, body(): jnp.einsum('sptgd,sbtd->stgpb', gathered, cache_view[:, 0], preferred_ele...  2.91 us
    dot_general x1, matrix products, body(): jnp.einsum('stgpb,sbtd->stgpd', weights.astype(jnp.bfloat16), cache_view[...  2.27 us
  transfers between devices with their start and end apart: 1, of which 0 were waited for; matrix products, arithmetic and copies ran while one was open for 25% of the time, Pallas kernels for 43%

profile of v4, /device:TPU:1, one launch (start us, length us, event | category | flops | bytes accessed | tf_op | source)
XLA Modules:
  0.0 109.5 jit_solution(11727486871424292590)
XLA Ops:
  0.7 1.3 %copy-done = bf16[512,1280]{1,0:T(8,128)(2,1)S(1)} copy-done((bf16[512,1280]{1,0:T(8,128)(2,1)S(1)}, bf16[512,1280]{1,0:T(8,128)(2,1)}, u32[]{:S(2)}) %copy-start) | copy-done | bytes 1310744
  2.0 1.1 fusion.39
  3.0 0.7 reshape.222.part_ref
  3.8 1.4 %copy.79.pick_ref = s32[1,16,4]{2,1,0:T(8,128)} copy(s32[1,16,4]{1,2,0:T(4,128)} %param.16) | data formatting | bytes 512 | tf_op args[7]
  5.1 0.6 maximum_bitcast_fusion.freq_ref
  5.7 18.0 %shard_map.104 = (bf16[16,20,128]{2,1,0:T(8,128)(2,1)}, bf16[64,2,128,128]{3,2,1,0:T(8,128)(2,1)}) custom-call(f32[16,20,128]{2,1,0:T(8,128)} %reshape.222.part_ref, f32[1,128]{1,0:T(1,128)} %maximum_bitcast_fusion.freq_ref, s32[8]{0:T(128)} %lengths_ref.1, s32[1,16,4]{2,1,0:T(8,128)} %copy.79.pick_ref, bf16[64,2,128,128]{3,2,1,0:T(8,128)(2,1)} %kv_hbm.1), custom_call_target="tpu_custom_call" | custom-call | bytes 8880128 | tf_op jit(solution)/shard_map/pallas_call | solution.py:109
  23.7 4.6 %all-to-all-start = ((bf16[16,4,2,128,128]{4,3,2,1,0:T(8,128)(2,1)}), bf16[16,4,2,128,128]{4,3,2,1,0:T(8,128)(2,1)}, u32[]{:S(2)}, u32[]{:S(2)}) async-start(bf16[16,4,2,128,128]{4,3,2,1,0:T(8,128)(2,1)} %bitcast.123), calls=%async_computation | async-start | bytes 8388608 | tf_op jit(solution)/shard_map/all_to_all | solution.py:317
  28.2 0.7 fusion.36
  28.9 4.8 %copy.135 = bf16[64,2,128,128]{3,2,0,1:T(8,128)(2,1)} copy(bf16[64,2,128,128]{3,2,1,0:T(8,128)(2,1)} %kv_hbm.1) | data formatting | bytes 8388608 | tf_op args[3]
  33.8 4.9 %compare_select_fusion.2 = (s32[64]{0:T(128)S(1)}, s32[64]{0:T(128)S(1)}, s32[64]{0:T(128)S(1)}) fusion(s32[]{:T(128)} %bitcast.2, s32[]{:T(128)} %bitcast.3, s32[]{:T(128)} %bitcast.4, s32[]{:T(128)} %bitcast.5, s32[]{:T(128)} %bitcast.6, s32[]{:T(128)} %bitcast.7, s32[]{:T(128)} %bitcast.8, s32[]{:T(128)} %bitcast.9, s32[64]{0:T(128)S(1)} %copy-done.6, ...), kind=kLoop, calls=%fused_computation.60 | loop fusion | flops 1216 | bytes 1312 | tf_op jit(solution)/shard_map/gather | solution.py:332
  38.8 0.6 copy-done.1
  39.4 0.7 gather_fusion
  40.1 0.1 fusion.24
  40.2 2.9 %fusion.38 = (f32[64,8,4]{1,2,0:T(4,128)S(1)}, f32[64,1,8,4,128]{4,2,3,0,1:T(8,128)S(1)}) fusion(bf16[64,4,8,128]{3,2,1,0:T(8,128)(2,1)S(1)} %gather_fusion, bf16[64,2,128,1,128]{4,2,0,3,1:T(8,128)(2,1)} %bitcast.121, pred[64,128]{1,0:T(8,128)(4,1)S(1)} %fusion.24), kind=kOutput, calls=%fused_computation.79 | convolution fusion | flops 67893248 | bytes 3686400 | tf_op jit(solution)/shard_map/sptgd,sbtd->stgpb/dot_general | solution.py:336
  43.1 0.8 fusion.15
  43.9 0.1 copy.82
  44.0 2.3 %fusion = f32[64,8,4,128]{3,2,1,0:T(4,128)S(1)} fusion(bf16[64,2,128,1,128]{4,2,0,3,1:T(8,128)(2,1)} %bitcast.122, bf16[64,8,4,128]{3,1,2,0:T(8,128)(2,1)S(1)} %get-tuple-element.10), kind=kOutput, calls=%fused_computation.5 | convolution fusion | flops 67108864 | bytes 3670016 | tf_op jit(solution)/shard_map/stgpb,sbtd->stgpd/dot_general | solution.py:347
  46.2 0.4 reshape.229
  46.7 0.1 copy.84
  46.8 0.7 iota_compare_fusion
  47.4 0.1 select_reduce_fusion
  47.6 0.7 gather_fusion.1
  48.3 0.9 fusion.35
  49.3 1.3 %fusion.37 = (f32[8,8,4]{1,2,0:T(4,128)S(1)}, f32[8,1,8,4,4]{2,4,3,0,1:T(4,128)S(1)}) fusion(bf16[8,4,1,10,128]{4,3,1,0,2:T(8,128)(2,1)} %copy-done.1, bf16[8,4,128,1]{2,0,1,3:T(8,128)(2,1)S(1)} %get-tuple-element.32, pred[4,4]{1,0:T(4,128)(4,1)S(1)} %iota_compare_fusion.3), kind=kOutput, calls=%fused_computation.78 | convolution fusion | flops 264960 | bytes 78864 | tf_op jit(solution)/shard_map/rptgd,rqtd->rtgpq/dot_general | solution.py:374
  50.6 0.1 copy.88
  50.8 0.1 copy.95
  50.8 0.3 convolution_select_fusion
  51.1 0.1 copy.93
  51.2 0.1 copy.90
  51.3 0.1 bitcast_multiply_fusion.1
  51.4 0.3 mul.76
  51.7 1.7 %fusion.6 = f32[8,32,128]{2,0,1:T(8,128)S(1)} fusion(f32[8,32,128]{2,0,1:T(8,128)S(1)} %bitcast_multiply_fusion.1, f32[8,32]{0,1:T(8,128)S(1)} %copy.90, s32[64]{0:T(128)} %param.14, f32[64,4096]{1,0:T(8,128)S(1)} %reshape.229, f32[8,8,32,128]{3,2,1,0:T(8,128)S(1)} %bitcast.124), kind=kOutput, calls=%fused_computation.13 | convolution fusion | flops 25494016 | bytes 2360576 | tf_op jit(solution)/shard_map/dot_general | solution.py:369
  53.5 0.1 copy.98
  53.6 0.1 copy.99
  53.7 0.1 fusion.17
  53.8 0.1 copy.100
  54.0 0.1 fusion.8
  54.1 0.1 reshape.240
  54.2 0.1 reshape.295
  54.4 0.1 reshape.294
  54.5 0.1 copy.78
  54.6 0.1 reshape.221
  54.7 0.1 pad.3.clone
  54.8 1.3 %scatter_custom_fusion = s32[65]{0:T(128)} fusion(s32[64]{0:T(128)S(1)} %fusion.31, s32[64]{0:T(128)S(1)} %iota.31, s32[]{:T(128)} %constant.14.clone.1), kind=kCustom, calls=%fused_computation.72 | custom fusion | bytes 264 | tf_op jit(solution)/shard_map/scatter | solution.py:323
  56.1 0.8 maximum_maximum_fusion.packed_ref
  56.9 46.9 %shard_map.105 = bf16[4,512]{1,0:T(4,128)(2,1)} custom-call(f32[16,32,128]{2,1,0:T(8,128)} %maximum_maximum_fusion.packed_ref, bf16[1024,512]{1,0:T(8,128)(2,1)} %w_ref.1), custom_call_target="tpu_custom_call" | custom-call | flops 33554432 | bytes 1572864 | tf_op jit(solution)/shard_map/pallas_call | solution.py:188
  103.8 5.1 %shard_map.106 = bf16[64,2,128,128]{3,2,1,0:T(8,128)(2,1)} custom-call(s32[64]{0:T(128)} %bitcast.134, bf16[64,2,128,128]{3,2,1,0:T(8,128)(2,1)} %bitcast.43.src_hbm), custom_call_target="tpu_custom_call" | custom-call | bytes 8388608 | tf_op jit(solution)/shard_map/pallas_call | solution.py:249
  108.9 0.6 copy.137
  (40 shorter events, 0.5 us)
Async XLA Ops:
  0.6 1.3 %copy-start = (bf16[512,1280]{1,0:T(8,128)(2,1)S(1)}, bf16[512,1280]{1,0:T(8,128)(2,1)}, u32[]{:S(2)}) copy-start(bf16[512,1280]{1,0:T(8,128)(2,1)} %param.10) | copy-start | bytes 3932164
  23.7 4.6 %copy-start.3 = (s32[8]{0:T(128)S(1)}, s32[8]{0:T(128)}, u32[]{:S(2)}) copy-start(s32[8]{0:T(128)} %lengths_ref.1) | copy-start | bytes 100
  23.7 80.1 %all-to-all-start = ((bf16[16,4,2,128,128]{4,3,2,1,0:T(8,128)(2,1)}), bf16[16,4,2,128,128]{4,3,2,1,0:T(8,128)(2,1)}, u32[]{:S(2)}, u32[]{:S(2)}) async-start(bf16[16,4,2,128,128]{4,3,2,1,0:T(8,128)(2,1)} %bitcast.123), calls=%async_computation | async-start | bytes 8388608 | tf_op jit(solution)/shard_map/all_to_all | solution.py:317
  28.9 4.9 %copy-start.6 = (s32[64]{0:T(128)S(1)}, s32[64]{0:T(128)}, u32[]{:S(2)}) copy-start(s32[64]{0:T(128)} %param.14) | copy-start | bytes 772
  28.9 4.9 %copy-start.9 = (s32[64]{0:T(128)S(1)}, s32[64]{0:T(128)}, u32[]{:S(2)}) copy-start(s32[64]{0:T(128)} %param.15) | copy-start | bytes 772
  28.9 9.8 %copy-start.2 = (bf16[16,20,128]{2,1,0:T(8,128)(2,1)S(1)}, bf16[16,20,128]{2,1,0:T(8,128)(2,1)}, u32[]{:S(2)}) copy-start(bf16[16,20,128]{2,1,0:T(8,128)(2,1)} %get-tuple-element.6) | copy-start | bytes 245764
  38.7 4.4 %copy-start.5 = (s32[1024]{0:T(1024)}, s32[1024]{0:T(1024)S(1)}, u32[]{:S(2)}) copy-start(s32[1024]{0:T(1024)S(1)} %pad_clamp_fusion) | copy-start | bytes 12292
  38.8 0.7 copy-start.1
  46.7 7.3 %copy-start.7 = (s32[64]{0:T(128)S(1)}, s32[64]{0:T(128)}, u32[]{:S(2)}) copy-start(s32[64]{0:T(128)} %param.14) | copy-start | bytes 772
  46.7 7.9 %copy-start.8 = (s32[1,16,4]{1,2,0:T(4,128)S(1)}, s32[1,16,4]{1,2,0:T(4,128)}, u32[]{:S(2)}) copy-start(s32[1,16,4]{1,2,0:T(4,128)} %param.17) | copy-start | bytes 772
  103.8 5.1 %copy-start.4 = (bf16[4,512]{1,0:T(4,128)(2,1)S(1)}, bf16[4,512]{1,0:T(4,128)(2,1)}, u32[]{:S(2)}) copy-start(bf16[4,512]{1,0:T(4,128)(2,1)} %shard_map.105) | copy-start | bytes 12292

commit v5 on v4

--- a/solution.py
+++ b/solution.py
@@ -1,6 +1,7 @@
 import functools
 
 import jax
+import numpy as np
 import jax.numpy as jnp
 from jax import lax
 from jax.experimental import pallas as pl
@@ -135,26 +136,30 @@
 
 
 def _attend_kernel(
-    n, m, rows, packed_ref, w_ref, out_ref, land_p, mine, land_a, part_c, land_c, sems
+    n, m, rows, acc_ref, stats_ref, w_ref, out_ref, land_p, land_s, mine, land_a, part_c, land_c,
+    sems,
 ):
     me = lax.axis_index("seq")
     me_h = lax.axis_index("head")
-    land_p[me] = packed_ref[me]
+    land_p[me] = acc_ref[me]
+    land_s[me] = stats_ref[me]
     _barrier(
         [{"seq": lax.rem(me + i, n)} for i in range(1, n)]
         + [{"head": lax.rem(me_h + i, m)} for i in range(1, m)]
     )
-    sent_p = _send_all("seq", n, me, lambda p: packed_ref.at[p], land_p, sems.at[0], sems.at[1])
+    sent_p = _send_all("seq", n, me, lambda p: acc_ref.at[p], land_p, sems.at[0], sems.at[1])
+    sent_s = _send_all("seq", n, me, lambda p: stats_ref.at[p], land_s, sems.at[6], sems.at[7])
+    _wait_all("seq", n, me, land_s, sems.at[6], sems.at[7])
     _wait_all("seq", n, me, land_p, sems.at[0], sems.at[1])
-    top = land_p[0, rows:, 0:1]
+    top = land_s[0, :, 0:1]
     for i in range(1, n):
-        top = jnp.maximum(top, land_p[i, rows:, 0:1])
+        top = jnp.maximum(top, land_s[i, :, 0:1])
     numerator = jnp.zeros((rows, HEAD), jnp.float32)
     denominator = jnp.zeros((rows, 1), jnp.float32)
     for i in range(n):
-        scale = jnp.exp(land_p[i, rows:, 0:1] - top)
-        denominator = denominator + land_p[i, rows:, 1:2] * scale
-        numerator = numerator + land_p[i, :rows] * scale
+        scale = jnp.exp(land_s[i, :, 0:1] - top)
+        denominator = denominator + land_s[i, :, 1:2] * scale
+        numerator = numerator + land_p[i].astype(jnp.float32) * scale
     attended = (numerator / denominator).astype(mine.dtype)
     mine[...] = attended
     land_a[me] = attended
@@ -175,36 +180,36 @@
     total = land_c[0]
     for j in range(1, m):
         total = total + land_c[j]
-    for copy in sent_p + sent_a + sent_c:
+    for copy in sent_p + sent_s + sent_a + sent_c:
         copy.wait_send()
     out_ref[...] = total.astype(out_ref.dtype)
 
 
-def attend_exchange(packed, out_weight, m):
-    n, two_rows, _ = packed.shape
-    rows = two_rows // 2
+def attend_exchange(acc, stats, out_weight, m):
+    n, rows, _ = acc.shape
     width = out_weight.shape[1]
     per = 2 * rows // m
     return pl.pallas_call(
         functools.partial(_attend_kernel, n, m, rows),
         out_shape=jax.ShapeDtypeStruct((per, width), jnp.bfloat16),
-        in_specs=[pl.BlockSpec(memory_space=pltpu.VMEM)] * 2,
+        in_specs=[pl.BlockSpec(memory_space=pltpu.VMEM)] * 3,
         out_specs=pl.BlockSpec(memory_space=pltpu.VMEM),
         scratch_shapes=[
-            pltpu.VMEM(packed.shape, jnp.float32),
+            pltpu.VMEM(acc.shape, acc.dtype),
+            pltpu.VMEM(stats.shape, jnp.float32),
             pltpu.VMEM((rows, HEAD), jnp.bfloat16),
             pltpu.VMEM((n, rows, HEAD), jnp.bfloat16),
             pltpu.VMEM((m, per, width), jnp.float32),
             pltpu.VMEM((m, per, width), jnp.float32),
-            pltpu.SemaphoreType.DMA((6, max(n, m))),
+            pltpu.SemaphoreType.DMA((8, max(n, m))),
         ],
         compiler_params=pltpu.CompilerParams(collective_id=1, has_side_effects=True),
         cost_estimate=pl.CostEstimate(
             flops=2 * 2 * rows * out_weight.shape[0] * width,
-            bytes_accessed=packed.size * 8 + out_weight.size * 2,
+            bytes_accessed=acc.size * 4 + stats.size * 8 + out_weight.size * 2,
             transcendentals=n * rows * HEAD,
         ),
-    )(packed, out_weight)
+    )(acc, stats, out_weight)
 
 
 def _pick_kernel(limit, index_ref, src_hbm, out_hbm, buf, sems, out_sem):
@@ -307,8 +312,10 @@
     partial = jnp.dot(normed, qkv_weight, preferred_element_type=jnp.float32)
     partial = partial.reshape(n_seq, rows_per * groups, HEAD)
     half_width = HEAD // 2
-    frequencies = rope_base ** (-(jnp.arange(half_width, dtype=jnp.float32) * 2.0 / HEAD))
-    freq_row = jnp.concatenate([frequencies, frequencies])[None, :]
+    frequencies = np.float32(rope_base) ** (
+        -(np.arange(half_width, dtype=np.float32) * np.float32(2.0) / np.float32(HEAD))
+    )
+    freq_row = jnp.asarray(np.concatenate([frequencies, frequencies])[None, :].astype(np.float32))
     qkv, outgoing = qkv_exchange(partial, freq_row, lengths, send_list, kv_cache)
     qkv = qkv.reshape(requests, POS, 1, groups, HEAD)
     local_kv = 1
@@ -408,9 +415,9 @@
         ],
         axis=-1,
     )
-    packed = jnp.concatenate([by_chunk(part_acc), stats], axis=1)
-    source_of, packed = lax.optimization_barrier((source_of, packed))
-    projected = attend_exchange(packed, out_weight, n_head)
+    acc_chunks = by_chunk(part_acc).astype(jnp.bfloat16)
+    source_of, acc_chunks, stats = lax.optimization_barrier((source_of, acc_chunks, stats))
+    projected = attend_exchange(acc_chunks, stats, out_weight, n_head)
     moved_cache = pick_blocks(source_of, incoming, arrivals)
     return (projected, moved_cache)
 

time: 110 us -> 108 us (0.982)
  Pallas kernels: 70 us -> 66.2 us
    pallas_call x1, Pallas kernels: 46.9 us -> 43.2 us  [attend_exchange(): pl.pallas_call(functools.partial(_attend_kernel, n, m, rows), out_shape=j...]
    unnamed x24 -> x22, local copies, waits for them, and re-layouts: 8.84 us -> 6.99 us
    reduce_sum x0 -> x1, other arithmetic: none -> 1.25 us  [body(): slot_sum = jnp.sum(weights, axis=-1)]
  transfers between devices with their start and end apart: 1 -> 1, of which waited for: 0 -> 0; matrix products, arithmetic and copies ran while one was open for 25% -> 29% of each run, Pallas kernels for 43% -> 40%
where the time goes in v5:
time: 108 us; the launch traced here: 107 us
  Pallas kernels  66.2 us (61%)
  local copies, waits for them, and re-layouts  17 us (16%)
  matrix products  9.64 us (9%)
  other arithmetic  8.85 us (8%)
  starting transfers between devices  4.68 us (4%)
    pallas_call x1, Pallas kernels, attend_exchange(): pl.pallas_call(functools.partial(_attend_kernel, n, m, rows), out_shape=j...  43.2 us
    pallas_call x1, Pallas kernels, qkv_exchange(): pl.pallas_call(functools.partial(_qkv_kernel, n, kv_cache.shape[0]), out_...  18 us
    unnamed x22, local copies, waits for them, and re-layouts  6.99 us
    pallas_call x1, Pallas kernels, pick_blocks(): pl.pallas_call(functools.partial(_pick_kernel, limit), out_shape=jax.Shap...  5.08 us
    gather x1, other arithmetic, body(): token_valid = (token_pos < lengths[slot_clip][:, None]) & live_slot[:, None]  5.02 us
    all_to_all x1, starting transfers between devices, body(): lax.all_to_all(outgoing, 'seq', split_axis=0, concat_axis=0, tiled=True)  4.68 us
    dot_general x1, matrix products, body(): jnp.einsum('sptgd,sbtd->stgpb', gathered, cache_view[:, 0], preferred_ele...  2.91 us
    dot_general x1, matrix products, body(): jnp.einsum('stgpb,sbtd->stgpd', weights.astype(jnp.bfloat16), cache_view[...  2.42 us
  transfers between devices with their start and end apart: 1, of which 0 were waited for; matrix products, arithmetic and copies ran while one was open for 29% of the time, Pallas kernels for 40%

profile of v5, /device:TPU:1, one launch (start us, length us, event | category | flops | bytes accessed | tf_op | source)
XLA Modules:
  0.0 107.4 jit_solution(8113245234361842899)
XLA Ops:
  0.6 1.4 %copy.80.pick_ref = s32[1,16,4]{2,1,0:T(8,128)} copy(s32[1,16,4]{1,2,0:T(4,128)} %param.17) | data formatting | bytes 512 | tf_op args[7]
  2.1 1.1 %fusion.40 = f32[32,1280]{1,0:T(8,128)S(1)} fusion(bf16[32,512]{1,0:T(8,128)(2,1)} %param.10, bf16[512,1280]{1,0:T(8,128)(2,1)S(1)} %copy-done), kind=kOutput, calls=%fused_computation.79 | convolution fusion | flops 41943040 | bytes 1507328 | tf_op jit(solution)/shard_map/dot_general | solution.py:312
  3.2 0.7 reshape.220.part_ref
  3.9 18.0 %shard_map.113 = (bf16[16,20,128]{2,1,0:T(8,128)(2,1)}, bf16[64,2,128,128]{3,2,1,0:T(8,128)(2,1)}) custom-call(f32[16,20,128]{2,1,0:T(8,128)} %reshape.220.part_ref, f32[1,128]{1,0:T(1,128)} %constant.12.clone.freq_ref, s32[8]{0:T(128)} %lengths_ref.1, s32[1,16,4]{2,1,0:T(8,128)} %copy.80.pick_ref, bf16[64,2,128,128]{3,2,1,0:T(8,128)(2,1)} %kv_hbm.1), custom_call_target="tpu_custom_call" | custom-call | bytes 8880128 | tf_op jit(solution)/shard_map/pallas_call | solution.py:110
  21.9 4.7 %all-to-all-start = ((bf16[16,4,2,128,128]{4,3,2,1,0:T(8,128)(2,1)}), bf16[16,4,2,128,128]{4,3,2,1,0:T(8,128)(2,1)}, u32[]{:S(2)}, u32[]{:S(2)}) async-start(bf16[16,4,2,128,128]{4,3,2,1,0:T(8,128)(2,1)} %bitcast.125), calls=%async_computation | async-start | bytes 8388608 | tf_op jit(solution)/shard_map/all_to_all | solution.py:324
  26.7 0.4 fusion.38
  27.1 0.1 fusion.18
  27.3 0.3 convolution_select_fusion
  27.6 0.7 fusion.37
  28.3 4.8 %copy.136 = bf16[64,2,128,128]{3,2,0,1:T(8,128)(2,1)} copy(bf16[64,2,128,128]{3,2,1,0:T(8,128)(2,1)} %kv_hbm.1) | data formatting | bytes 8388608 | tf_op args[3]
  33.1 0.1 copy.79
  33.2 0.6 reshape.219
  33.8 0.1 copy.101
  33.9 0.7 copy.102
  34.5 0.1 copy.89
  34.6 0.7 copy.90
  35.3 0.1 copy.94
  35.4 5.0 %compare_select_fusion.2 = (s32[64]{0:T(128)S(1)}, s32[64]{0:T(128)S(1)}, s32[64]{0:T(128)S(1)}) fusion(s32[]{:T(128)} %bitcast.2, s32[]{:T(128)} %bitcast.3, s32[]{:T(128)} %bitcast.4, s32[]{:T(128)} %bitcast.5, s32[]{:T(128)} %bitcast.6, s32[]{:T(128)} %bitcast.7, s32[]{:T(128)} %bitcast.8, s32[]{:T(128)} %bitcast.9, s32[64]{0:T(128)S(1)} %copy-done.5, ...), kind=kLoop, calls=%fused_computation.61 | loop fusion | flops 1216 | bytes 1312 | tf_op jit(solution)/shard_map/gather | solution.py:339
  40.4 0.7 gather_fusion
  41.1 0.1 fusion.25
  41.2 2.9 %fusion.39 = (f32[64,8,4]{1,2,0:T(4,128)S(1)}, f32[64,1,8,4,128]{4,2,3,0,1:T(8,128)S(1)}) fusion(bf16[64,4,8,128]{3,2,1,0:T(8,128)(2,1)S(1)} %gather_fusion, bf16[64,2,128,1,128]{4,2,0,3,1:T(8,128)(2,1)} %bitcast.122, pred[64,128]{1,0:T(8,128)(4,1)S(1)} %fusion.25), kind=kOutput, calls=%fused_computation.78 | convolution fusion | flops 67893248 | bytes 3686400 | tf_op jit(solution)/shard_map/sptgd,sbtd->stgpb/dot_general | solution.py:343
  44.1 0.1 copy.83
  44.2 1.2 %fusion.14 = (f32[64,8,4]{1,2,0:T(4,128)S(1)}, bf16[64,8,4,128]{3,1,2,0:T(8,128)(2,1)}) fusion(f32[64,1,8,4,128]{4,2,3,0,1:T(8,128)S(1)} %get-tuple-element.32, f32[64,8,4]{1,2,0:T(4,128)S(1)} %get-tuple-element.31, pred[64,128]{1,0:T(8,128)(4,1)S(1)} %fusion.25), kind=kLoop, calls=%fused_computation.26 | loop fusion | flops 1046528 | bytes 1597440 | tf_op jit(solution)/shard_map/reduce_sum | solution.py:353
  45.5 0.7 copy.99
  46.2 2.4 %fusion = f32[64,8,4,128]{3,2,1,0:T(4,128)S(1)} fusion(bf16[64,2,128,1,128]{4,2,0,3,1:T(8,128)(2,1)} %bitcast.123, bf16[64,8,4,128]{3,1,2,0:T(8,128)(2,1)} %get-tuple-element.13), kind=kOutput, calls=%fused_computation.5 | convolution fusion | flops 67108864 | bytes 3670016 | tf_op jit(solution)/shard_map/stgpb,sbtd->stgpd/dot_general | solution.py:354
  48.6 0.4 reshape.227
  49.0 0.1 copy.85
  49.1 0.7 iota_compare_fusion
  49.8 0.1 select_reduce_fusion
  50.0 0.7 bitcast_maximum_fusion
  50.7 0.1 copy.91
  50.7 0.1 copy.96
  50.8 0.8 copy.100
  51.7 0.7 gather_fusion.1
  52.4 0.8 fusion.9
  53.3 0.1 reshape.236
  53.4 0.1 reshape.291
  53.5 0.1 reshape.290
  53.6 0.1 bitcast_multiply_fusion.1
  53.7 0.3 mul.74
  54.0 1.7 %fusion.7 = bf16[8,32,128]{2,0,1:T(8,128)(2,1)S(1)} fusion(f32[8,32,128]{2,0,1:T(8,128)S(1)} %bitcast_multiply_fusion.1, f32[8,32]{0,1:T(8,128)S(1)} %copy.91, s32[64]{0:T(128)} %param.15, f32[64,4096]{1,0:T(8,128)S(1)} %reshape.227, f32[8,8,32,128]{3,2,1,0:T(8,128)S(1)} %bitcast.124), kind=kOutput, calls=%fused_computation.15 | convolution fusion | flops 25526784 | bytes 2295040 | tf_op jit(solution)/shard_map/dot_general | solution.py:376
  55.7 0.6 copy.97
  56.4 0.1 pad.2.clone
  56.5 1.3 %scatter_custom_fusion = s32[65]{0:T(128)} fusion(s32[64]{0:T(128)S(1)} %fusion.32, s32[64]{0:T(128)S(1)} %iota.26, s32[]{:T(128)} %constant.13.clone.1), kind=kCustom, calls=%fused_computation.71 | custom fusion | bytes 264 | tf_op jit(solution)/shard_map/scatter | solution.py:330
  57.7 0.8 maximum_maximum_fusion.stats_ref
  58.5 43.2 %shard_map.114 = bf16[4,512]{1,0:T(4,128)(2,1)} custom-call(bf16[16,16,128]{2,1,0:T(8,128)(2,1)} %bitcast.126, f32[16,16,128]{2,1,0:T(8,128)} %maximum_maximum_fusion.stats_ref, bf16[1024,512]{1,0:T(8,128)(2,1)} %w_ref.1), custom_call_target="tpu_custom_call" | custom-call | flops 33554432 | bytes 1441792 | tf_op jit(solution)/shard_map/pallas_call | solution.py:192
  101.7 5.1 %shard_map.115 = bf16[64,2,128,128]{3,2,1,0:T(8,128)(2,1)} custom-call(s32[64]{0:T(128)} %bitcast.137, bf16[64,2,128,128]{3,2,1,0:T(8,128)(2,1)} %bitcast.42.src_hbm), custom_call_target="tpu_custom_call" | custom-call | bytes 8388608 | tf_op jit(solution)/shard_map/pallas_call | solution.py:254
  106.8 0.6 copy.140
  (36 shorter events, 0.3 us)
Async XLA Ops:
  0.6 1.5 %copy-start = (bf16[512,1280]{1,0:T(8,128)(2,1)S(1)}, bf16[512,1280]{1,0:T(8,128)(2,1)}, u32[]{:S(2)}) copy-start(bf16[512,1280]{1,0:T(8,128)(2,1)} %param.11) | copy-start | bytes 3932164
  21.9 4.7 %copy-start.1 = (bf16[16,20,128]{2,1,0:T(8,128)(2,1)S(1)}, bf16[16,20,128]{2,1,0:T(8,128)(2,1)}, u32[]{:S(2)}) copy-start(bf16[16,20,128]{2,1,0:T(8,128)(2,1)} %get-tuple-element.7) | copy-start | bytes 245764
  21.9 5.7 %copy-start.2 = (s32[8]{0:T(128)S(1)}, s32[8]{0:T(128)}, u32[]{:S(2)}) copy-start(s32[8]{0:T(128)} %lengths_ref.1) | copy-start | bytes 100
  21.9 79.8 %all-to-all-start = ((bf16[16,4,2,128,128]{4,3,2,1,0:T(8,128)(2,1)}), bf16[16,4,2,128,128]{4,3,2,1,0:T(8,128)(2,1)}, u32[]{:S(2)}, u32[]{:S(2)}) async-start(bf16[16,4,2,128,128]{4,3,2,1,0:T(8,128)(2,1)} %bitcast.125), calls=%async_computation | async-start | bytes 8388608 | tf_op jit(solution)/shard_map/all_to_all | solution.py:324
  28.2 4.8 %copy-start.6 = (s32[1,16,4]{1,2,0:T(4,128)S(1)}, s32[1,16,4]{1,2,0:T(4,128)}, u32[]{:S(2)}) copy-start(s32[1,16,4]{1,2,0:T(4,128)} %param.18) | copy-start | bytes 772
  28.2 7.1 %copy-start.5 = (s32[64]{0:T(128)S(1)}, s32[64]{0:T(128)}, u32[]{:S(2)}) copy-start(s32[64]{0:T(128)} %param.15) | copy-start | bytes 772
  28.2 7.1 %copy-start.8 = (s32[64]{0:T(128)S(1)}, s32[64]{0:T(128)}, u32[]{:S(2)}) copy-start(s32[64]{0:T(128)} %param.16) | copy-start | bytes 772
  40.4 0.8 copy-start.4
  49.0 7.4 %copy-start.7 = (s32[64,1]{0,1:T(1,128)S(1)}, s32[64,1]{0,1:T(1,128)}, u32[]{:S(2)}) copy-start(s32[64,1]{0,1:T(1,128)} %reshape.219) | copy-start | bytes 772
  101.7 5.1 %copy-start.3 = (bf16[4,512]{1,0:T(4,128)(2,1)S(1)}, bf16[4,512]{1,0:T(4,128)(2,1)}, u32[]{:S(2)}) copy-start(bf16[4,512]{1,0:T(4,128)(2,1)} %shard_map.114) | copy-start | bytes 12292

commit v6 on v5

--- a/solution.py
+++ b/solution.py
@@ -212,37 +212,30 @@
     )(acc, stats, out_weight)
 
 
-def _pick_kernel(limit, index_ref, src_hbm, out_hbm, buf, sems, out_sem):
-    count = buf.shape[0]
-
-    def start(j, carry):
+def _place_kernel(limit, index_ref, src_hbm, out_hbm, buf, blank, in_sem, out_sems):
+    load = pltpu.make_async_copy(src_hbm, buf, in_sem)
+    load.start()
+    blank[...] = jnp.zeros(blank.shape, blank.dtype)
+    load.wait()
+
+    def send(j, carry):
         k = index_ref[j]
 
         @pl.when(k < limit)
         def _():
-            pltpu.make_async_copy(src_hbm.at[jnp.minimum(k, limit - 1)], buf.at[j], sems.at[j]).start()
+            pltpu.make_async_copy(buf.at[jnp.minimum(k, limit - 1)], out_hbm.at[j], out_sems.at[j]).start()
 
         @pl.when(k >= limit)
         def _():
-            buf[j] = jnp.zeros(buf.shape[1:], buf.dtype)
+            pltpu.make_async_copy(blank, out_hbm.at[j], out_sems.at[j]).start()
 
         return carry
 
-    def send(j, carry):
-        k = index_ref[j]
-
-        @pl.when(k < limit)
-        def _():
-            pltpu.make_async_copy(src_hbm.at[0], buf.at[j], sems.at[j]).wait()
-
-        pltpu.make_async_copy(buf.at[j], out_hbm.at[j], out_sem.at[j]).start()
+    def finish(j, carry):
+        pltpu.make_async_copy(blank, out_hbm.at[j], out_sems.at[j]).wait()
         return carry
 
-    def finish(j, carry):
-        pltpu.make_async_copy(buf.at[j], out_hbm.at[j], out_sem.at[j]).wait()
-        return carry
-
-    lax.fori_loop(0, count, start, 0)
+    count = out_hbm.shape[0]
     lax.fori_loop(0, count, send, 0)
     lax.fori_loop(0, count, finish, 0)
 
@@ -252,7 +245,7 @@
     shape = (count,) + source.shape[1:]
     nbytes = count * source[0].size * source.dtype.itemsize
     return pl.pallas_call(
-        functools.partial(_pick_kernel, limit),
+        functools.partial(_place_kernel, limit),
         out_shape=jax.ShapeDtypeStruct(shape, source.dtype),
         in_specs=[
             pl.BlockSpec(memory_space=pltpu.SMEM),
@@ -260,8 +253,9 @@
         ],
         out_specs=pl.BlockSpec(memory_space=pl.ANY),
         scratch_shapes=[
-            pltpu.VMEM(shape, source.dtype),
-            pltpu.SemaphoreType.DMA((count,)),
+            pltpu.VMEM(source.shape, source.dtype),
+            pltpu.VMEM(source.shape[1:], source.dtype),
+            pltpu.SemaphoreType.DMA(()),
             pltpu.SemaphoreType.DMA((count,)),
         ],
         cost_estimate=pl.CostEstimate(flops=0, bytes_accessed=2 * nbytes, transcendentals=0),

time: 108 us -> 108 us (level)
  no operation moved by 1% of the time
where the time goes in v6:
time: 108 us
  Pallas kernels  66.6 us (62%)
  local copies, waits for them, and re-layouts  17 us (16%)
  matrix products  9.64 us (9%)
  other arithmetic  8.85 us (8%)
  starting transfers between devices  4.68 us (4%)
    pallas_call x1, Pallas kernels, attend_exchange(): pl.pallas_call(functools.partial(_attend_kernel, n, m, rows), out_shape=j...  43.2 us
    pallas_call x1, Pallas kernels, qkv_exchange(): pl.pallas_call(functools.partial(_qkv_kernel, n, kv_cache.shape[0]), out_...  18 us
    unnamed x22, local copies, waits for them, and re-layouts  6.99 us
    pallas_call x1, Pallas kernels, pick_blocks(): pl.pallas_call(functools.partial(_place_kernel, limit), out_shape=jax.Sha...  5.39 us
    gather x1, other arithmetic, body(): token_valid = (token_pos < lengths[slot_clip][:, None]) & live_slot[:, None]  5.02 us
    all_to_all x1, starting transfers between devices, body(): lax.all_to_all(outgoing, 'seq', split_axis=0, concat_axis=0, tiled=True)  4.68 us
    dot_general x1, matrix products, body(): jnp.einsum('sptgd,sbtd->stgpb', gathered, cache_view[:, 0], preferred_ele...  2.91 us
    dot_general x1, matrix products, body(): jnp.einsum('stgpb,sbtd->stgpd', weights.astype(jnp.bfloat16), cache_view[...  2.42 us
  transfers between devices with their start and end apart: 1, of which 0 were waited for; matrix products, arithmetic and copies ran while one was open for 29% of the time, Pallas kernels for 40%

profile of v6, /device:TPU:1, one launch (start us, length us, event | category | flops | bytes accessed | tf_op | source)
XLA Modules:
  0.0 107.7 jit_solution(12824024575772581000)
XLA Ops:
  0.6 1.4 %copy.80.pick_ref = s32[1,16,4]{2,1,0:T(8,128)} copy(s32[1,16,4]{1,2,0:T(4,128)} %param.17) | data formatting | bytes 512 | tf_op args[7]
  2.1 1.1 %fusion.40 = f32[32,1280]{1,0:T(8,128)S(1)} fusion(bf16[32,512]{1,0:T(8,128)(2,1)} %param.10, bf16[512,1280]{1,0:T(8,128)(2,1)S(1)} %copy-done), kind=kOutput, calls=%fused_computation.79 | convolution fusion | flops 41943040 | bytes 1507328 | tf_op jit(solution)/shard_map/dot_general | solution.py:306
  3.2 0.7 reshape.220.part_ref
  3.9 18.0 %shard_map.113 = (bf16[16,20,128]{2,1,0:T(8,128)(2,1)}, bf16[64,2,128,128]{3,2,1,0:T(8,128)(2,1)}) custom-call(f32[16,20,128]{2,1,0:T(8,128)} %reshape.220.part_ref, f32[1,128]{1,0:T(1,128)} %constant.12.clone.freq_ref, s32[8]{0:T(128)} %lengths_ref.1, s32[1,16,4]{2,1,0:T(8,128)} %copy.80.pick_ref, bf16[64,2,128,128]{3,2,1,0:T(8,128)(2,1)} %kv_hbm.1), custom_call_target="tpu_custom_call" | custom-call | bytes 8880128 | tf_op jit(solution)/shard_map/pallas_call | solution.py:110
  21.9 4.7 %all-to-all-start = ((bf16[16,4,2,128,128]{4,3,2,1,0:T(8,128)(2,1)}), bf16[16,4,2,128,128]{4,3,2,1,0:T(8,128)(2,1)}, u32[]{:S(2)}, u32[]{:S(2)}) async-start(bf16[16,4,2,128,128]{4,3,2,1,0:T(8,128)(2,1)} %bitcast.125), calls=%async_computation | async-start | bytes 8388608 | tf_op jit(solution)/shard_map/all_to_all | solution.py:318
  26.7 0.4 fusion.38
  27.1 0.1 fusion.18
  27.3 0.3 convolution_select_fusion
  27.6 0.7 fusion.37
  28.3 4.8 %copy.136 = bf16[64,2,128,128]{3,2,0,1:T(8,128)(2,1)} copy(bf16[64,2,128,128]{3,2,1,0:T(8,128)(2,1)} %kv_hbm.1) | data formatting | bytes 8388608 | tf_op args[3]
  33.1 0.1 copy.79
  33.2 0.6 reshape.219
  33.8 0.1 copy.101
  33.9 0.7 copy.102
  34.5 0.1 copy.89
  34.6 0.7 copy.90
  35.3 0.1 copy.94
  35.4 5.0 %compare_select_fusion.2 = (s32[64]{0:T(128)S(1)}, s32[64]{0:T(128)S(1)}, s32[64]{0:T(128)S(1)}) fusion(s32[]{:T(128)} %bitcast.2, s32[]{:T(128)} %bitcast.3, s32[]{:T(128)} %bitcast.4, s32[]{:T(128)} %bitcast.5, s32[]{:T(128)} %bitcast.6, s32[]{:T(128)} %bitcast.7, s32[]{:T(128)} %bitcast.8, s32[]{:T(128)} %bitcast.9, s32[64]{0:T(128)S(1)} %copy-done.5, ...), kind=kLoop, calls=%fused_computation.61 | loop fusion | flops 1216 | bytes 1312 | tf_op jit(solution)/shard_map/gather | solution.py:333
  40.4 0.7 gather_fusion
  41.1 0.1 fusion.25
  41.2 2.9 %fusion.39 = (f32[64,8,4]{1,2,0:T(4,128)S(1)}, f32[64,1,8,4,128]{4,2,3,0,1:T(8,128)S(1)}) fusion(bf16[64,4,8,128]{3,2,1,0:T(8,128)(2,1)S(1)} %gather_fusion, bf16[64,2,128,1,128]{4,2,0,3,1:T(8,128)(2,1)} %bitcast.122, pred[64,128]{1,0:T(8,128)(4,1)S(1)} %fusion.25), kind=kOutput, calls=%fused_computation.78 | convolution fusion | flops 67893248 | bytes 3686400 | tf_op jit(solution)/shard_map/sptgd,sbtd->stgpb/dot_general | solution.py:337
  44.1 0.1 copy.83
  44.2 1.2 %fusion.14 = (f32[64,8,4]{1,2,0:T(4,128)S(1)}, bf16[64,8,4,128]{3,1,2,0:T(8,128)(2,1)}) fusion(f32[64,1,8,4,128]{4,2,3,0,1:T(8,128)S(1)} %get-tuple-element.32, f32[64,8,4]{1,2,0:T(4,128)S(1)} %get-tuple-element.31, pred[64,128]{1,0:T(8,128)(4,1)S(1)} %fusion.25), kind=kLoop, calls=%fused_computation.26 | loop fusion | flops 1046528 | bytes 1597440 | tf_op jit(solution)/shard_map/reduce_sum | solution.py:347
  45.5 0.7 copy.99
  46.2 2.4 %fusion = f32[64,8,4,128]{3,2,1,0:T(4,128)S(1)} fusion(bf16[64,2,128,1,128]{4,2,0,3,1:T(8,128)(2,1)} %bitcast.123, bf16[64,8,4,128]{3,1,2,0:T(8,128)(2,1)} %get-tuple-element.13), kind=kOutput, calls=%fused_computation.5 | convolution fusion | flops 67108864 | bytes 3670016 | tf_op jit(solution)/shard_map/stgpb,sbtd->stgpd/dot_general | solution.py:348
  48.6 0.4 reshape.227
  49.0 0.1 copy.85
  49.1 0.7 iota_compare_fusion
  49.8 0.1 select_reduce_fusion
  50.0 0.7 bitcast_maximum_fusion
  50.7 0.1 copy.91
  50.7 0.1 copy.96
  50.8 0.8 copy.100
  51.7 0.7 gather_fusion.1
  52.4 0.8 fusion.9
  53.3 0.1 reshape.236
  53.4 0.1 reshape.291
  53.5 0.1 reshape.290
  53.6 0.1 bitcast_multiply_fusion.1
  53.7 0.3 mul.74
  54.0 1.7 %fusion.7 = bf16[8,32,128]{2,0,1:T(8,128)(2,1)S(1)} fusion(f32[8,32,128]{2,0,1:T(8,128)S(1)} %bitcast_multiply_fusion.1, f32[8,32]{0,1:T(8,128)S(1)} %copy.91, s32[64]{0:T(128)} %param.15, f32[64,4096]{1,0:T(8,128)S(1)} %reshape.227, f32[8,8,32,128]{3,2,1,0:T(8,128)S(1)} %bitcast.124), kind=kOutput, calls=%fused_computation.15 | convolution fusion | flops 25526784 | bytes 2295040 | tf_op jit(solution)/shard_map/dot_general | solution.py:370
  55.7 0.6 copy.97
  56.4 0.1 pad.2.clone
  56.5 1.3 %scatter_custom_fusion = s32[65]{0:T(128)} fusion(s32[64]{0:T(128)S(1)} %fusion.32, s32[64]{0:T(128)S(1)} %iota.26, s32[]{:T(128)} %constant.13.clone.1), kind=kCustom, calls=%fused_computation.71 | custom fusion | bytes 264 | tf_op jit(solution)/shard_map/scatter | solution.py:324
  57.7 0.8 maximum_maximum_fusion.stats_ref
  58.5 43.2 %shard_map.114 = bf16[4,512]{1,0:T(4,128)(2,1)} custom-call(bf16[16,16,128]{2,1,0:T(8,128)(2,1)} %bitcast.126, f32[16,16,128]{2,1,0:T(8,128)} %maximum_maximum_fusion.stats_ref, bf16[1024,512]{1,0:T(8,128)(2,1)} %w_ref.1), custom_call_target="tpu_custom_call" | custom-call | flops 33554432 | bytes 1441792 | tf_op jit(solution)/shard_map/pallas_call | solution.py:192
  101.7 5.4 %shard_map.115 = bf16[64,2,128,128]{3,2,1,0:T(8,128)(2,1)} custom-call(s32[64]{0:T(128)} %bitcast.137, bf16[64,2,128,128]{3,2,1,0:T(8,128)(2,1)} %bitcast.42.src_hbm), custom_call_target="tpu_custom_call" | custom-call | bytes 8388608 | tf_op jit(solution)/shard_map/pallas_call | solution.py:247
  107.1 0.6 copy.140
  (36 shorter events, 0.3 us)
Async XLA Ops:
  0.6 1.5 %copy-start = (bf16[512,1280]{1,0:T(8,128)(2,1)S(1)}, bf16[512,1280]{1,0:T(8,128)(2,1)}, u32[]{:S(2)}) copy-start(bf16[512,1280]{1,0:T(8,128)(2,1)} %param.11) | copy-start | bytes 3932164
  21.9 4.7 %copy-start.1 = (bf16[16,20,128]{2,1,0:T(8,128)(2,1)S(1)}, bf16[16,20,128]{2,1,0:T(8,128)(2,1)}, u32[]{:S(2)}) copy-start(bf16[16,20,128]{2,1,0:T(8,128)(2,1)} %get-tuple-element.7) | copy-start | bytes 245764
  21.9 5.7 %copy-start.2 = (s32[8]{0:T(128)S(1)}, s32[8]{0:T(128)}, u32[]{:S(2)}) copy-start(s32[8]{0:T(128)} %lengths_ref.1) | copy-start | bytes 100
  21.9 79.8 %all-to-all-start = ((bf16[16,4,2,128,128]{4,3,2,1,0:T(8,128)(2,1)}), bf16[16,4,2,128,128]{4,3,2,1,0:T(8,128)(2,1)}, u32[]{:S(2)}, u32[]{:S(2)}) async-start(bf16[16,4,2,128,128]{4,3,2,1,0:T(8,128)(2,1)} %bitcast.125), calls=%async_computation | async-start | bytes 8388608 | tf_op jit(solution)/shard_map/all_to_all | solution.py:318
  28.2 4.8 %copy-start.6 = (s32[1,16,4]{1,2,0:T(4,128)S(1)}, s32[1,16,4]{1,2,0:T(4,128)}, u32[]{:S(2)}) copy-start(s32[1,16,4]{1,2,0:T(4,128)} %param.18) | copy-start | bytes 772
  28.2 7.1 %copy-start.5 = (s32[64]{0:T(128)S(1)}, s32[64]{0:T(128)}, u32[]{:S(2)}) copy-start(s32[64]{0:T(128)} %param.15) | copy-start | bytes 772
  28.2 7.1 %copy-start.8 = (s32[64]{0:T(128)S(1)}, s32[64]{0:T(128)}, u32[]{:S(2)}) copy-start(s32[64]{0:T(128)} %param.16) | copy-start | bytes 772
  40.4 0.8 copy-start.4
  49.0 7.4 %copy-start.7 = (s32[64,1]{0,1:T(1,128)S(1)}, s32[64,1]{0,1:T(1,128)}, u32[]{:S(2)}) copy-start(s32[64,1]{0,1:T(1,128)} %reshape.219) | copy-start | bytes 772
  101.7 5.4 %copy-start.3 = (bf16[4,512]{1,0:T(4,128)(2,1)S(1)}, bf16[4,512]{1,0:T(4,128)(2,1)}, u32[]{:S(2)}) copy-start(bf16[4,512]{1,0:T(4,128)(2,1)} %shard_map.114) | copy-start | bytes 12292

commit v7 on v5

--- a/solution.py
+++ b/solution.py
@@ -212,6 +212,91 @@
     )(acc, stats, out_weight)
 
 
+def _migrate_kernel(
+    n, scale, requests, req_ref, blk_ref, len_ref, q_ref, kv_ref, sent_hbm,
+    m_ref, l_ref, acc_ref, got_hbm, send_sem, recv_sem, local_sem,
+):
+    me = lax.axis_index("seq")
+    _barrier([{"seq": lax.rem(me + i, n)} for i in range(1, n)])
+    copies = []
+    for i in range(1, n):
+        peer = lax.rem(me + i, n)
+        copy = pltpu.make_async_remote_copy(
+            src_ref=sent_hbm.at[peer],
+            dst_ref=got_hbm.at[me],
+            send_sem=send_sem.at[peer],
+            recv_sem=recv_sem.at[me],
+            device_id={"seq": peer},
+            device_id_type=MESH,
+        )
+        copy.start()
+        copies.append(copy)
+    own = pltpu.make_async_copy(sent_hbm.at[me], got_hbm.at[me], local_sem)
+    own.start()
+
+    def slot(s, carry):
+        owner = req_ref[s]
+        r = jnp.minimum(owner, requests - 1)
+        q = q_ref[r]
+        keys = kv_ref[s, 0]
+        scores = lax.dot_general(
+            q, keys, (((1,), (1,)), ((), ())), preferred_element_type=jnp.float32
+        ) * scale
+        lane = lax.broadcasted_iota(jnp.int32, scores.shape, 1)
+        valid = (lane < len_ref[r] - blk_ref[s] * BLOCK) & (owner < requests)
+        scores = jnp.where(valid, scores, neg_large)
+        top = jnp.max(scores, axis=1, keepdims=True)
+        weights = jnp.where(valid, jnp.exp(scores - top), 0.0)
+        m_ref[s] = jnp.broadcast_to(top, scores.shape)
+        l_ref[s] = jnp.broadcast_to(jnp.sum(weights, axis=1, keepdims=True), scores.shape)
+        acc_ref[s] = jnp.dot(
+            weights.astype(jnp.bfloat16), kv_ref[s, 1], preferred_element_type=jnp.float32
+        )
+        return carry
+
+    lax.fori_loop(0, kv_ref.shape[0], slot, 0)
+    _wait_all("seq", n, me, got_hbm, send_sem, recv_sem)
+    for copy in copies:
+        copy.wait_send()
+    own.wait()
+
+
+def migrate_and_attend(slot_request, slot_block, lengths, queries, kv_cache, outgoing, scale):
+    n = outgoing.shape[0]
+    slots = kv_cache.shape[0]
+    rows = queries.shape[1]
+    per_slot = (slots, rows, HEAD)
+    return pl.pallas_call(
+        functools.partial(_migrate_kernel, n, scale, lengths.shape[0]),
+        out_shape=(
+            jax.ShapeDtypeStruct(per_slot, jnp.float32),
+            jax.ShapeDtypeStruct(per_slot, jnp.float32),
+            jax.ShapeDtypeStruct(per_slot, jnp.float32),
+            jax.ShapeDtypeStruct(outgoing.shape, outgoing.dtype),
+        ),
+        in_specs=[pl.BlockSpec(memory_space=pltpu.SMEM)] * 3
+        + [pl.BlockSpec(memory_space=pltpu.VMEM)] * 2
+        + [pl.BlockSpec(memory_space=pl.ANY)],
+        out_specs=(
+            pl.BlockSpec(memory_space=pltpu.VMEM),
+            pl.BlockSpec(memory_space=pltpu.VMEM),
+            pl.BlockSpec(memory_space=pltpu.VMEM),
+            pl.BlockSpec(memory_space=pl.ANY),
+        ),
+        scratch_shapes=[
+            pltpu.SemaphoreType.DMA((n,)),
+            pltpu.SemaphoreType.DMA((n,)),
+            pltpu.SemaphoreType.DMA(()),
+        ],
+        compiler_params=pltpu.CompilerParams(collective_id=2, has_side_effects=True),
+        cost_estimate=pl.CostEstimate(
+            flops=4 * slots * rows * BLOCK * HEAD,
+            bytes_accessed=kv_cache.size * 2 + 2 * outgoing.size * 2,
+            transcendentals=slots * rows * BLOCK,
+        ),
+    )(slot_request, slot_block, lengths, queries, kv_cache, outgoing)
+
+
 def _pick_kernel(limit, index_ref, src_hbm, out_hbm, buf, sems, out_sem):
     count = buf.shape[0]
 
@@ -321,9 +406,7 @@
     local_kv = 1
 
     outgoing = outgoing.reshape((lax.axis_size("seq"), -1) + kv_cache.shape[1:])
-    incoming = lax.all_to_all(outgoing, "seq", split_axis=0, concat_axis=0, tiled=True)
-    incoming = incoming.reshape((-1,) + kv_cache.shape[1:])
-    arrivals = incoming.shape[0]
+    arrivals = outgoing.shape[0] * outgoing.shape[1]
     source_of = (
         jnp.full((slot_count + 1,), arrivals, jnp.int32)
         .at[recv_list.reshape(-1)]
@@ -334,31 +417,16 @@
     values_new = qkv[:, :, :, group_size + 1]
 
     slot_clip = jnp.minimum(slot_request, requests - 1)
-    live_slot = slot_request < requests
-    token_pos = slot_block[:, None] * BLOCK + jnp.arange(BLOCK, dtype=jnp.int32)[None, :]
-    token_valid = (token_pos < lengths[slot_clip][:, None]) & live_slot[:, None]
-    cache_view = kv_cache.reshape(slot_count, 2, BLOCK, local_kv, HEAD)
-    gathered = queries[slot_clip]
-    scores = (
-        jnp.einsum(
-            "sptgd,sbtd->stgpb", gathered, cache_view[:, 0], preferred_element_type=jnp.float32
-        )
-        * scale_factor
-    )
-    scores = jnp.where(token_valid[:, None, None, None, :], scores, neg_large)
-    slot_max = jnp.max(scores, axis=-1)
-    weights = jnp.where(
-        token_valid[:, None, None, None, :], jnp.exp(scores - slot_max[..., None]), 0.0
-    )
-    slot_sum = jnp.sum(weights, axis=-1)
-    slot_acc = jnp.einsum(
-        "stgpb,sbtd->stgpd",
-        weights.astype(jnp.bfloat16),
-        cache_view[:, 1],
-        preferred_element_type=jnp.float32,
-    )
+    per_request_q = queries[:, :, 0].transpose(0, 2, 1, 3).reshape(requests, group_size * POS, HEAD)
+    slot_m, slot_l, slot_a, incoming = migrate_and_attend(
+        slot_request, slot_block, lengths, per_request_q, kv_cache, outgoing, scale_factor
+    )
+    incoming = incoming.reshape((-1,) + kv_cache.shape[1:])
+    slot_max = slot_m[:, :, 0]
+    slot_sum = slot_l[:, :, 0]
+    slot_acc = slot_a
     flat_width = local_kv * group_size * POS
-    slot_max_flat = slot_max.reshape(slot_count, flat_width)
+    slot_max_flat = slot_max
     member = slot_request[:, None] == jnp.arange(requests, dtype=jnp.int32)[None, :]
     request_max = jnp.max(
         jnp.where(member[:, None, :], slot_max_flat[:, :, None], neg_large), axis=0

time: 108 us -> 138 us (1.28)
  Pallas kernels: 66.2 us -> 110 us
  matrix products: 9.64 us -> 3.62 us
  other arithmetic: 8.85 us -> 3.93 us
  starting transfers between devices: 4.68 us -> 0 us
    pallas_call x0 -> x1, Pallas kernels: none -> 62.7 us  [migrate_and_attend(): pl.pallas_call(functools.partial(_migrate_kernel, n, scale, lengths.shape...]
    pallas_call x1, Pallas kernels: 43.2 us -> 24.6 us  [attend_exchange(): pl.pallas_call(functools.partial(_attend_kernel, n, m, rows), out_shape=j...]
    dot_general x2 -> x0, matrix products: 5.33 us -> none  [the longest x1 2.91 us: body(): jnp.einsum('sptgd,sbtd->stgpb', gathered, cache_view[:, 0], preferred_ele...]
    gather x2 -> x1, other arithmetic: 5.02 us -> 0.02 us  [body(): rescale = jnp.exp(slot_max_flat - request_max[slot_clip])]
    all_to_all x1 -> x0, starting transfers between devices: 4.68 us -> none  [body(): lax.all_to_all(outgoing, 'seq', split_axis=0, concat_axis=0, tiled=True)]
    unnamed x22 -> x13, local copies, waits for them, and re-layouts: 6.99 us -> 4.03 us
    slice x1, local copies, waits for them, and re-layouts: 0.01 us -> 1.87 us  [body(): slot_max = slot_m[:, :, 0]]
    squeeze x0 -> x1, local copies, waits for them, and re-layouts: none -> 1.67 us  [body(): slot_sum = slot_l[:, :, 0]]
  transfers between devices with their start and end apart: 1 -> 0, of which waited for: 0 -> 0; matrix products, arithmetic and copies ran while one was open for 29% -> 0% of each run, Pallas kernels for 40% -> 0%
where the time goes in v7:
time: 138 us; the launch traced here: 137 us
  Pallas kernels  110 us (80%)
  local copies, waits for them, and re-layouts  18.1 us (13%)
  other arithmetic  3.93 us (3%)
  matrix products  3.62 us (3%)
    pallas_call x1, Pallas kernels, migrate_and_attend(): pl.pallas_call(functools.partial(_migrate_kernel, n, scale, lengths.shape...  62.7 us
    pallas_call x1, Pallas kernels, attend_exchange(): pl.pallas_call(functools.partial(_attend_kernel, n, m, rows), out_shape=j...  24.6 us
    pallas_call x1, Pallas kernels, qkv_exchange(): pl.pallas_call(functools.partial(_qkv_kernel, n, kv_cache.shape[0]), out_...  18 us
    pallas_call x1, Pallas kernels, pick_blocks(): pl.pallas_call(functools.partial(_pick_kernel, limit), out_shape=jax.Shap...  5.08 us
    unnamed x13, local copies, waits for them, and re-layouts  4.03 us

profile of v7, /device:TPU:1, one launch (start us, length us, event | category | flops | bytes accessed | tf_op | source)
XLA Modules:
  0.0 136.9 jit_solution(10250380036395104437)
XLA Ops:
  0.6 0.0 copy-start
  0.6 1.3 copy-done
  2.0 1.1 fusion.31
  3.0 0.7 reshape.128.part_ref
  3.8 1.4 copy.140.pick_ref
  5.1 18.0 %shard_map.113 = (bf16[16,20,128]{2,1,0:T(8,128)(2,1)}, bf16[64,2,128,128]{3,2,1,0:T(8,128)(2,1)}) custom-call(f32[16,20,128]{2,1,0:T(8,128)} %reshape.128.part_ref, f32[1,128]{1,0:T(1,128)} %constant.28.clone.freq_ref, s32[8]{0:T(128)} %len_ref.1, s32[1,16,4]{2,1,0:T(8,128)} %copy.140.pick_ref, bf16[64,2,128,128]{3,2,1,0:T(8,128)(2,1)} %kv_ref.1), custom_call_target="tpu_custom_call" | custom-call | bytes 8880128 | tf_op jit(solution)/shard_map/pallas_call | solution.py:110
  23.1 0.9 reshape.129
  24.1 0.4 fusion.30
  24.5 0.1 fusion.9
  24.6 0.1 copy.151
  24.7 0.1 copy.152
  24.8 0.7 copy.141
  25.5 62.7 %shard_map.114 = (f32[64,32,128]{2,1,0:T(8,128)}, f32[64,32,128]{2,1,0:T(8,128)}, f32[64,32,128]{2,1,0:T(8,128)}, bf16[16,4,2,128,128]{4,3,2,1,0:T(8,128)(2,1)}) custom-call(s32[64]{0:T(128)} %req_ref.1, s32[64]{0:T(128)} %blk_ref.1, s32[8]{0:T(128)} %len_ref.1, bf16[8,32,128]{2,1,0:T(8,128)(2,1)} %bitcast.99, bf16[64,2,128,128]{3,2,1,0:T(8,128)(2,1)} %kv_ref.1, ...), custom_call_target="tpu_custom_call" | custom-call | flops 134217728 | bytes 12582912 | tf_op jit(solution)/shard_map/pallas_call | solution.py:269
  88.2 0.0 copy-start.1
  88.2 1.9 %copy.142 = f32[64,32,1]{0,1,2:T(8,128)S(1)} copy(f32[64,32,1]{2,1,0:T(8,128)} %bitcast.92) | data formatting | bytes 16384 | tf_op jit(solution)/shard_map/slice | solution.py:425
  90.1 0.0 copy-done.3
  90.1 0.1 select_reduce_fusion
  90.2 0.1 copy.143
  90.3 0.1 copy.164
  90.4 0.1 copy.165
  90.5 0.6 gather_fusion
  91.1 1.7 %copy.179 = f32[64,32,1]{1,0,2:T(8,128)S(1)} copy(f32[64,32,1]{2,1,0:T(8,128)} %bitcast.93) | data formatting | bytes 16384 | tf_op jit(solution)/shard_map/jit(_where)/broadcast_in_dim | solution.py:432
  92.7 1.7 %copy.178 = f32[64,32,1]{1,0,2:T(8,128)S(1)} copy(f32[64,32,1]{2,1,0:T(8,128)} %bitcast.97) | data formatting | bytes 16384 | tf_op jit(solution)/shard_map/squeeze | solution.py:426
  94.4 0.1 fusion.3
  94.6 0.1 reshape.138
  94.7 0.1 reshape.162
  94.8 0.1 reshape.136
  94.9 0.1 reshape.161
  95.0 0.1 pad.2.clone
  95.1 0.8 maximum_maximum_fusion.stats_ref
  95.8 0.1 copy.158
  95.9 0.3 convolution_select_fusion
  96.2 0.1 copy.156
  96.3 0.1 bitcast_multiply_fusion
  96.4 0.1 copy.153
  96.4 0.0 copy-done.2
  96.4 1.2 copy.145
  97.7 1.2 subtract_exponential_fusion
  98.9 1.7 %copy.173 = f32[64,32,1]{1,0,2:T(8,128)S(1)} copy(f32[64,32,1]{2,1,0:T(8,128)} %subtract_exponential_fusion) | data formatting | bytes 16384 | tf_op jit(solution)/shard_map/mul | solution.py:441
  100.5 1.6 %broadcast_multiply_fusion = f32[64,32,128]{2,1,0:T(8,128)S(1)} fusion(f32[64,32,128]{2,1,0:T(8,128)} %get-tuple-element.13, f32[64,32]{1,0:T(8,128)S(1)} %bitcast.102), kind=kLoop, calls=%fused_computation.15 | loop fusion | flops 262144 | bytes 2105344 | tf_op jit(solution)/shard_map/mul | solution.py:441
  102.1 1.7 %fusion.1 = bf16[8,32,128]{2,0,1:T(8,128)(2,1)S(1)} fusion(f32[8,32,128]{2,0,1:T(8,128)S(1)} %bitcast_multiply_fusion, f32[8,32]{0,1:T(8,128)S(1)} %copy.153, s32[64]{0:T(128)} %req_ref.1, f32[8,8,32,128]{3,2,1,0:T(8,128)S(1)} %bitcast.96), kind=kOutput, calls=%fused_computation.5 | convolution fusion | flops 25264640 | bytes 1246464 | tf_op jit(solution)/shard_map/dot_general | solution.py:444
  103.8 0.7 copy.159
  104.5 0.1 copy.139
  104.6 0.1 reshape.127
  104.7 1.3 scatter_custom_fusion
  105.9 5.1 %shard_map.116 = bf16[64,2,128,128]{3,2,1,0:T(8,128)(2,1)} custom-call(s32[64]{0:T(128)} %bitcast.110, bf16[64,2,128,128]{3,2,1,0:T(8,128)(2,1)} %bitcast.94), custom_call_target="tpu_custom_call" | custom-call | bytes 8388608 | tf_op jit(solution)/shard_map/pallas_call | solution.py:339
  111.0 24.6 %shard_map.115 = bf16[4,512]{1,0:T(4,128)(2,1)} custom-call(bf16[16,16,128]{2,1,0:T(8,128)(2,1)} %bitcast.100, f32[16,16,128]{2,1,0:T(8,128)} %maximum_maximum_fusion.stats_ref, bf16[1024,512]{1,0:T(8,128)(2,1)} %w_ref.1), custom_call_target="tpu_custom_call" | custom-call | flops 33554432 | bytes 1441792 | tf_op jit(solution)/shard_map/pallas_call | solution.py:192
  135.6 1.3 copy.200
  (20 shorter events, 0.2 us)
Async XLA Ops:
  0.6 1.3 copy-start
  25.5 64.6 %copy-start.3 = (s32[64]{0:T(128)S(1)}, s32[64]{0:T(128)}, u32[]{:S(2)}) copy-start(s32[64]{0:T(128)} %req_ref.1) | copy-start | bytes 772
  88.2 9.4 %copy-start.1 = (f32[64,32,128]{2,1,0:T(8,128)S(1)}, f32[64,32,128]{2,1,0:T(8,128)}, u32[]{:S(2)}) copy-start(f32[64,32,128]{2,1,0:T(8,128)} %get-tuple-element.14) | copy-start | bytes 3145732
  91.1 5.4 %copy-start.2 = (f32[64,32]{1,0:T(8,128)}, f32[64,32]{1,0:T(8,128)S(1)}, u32[]{:S(2)}) copy-start(f32[64,32]{1,0:T(8,128)S(1)} %gather_fusion) | copy-start | bytes 24580
  98.9 5.6 %copy-start.4 = (s32[1,16,4]{1,2,0:T(4,128)S(1)}, s32[1,16,4]{1,2,0:T(4,128)}, u32[]{:S(2)}) copy-start(s32[1,16,4]{1,2,0:T(4,128)} %param.18) | copy-start | bytes 772

commit v8 on v5

--- a/solution.py
+++ b/solution.py
@@ -58,20 +58,42 @@
 
 
 def _qkv_kernel(
-    n, limit, part_ref, freq_ref, lengths_ref, pick_ref, kv_hbm, out_ref, sent_hbm,
-    land_a, mine, land_b, sems, kv_vmem, sent_vmem, local_sems,
+    n, limit, x_hbm, w_hbm, freq_ref, lengths_ref, pick_hbm, kv_hbm, out_ref, sent_hbm,
+    x_vmem, w_vmem, part_ref, pick_ref, land_a, mine, land_b, sems, kv_vmem, sent_vmem, local_sems,
 ):
     me = lax.axis_index("seq")
+    loads = [
+        pltpu.make_async_copy(x_hbm, x_vmem, local_sems.at[2]),
+        pltpu.make_async_copy(w_hbm, w_vmem, local_sems.at[3]),
+        pltpu.make_async_copy(pick_hbm, pick_ref, local_sems.at[4]),
+    ]
+    for load in loads:
+        load.start()
     kv_in = pltpu.make_async_copy(kv_hbm, kv_vmem, local_sems.at[0])
     kv_in.start()
+    barrier = pltpu.get_barrier_semaphore()
+    for i in range(1, n):
+        pl.semaphore_signal(
+            barrier, inc=1, device_id={"seq": lax.rem(me + i, n)}, device_id_type=MESH
+        )
+    for load in loads:
+        load.wait()
+    product = jnp.dot(x_vmem[...], w_vmem[...], preferred_element_type=jnp.float32)
+    groups = product.shape[1] // HEAD
+    per = part_ref.shape[1] // groups
+    for j in range(n):
+        for k in range(per):
+            row = product[per * j + k : per * j + k + 1]
+            for g in range(groups):
+                part_ref[j, k * groups + g : k * groups + g + 1, :] = row[:, g * HEAD : (g + 1) * HEAD]
     land_a[me] = part_ref[me]
-    _barrier([{"seq": lax.rem(me + i, n)} for i in range(1, n)])
+    pl.semaphore_wait(barrier, n - 1)
     sent_a = _send_all("seq", n, me, lambda p: part_ref.at[p], land_a, sems.at[0], sems.at[1])
     kv_in.wait()
 
     def pick(j, carry):
-        per = pick_ref.shape[2]
-        sent_vmem[j] = kv_vmem[jnp.minimum(pick_ref[0, j // per, j % per], limit - 1)]
+        per = pick_ref.shape[1]
+        sent_vmem[j] = kv_vmem[jnp.minimum(pick_ref[0, j % per, j // per], limit - 1)]
         return carry
 
     lax.fori_loop(0, sent_vmem.shape[0], pick, 0)
@@ -104,35 +126,41 @@
     kv_out.wait()
 
 
-def qkv_exchange(partial, freq, lengths, pick, kv_cache):
-    n = partial.shape[0]
+def qkv_exchange(normed, qkv_weight, freq, lengths, pick, kv_cache, n):
+    rows = normed.shape[0]
+    groups = qkv_weight.shape[1] // HEAD
+    chunk = (n, rows // n * groups, HEAD)
     picked = (pick.size,) + kv_cache.shape[1:]
     return pl.pallas_call(
         functools.partial(_qkv_kernel, n, kv_cache.shape[0]),
         out_shape=(
-            jax.ShapeDtypeStruct(partial.shape, jnp.bfloat16),
+            jax.ShapeDtypeStruct(chunk, jnp.bfloat16),
             jax.ShapeDtypeStruct(picked, kv_cache.dtype),
         ),
-        in_specs=[pl.BlockSpec(memory_space=pltpu.VMEM)] * 2
-        + [pl.BlockSpec(memory_space=pltpu.SMEM)] * 2
-        + [pl.BlockSpec(memory_space=pl.ANY)],
+        in_specs=[pl.BlockSpec(memory_space=pl.ANY)] * 2
+        + [pl.BlockSpec(memory_space=pltpu.VMEM), pl.BlockSpec(memory_space=pltpu.SMEM)]
+        + [pl.BlockSpec(memory_space=pl.ANY)] * 2,
         out_specs=(pl.BlockSpec(memory_space=pltpu.VMEM), pl.BlockSpec(memory_space=pl.ANY)),
         scratch_shapes=[
-            pltpu.VMEM(partial.shape, jnp.float32),
-            pltpu.VMEM(partial.shape[1:], jnp.bfloat16),
-            pltpu.VMEM(partial.shape, jnp.bfloat16),
+            pltpu.VMEM(normed.shape, normed.dtype),
+            pltpu.VMEM(qkv_weight.shape, qkv_weight.dtype),
+            pltpu.VMEM(chunk, jnp.float32),
+            pltpu.SMEM(pick.shape, pick.dtype),
+            pltpu.VMEM(chunk, jnp.float32),
+            pltpu.VMEM(chunk[1:], jnp.bfloat16),
+            pltpu.VMEM(chunk, jnp.bfloat16),
             pltpu.SemaphoreType.DMA((4, n)),
             pltpu.VMEM(kv_cache.shape, kv_cache.dtype),
             pltpu.VMEM(picked, kv_cache.dtype),
-            pltpu.SemaphoreType.DMA((2,)),
+            pltpu.SemaphoreType.DMA((5,)),
         ],
         compiler_params=pltpu.CompilerParams(collective_id=0, has_side_effects=True),
         cost_estimate=pl.CostEstimate(
-            flops=0,
-            bytes_accessed=partial.size * 12 + 2 * kv_cache.size * kv_cache.dtype.itemsize,
+            flops=2 * rows * normed.shape[1] * qkv_weight.shape[1],
+            bytes_accessed=qkv_weight.size * 2 + 2 * kv_cache.size * kv_cache.dtype.itemsize,
             transcendentals=0,
         ),
-    )(partial, freq, lengths, pick, kv_cache)
+    )(normed, qkv_weight, freq, lengths, pick, kv_cache)
 
 
 def _attend_kernel(
@@ -309,14 +337,14 @@
     rows_per = rows // n_seq
     groups = qkv_weight.shape[1] // HEAD
 
-    partial = jnp.dot(normed, qkv_weight, preferred_element_type=jnp.float32)
-    partial = partial.reshape(n_seq, rows_per * groups, HEAD)
     half_width = HEAD // 2
     frequencies = np.float32(rope_base) ** (
         -(np.arange(half_width, dtype=np.float32) * np.float32(2.0) / np.float32(HEAD))
     )
     freq_row = jnp.asarray(np.concatenate([frequencies, frequencies])[None, :].astype(np.float32))
-    qkv, outgoing = qkv_exchange(partial, freq_row, lengths, send_list, kv_cache)
+    qkv, outgoing = qkv_exchange(
+        normed, qkv_weight, freq_row, lengths, send_list.transpose(0, 2, 1), kv_cache, n_seq
+    )
     qkv = qkv.reshape(requests, POS, 1, groups, HEAD)
     local_kv = 1
 

time: 108 us -> 105 us (0.972)
  Pallas kernels: 66.2 us -> 72.8 us
  local copies, waits for them, and re-layouts: 17 us -> 11.7 us
  matrix products: 9.64 us -> 7.13 us
  other arithmetic: 8.85 us -> 6.96 us
    pallas_call x1, Pallas kernels: 43.2 us -> 49.7 us  [attend_exchange(): pl.pallas_call(functools.partial(_attend_kernel, n, m, rows), out_shape=j...]
    unnamed x22 -> x15, local copies, waits for them, and re-layouts: 6.99 us -> 5.53 us
    dot_general x1 -> x0, matrix products: 1.08 us -> none  [body(): partial = jnp.dot(normed, qkv_weight, preferred_element_type=jnp.float32)]
  transfers between devices with their start and end apart: 1 -> 1, of which waited for: 0 -> 0; matrix products, arithmetic and copies ran while one was open for 29% -> 24% of each run, Pallas kernels for 40% -> 48%
where the time goes in v8:
time: 105 us; the launch traced here: 104 us
  Pallas kernels  72.8 us (69%)
  local copies, waits for them, and re-layouts  11.7 us (11%)
  matrix products  7.13 us (7%)
  other arithmetic  6.96 us (7%)
  starting transfers between devices  4.68 us (4%)
    pallas_call x1, Pallas kernels, attend_exchange(): pl.pallas_call(functools.partial(_attend_kernel, n, m, rows), out_shape=j...  49.7 us
    pallas_call x1, Pallas kernels, qkv_exchange(): pl.pallas_call(functools.partial(_qkv_kernel, n, kv_cache.shape[0]), out_...  17.8 us
    unnamed x15, local copies, waits for them, and re-layouts  5.53 us
    pallas_call x1, Pallas kernels, pick_blocks(): pl.pallas_call(functools.partial(_pick_kernel, limit), out_shape=jax.Shap...  5.21 us
    gather x1, other arithmetic, body(): token_valid = (token_pos < lengths[slot_clip][:, None]) & live_slot[:, None]  4.95 us
    all_to_all x1, starting transfers between devices, body(): lax.all_to_all(outgoing, 'seq', split_axis=0, concat_axis=0, tiled=True)  4.68 us
    dot_general x1, matrix products, body(): jnp.einsum('sptgd,sbtd->stgpb', gathered, cache_view[:, 0], preferred_ele...  2.91 us
    dot_general x1, matrix products, body(): jnp.einsum('stgpb,sbtd->stgpd', weights.astype(jnp.bfloat16), cache_view[...  2.26 us
  transfers between devices with their start and end apart: 1, of which 0 were waited for; matrix products, arithmetic and copies ran while one was open for 24% of the time, Pallas kernels for 48%

profile of v8, /device:TPU:1, one launch (start us, length us, event | category | flops | bytes accessed | tf_op | source)
XLA Modules:
  0.0 104.2 jit_solution(16123434144531030275)
XLA Ops:
  0.6 17.8 %shard_map.113 = (bf16[16,20,128]{2,1,0:T(8,128)(2,1)}, bf16[64,2,128,128]{3,2,1,0:T(8,128)(2,1)}) custom-call(bf16[32,512]{1,0:T(8,128)(2,1)} %x_hbm.1, bf16[512,1280]{1,0:T(8,128)(2,1)} %w_hbm.1, f32[1,128]{1,0:T(1,128)} %constant.12.clone.freq_ref, s32[8]{0:T(128)} %lengths_ref.1, s32[1,4,16]{2,1,0:T(4,128)} %bitcast.135, bf16[64,2,128,128]{3,2,1,0:T(8,128)(2,1)} %kv_hbm.1), custom_call_target="tpu_custom_call" | custom-call | flops 41943040 | bytes 9699328 | tf_op jit(solution)/shard_map/pallas_call | solution.py:134
  18.5 0.0 copy-start.1
  18.5 4.7 %all-to-all-start = ((bf16[16,4,2,128,128]{4,3,2,1,0:T(8,128)(2,1)}), bf16[16,4,2,128,128]{4,3,2,1,0:T(8,128)(2,1)}, u32[]{:S(2)}, u32[]{:S(2)}) async-start(bf16[16,4,2,128,128]{4,3,2,1,0:T(8,128)(2,1)} %bitcast.123), calls=%async_computation | async-start | bytes 8388608 | tf_op jit(solution)/shard_map/all_to_all | solution.py:352
  23.3 0.4 fusion.38
  23.7 0.1 fusion.18
  23.9 0.3 convolution_select_fusion
  24.2 0.0 copy-done.1
  24.2 0.7 fusion.37
  24.9 4.8 %copy.132 = bf16[64,2,128,128]{3,2,0,1:T(8,128)(2,1)} copy(bf16[64,2,128,128]{3,2,1,0:T(8,128)(2,1)} %kv_hbm.1) | data formatting | bytes 8388608 | tf_op args[3]
  29.7 0.1 copy.76
  29.8 0.1 reshape.216
  29.9 0.1 copy.90
  29.9 0.1 copy.85
  30.0 0.1 copy.86
  30.1 4.9 %compare_select_fusion.2 = (s32[64]{0:T(128)S(1)}, s32[64]{0:T(128)S(1)}, s32[64]{0:T(128)S(1)}) fusion(s32[]{:T(128)} %bitcast.2, s32[]{:T(128)} %bitcast.3, s32[]{:T(128)} %bitcast.4, s32[]{:T(128)} %bitcast.5, s32[]{:T(128)} %bitcast.6, s32[]{:T(128)} %bitcast.7, s32[]{:T(128)} %bitcast.8, s32[]{:T(128)} %bitcast.9, s32[64]{0:T(128)S(1)} %copy-done.3, ...), kind=kLoop, calls=%fused_computation.61 | loop fusion | flops 1216 | bytes 1312 | tf_op jit(solution)/shard_map/gather | solution.py:367
  35.1 0.7 gather_fusion
  35.8 0.1 fusion.25
  35.9 2.9 %fusion.39 = (f32[64,8,4]{1,2,0:T(4,128)S(1)}, f32[64,1,8,4,128]{4,2,3,0,1:T(8,128)S(1)}) fusion(bf16[64,4,8,128]{3,2,1,0:T(8,128)(2,1)S(1)} %gather_fusion, bf16[64,2,128,1,128]{4,2,0,3,1:T(8,128)(2,1)} %bitcast.120, pred[64,128]{1,0:T(8,128)(4,1)S(1)} %fusion.25), kind=kOutput, calls=%fused_computation.78 | convolution fusion | flops 67893248 | bytes 3686400 | tf_op jit(solution)/shard_map/sptgd,sbtd->stgpb/dot_general | solution.py:371
  38.8 0.1 copy.79
  38.9 0.1 copy.81
  39.0 0.1 select_reduce_fusion
  39.1 0.1 copy.80
  39.2 0.1 copy.92
  39.2 0.1 copy.87
  39.3 0.8 fusion.14
  40.1 2.3 %fusion = f32[64,8,4,128]{3,2,1,0:T(4,128)S(1)} fusion(bf16[64,2,128,1,128]{4,2,0,3,1:T(8,128)(2,1)} %bitcast.121, bf16[64,8,4,128]{3,1,2,0:T(8,128)(2,1)S(1)} %get-tuple-element.13), kind=kOutput, calls=%fused_computation.5 | convolution fusion | flops 67108864 | bytes 3670016 | tf_op jit(solution)/shard_map/stgpb,sbtd->stgpd/dot_general | solution.py:382
  42.4 0.4 reshape.223
  42.8 0.6 gather_fusion.1
  43.4 0.1 bitcast_multiply_fusion.1
  43.5 0.3 mul.74
  43.8 1.1 %fusion.7 = bf16[8,32,128]{2,0,1:T(8,128)(2,1)S(1)} fusion(f32[8,32,128]{2,0,1:T(8,128)S(1)} %bitcast_multiply_fusion.1, f32[8,32]{0,1:T(8,128)S(1)} %copy.87, s32[64]{0:T(128)S(1)} %copy-done.3, f32[64,4096]{1,0:T(8,128)S(1)} %reshape.223, f32[8,8,32,128]{3,2,1,0:T(8,128)S(1)} %bitcast.122), kind=kOutput, calls=%fused_computation.15 | convolution fusion | flops 25526784 | bytes 2295040 | tf_op jit(solution)/shard_map/dot_general | solution.py:404
  45.0 0.7 copy.93
  45.6 0.1 copy.95
  45.7 0.1 copy.96
  45.8 0.1 copy.97
  45.9 0.1 copy.98
  45.9 0.1 fusion.9
  46.1 0.1 reshape.232
  46.2 0.1 reshape.287
  46.3 0.1 reshape.229
  46.4 0.1 reshape.286
  46.5 0.1 pad.2.clone
  46.6 1.3 %scatter_custom_fusion = s32[65]{0:T(128)} fusion(s32[64]{0:T(128)S(1)} %fusion.32, s32[64]{0:T(128)S(1)} %iota.26, s32[]{:T(128)} %constant.13.clone.1), kind=kCustom, calls=%fused_computation.71 | custom fusion | bytes 264 | tf_op jit(solution)/shard_map/scatter | solution.py:358
  47.9 0.8 maximum_maximum_fusion.stats_ref
  48.6 49.7 %shard_map.114 = bf16[4,512]{1,0:T(4,128)(2,1)} custom-call(bf16[16,16,128]{2,1,0:T(8,128)(2,1)} %bitcast.124, f32[16,16,128]{2,1,0:T(8,128)} %maximum_maximum_fusion.stats_ref, bf16[1024,512]{1,0:T(8,128)(2,1)} %w_ref.1), custom_call_target="tpu_custom_call" | custom-call | flops 33554432 | bytes 1441792 | tf_op jit(solution)/shard_map/pallas_call | solution.py:220
  98.3 0.0 all-to-all-done
  98.4 5.2 %shard_map.115 = bf16[64,2,128,128]{3,2,1,0:T(8,128)(2,1)} custom-call(s32[64]{0:T(128)} %bitcast.136, bf16[64,2,128,128]{3,2,1,0:T(8,128)(2,1)} %bitcast.43.src_hbm), custom_call_target="tpu_custom_call" | custom-call | bytes 8388608 | tf_op jit(solution)/shard_map/pallas_call | solution.py:282
  103.6 0.6 copy.136
  (27 shorter events, 0.2 us)
Async XLA Ops:
  18.5 4.7 %copy-start = (bf16[16,20,128]{2,1,0:T(8,128)(2,1)S(1)}, bf16[16,20,128]{2,1,0:T(8,128)(2,1)}, u32[]{:S(2)}) copy-start(bf16[16,20,128]{2,1,0:T(8,128)(2,1)} %get-tuple-element.7) | copy-start | bytes 245764
  18.5 5.7 %copy-start.1 = (s32[8]{0:T(128)S(1)}, s32[8]{0:T(128)}, u32[]{:S(2)}) copy-start(s32[8]{0:T(128)} %lengths_ref.1) | copy-start | bytes 100
  18.5 79.8 %all-to-all-start = ((bf16[16,4,2,128,128]{4,3,2,1,0:T(8,128)(2,1)}), bf16[16,4,2,128,128]{4,3,2,1,0:T(8,128)(2,1)}, u32[]{:S(2)}, u32[]{:S(2)}) async-start(bf16[16,4,2,128,128]{4,3,2,1,0:T(8,128)(2,1)} %bitcast.123), calls=%async_computation | async-start | bytes 8388608 | tf_op jit(solution)/shard_map/all_to_all | solution.py:352
  24.8 4.8 %copy-start.4 = (s32[1,16,4]{1,2,0:T(4,128)S(1)}, s32[1,16,4]{1,2,0:T(4,128)}, u32[]{:S(2)}) copy-start(s32[1,16,4]{1,2,0:T(4,128)} %param.18) | copy-start | bytes 772
  24.8 5.2 %copy-start.3 = (s32[64]{0:T(128)S(1)}, s32[64]{0:T(128)}, u32[]{:S(2)}) copy-start(s32[64]{0:T(128)} %param.15) | copy-start | bytes 772
  24.8 5.2 %copy-start.5 = (s32[64]{0:T(128)S(1)}, s32[64]{0:T(128)}, u32[]{:S(2)}) copy-start(s32[64]{0:T(128)} %param.16) | copy-start | bytes 772
  98.3 5.2 %copy-start.2 = (bf16[4,512]{1,0:T(4,128)(2,1)S(1)}, bf16[4,512]{1,0:T(4,128)(2,1)}, u32[]{:S(2)}) copy-start(bf16[4,512]{1,0:T(4,128)(2,1)} %shard_map.114) | copy-start | bytes 12292

commit v9 on v8

--- a/solution.py
+++ b/solution.py
@@ -240,39 +240,29 @@
     )(acc, stats, out_weight)
 
 
-def _pick_kernel(limit, index_ref, src_hbm, out_hbm, buf, sems, out_sem):
-    count = buf.shape[0]
-
-    def start(j, carry):
+def _place_kernel(limit, index_ref, src_hbm, out_hbm, buf, res, sems):
+    load = pltpu.make_async_copy(src_hbm, buf, sems.at[0])
+    load.start()
+    load.wait()
+    count = res.shape[0]
+    half = count // 2
+
+    def put(j, carry):
         k = index_ref[j]
-
-        @pl.when(k < limit)
-        def _():
-            pltpu.make_async_copy(src_hbm.at[jnp.minimum(k, limit - 1)], buf.at[j], sems.at[j]).start()
-
-        @pl.when(k >= limit)
-        def _():
-            buf[j] = jnp.zeros(buf.shape[1:], buf.dtype)
-
+        block = buf[jnp.minimum(k, limit - 1)]
+        res[j] = jnp.where(k < limit, block, jnp.zeros_like(block))
         return carry
 
-    def send(j, carry):
-        k = index_ref[j]
-
-        @pl.when(k < limit)
-        def _():
-            pltpu.make_async_copy(src_hbm.at[0], buf.at[j], sems.at[j]).wait()
-
-        pltpu.make_async_copy(buf.at[j], out_hbm.at[j], out_sem.at[j]).start()
-        return carry
-
-    def finish(j, carry):
-        pltpu.make_async_copy(buf.at[j], out_hbm.at[j], out_sem.at[j]).wait()
-        return carry
-
-    lax.fori_loop(0, count, start, 0)
-    lax.fori_loop(0, count, send, 0)
-    lax.fori_loop(0, count, finish, 0)
+    lax.fori_loop(0, half, put, 0)
+    first = pltpu.make_async_copy(res.at[pl.ds(0, half)], out_hbm.at[pl.ds(0, half)], sems.at[1])
+    first.start()
+    lax.fori_loop(half, count, put, 0)
+    second = pltpu.make_async_copy(
+        res.at[pl.ds(half, count - half)], out_hbm.at[pl.ds(half, count - half)], sems.at[2]
+    )
+    second.start()
+    first.wait()
+    second.wait()
 
 
 def pick_blocks(index, source, limit):
@@ -280,7 +270,7 @@
     shape = (count,) + source.shape[1:]
     nbytes = count * source[0].size * source.dtype.itemsize
     return pl.pallas_call(
-        functools.partial(_pick_kernel, limit),
+        functools.partial(_place_kernel, limit),
         out_shape=jax.ShapeDtypeStruct(shape, source.dtype),
         in_specs=[
             pl.BlockSpec(memory_space=pltpu.SMEM),
@@ -288,9 +278,9 @@
         ],
         out_specs=pl.BlockSpec(memory_space=pl.ANY),
         scratch_shapes=[
+            pltpu.VMEM(source.shape, source.dtype),
             pltpu.VMEM(shape, source.dtype),
-            pltpu.SemaphoreType.DMA((count,)),
-            pltpu.SemaphoreType.DMA((count,)),
+            pltpu.SemaphoreType.DMA((3,)),
         ],
         cost_estimate=pl.CostEstimate(flops=0, bytes_accessed=2 * nbytes, transcendentals=0),
     )(index, source)

time: 105 us -> 105 us (level)
  transfers between devices with their start and end apart: 1 -> 1, of which waited for: 0 -> 0; matrix products, arithmetic and copies ran while one was open for 24% -> 24% of each run, Pallas kernels for 48% -> 47%
where the time goes in v9:
time: 105 us
  Pallas kernels  73.3 us (70%)
  local copies, waits for them, and re-layouts  11.7 us (11%)
  matrix products  7.13 us (7%)
  other arithmetic  6.96 us (7%)
  starting transfers between devices  4.68 us (4%)
    pallas_call x1, Pallas kernels, attend_exchange(): pl.pallas_call(functools.partial(_attend_kernel, n, m, rows), out_shape=j...  49.7 us
    pallas_call x1, Pallas kernels, qkv_exchange(): pl.pallas_call(functools.partial(_qkv_kernel, n, kv_cache.shape[0]), out_...  17.8 us
    pallas_call x1, Pallas kernels, pick_blocks(): pl.pallas_call(functools.partial(_place_kernel, limit), out_shape=jax.Sha...  5.7 us
    unnamed x15, local copies, waits for them, and re-layouts  5.53 us
    gather x1, other arithmetic, body(): token_valid = (token_pos < lengths[slot_clip][:, None]) & live_slot[:, None]  4.95 us
    all_to_all x1, starting transfers between devices, body(): lax.all_to_all(outgoing, 'seq', split_axis=0, concat_axis=0, tiled=True)  4.68 us
    dot_general x1, matrix products, body(): jnp.einsum('sptgd,sbtd->stgpb', gathered, cache_view[:, 0], preferred_ele...  2.91 us
    dot_general x1, matrix products, body(): jnp.einsum('stgpb,sbtd->stgpd', weights.astype(jnp.bfloat16), cache_view[...  2.26 us
  transfers between devices with their start and end apart: 1, of which 0 were waited for; matrix products, arithmetic and copies ran while one was open for 24% of the time, Pallas kernels for 47%

profile of v9, /device:TPU:1, one launch (start us, length us, event | category | flops | bytes accessed | tf_op | source)
XLA Modules:
  0.0 104.7 jit_solution(17133022063592887034)
XLA Ops:
  0.6 17.8 %shard_map.113 = (bf16[16,20,128]{2,1,0:T(8,128)(2,1)}, bf16[64,2,128,128]{3,2,1,0:T(8,128)(2,1)}) custom-call(bf16[32,512]{1,0:T(8,128)(2,1)} %x_hbm.1, bf16[512,1280]{1,0:T(8,128)(2,1)} %w_hbm.1, f32[1,128]{1,0:T(1,128)} %constant.12.clone.freq_ref, s32[8]{0:T(128)} %lengths_ref.1, s32[1,4,16]{2,1,0:T(4,128)} %bitcast.135, bf16[64,2,128,128]{3,2,1,0:T(8,128)(2,1)} %kv_hbm.1), custom_call_target="tpu_custom_call" | custom-call | flops 41943040 | bytes 9699328 | tf_op jit(solution)/shard_map/pallas_call | solution.py:134
  18.5 0.0 copy-start.1
  18.5 4.7 %all-to-all-start = ((bf16[16,4,2,128,128]{4,3,2,1,0:T(8,128)(2,1)}), bf16[16,4,2,128,128]{4,3,2,1,0:T(8,128)(2,1)}, u32[]{:S(2)}, u32[]{:S(2)}) async-start(bf16[16,4,2,128,128]{4,3,2,1,0:T(8,128)(2,1)} %bitcast.123), calls=%async_computation | async-start | bytes 8388608 | tf_op jit(solution)/shard_map/all_to_all | solution.py:342
  23.3 0.4 fusion.38
  23.7 0.1 fusion.18
  23.9 0.3 convolution_select_fusion
  24.2 0.0 copy-done.1
  24.2 0.7 fusion.37
  24.9 4.8 %copy.132 = bf16[64,2,128,128]{3,2,0,1:T(8,128)(2,1)} copy(bf16[64,2,128,128]{3,2,1,0:T(8,128)(2,1)} %kv_hbm.1) | data formatting | bytes 8388608 | tf_op args[3]
  29.7 0.1 copy.76
  29.8 0.1 reshape.216
  29.9 0.1 copy.90
  29.9 0.1 copy.85
  30.0 0.1 copy.86
  30.1 4.9 %compare_select_fusion.2 = (s32[64]{0:T(128)S(1)}, s32[64]{0:T(128)S(1)}, s32[64]{0:T(128)S(1)}) fusion(s32[]{:T(128)} %bitcast.2, s32[]{:T(128)} %bitcast.3, s32[]{:T(128)} %bitcast.4, s32[]{:T(128)} %bitcast.5, s32[]{:T(128)} %bitcast.6, s32[]{:T(128)} %bitcast.7, s32[]{:T(128)} %bitcast.8, s32[]{:T(128)} %bitcast.9, s32[64]{0:T(128)S(1)} %copy-done.3, ...), kind=kLoop, calls=%fused_computation.61 | loop fusion | flops 1216 | bytes 1312 | tf_op jit(solution)/shard_map/gather | solution.py:357
  35.1 0.7 gather_fusion
  35.8 0.1 fusion.25
  35.9 2.9 %fusion.39 = (f32[64,8,4]{1,2,0:T(4,128)S(1)}, f32[64,1,8,4,128]{4,2,3,0,1:T(8,128)S(1)}) fusion(bf16[64,4,8,128]{3,2,1,0:T(8,128)(2,1)S(1)} %gather_fusion, bf16[64,2,128,1,128]{4,2,0,3,1:T(8,128)(2,1)} %bitcast.120, pred[64,128]{1,0:T(8,128)(4,1)S(1)} %fusion.25), kind=kOutput, calls=%fused_computation.78 | convolution fusion | flops 67893248 | bytes 3686400 | tf_op jit(solution)/shard_map/sptgd,sbtd->stgpb/dot_general | solution.py:361
  38.8 0.1 copy.79
  38.9 0.1 copy.81
  39.0 0.1 select_reduce_fusion
  39.1 0.1 copy.80
  39.2 0.1 copy.92
  39.2 0.1 copy.87
  39.3 0.8 fusion.14
  40.1 2.3 %fusion = f32[64,8,4,128]{3,2,1,0:T(4,128)S(1)} fusion(bf16[64,2,128,1,128]{4,2,0,3,1:T(8,128)(2,1)} %bitcast.121, bf16[64,8,4,128]{3,1,2,0:T(8,128)(2,1)S(1)} %get-tuple-element.13), kind=kOutput, calls=%fused_computation.5 | convolution fusion | flops 67108864 | bytes 3670016 | tf_op jit(solution)/shard_map/stgpb,sbtd->stgpd/dot_general | solution.py:372
  42.4 0.4 reshape.223
  42.8 0.6 gather_fusion.1
  43.4 0.1 bitcast_multiply_fusion.1
  43.5 0.3 mul.74
  43.8 1.1 %fusion.7 = bf16[8,32,128]{2,0,1:T(8,128)(2,1)S(1)} fusion(f32[8,32,128]{2,0,1:T(8,128)S(1)} %bitcast_multiply_fusion.1, f32[8,32]{0,1:T(8,128)S(1)} %copy.87, s32[64]{0:T(128)S(1)} %copy-done.3, f32[64,4096]{1,0:T(8,128)S(1)} %reshape.223, f32[8,8,32,128]{3,2,1,0:T(8,128)S(1)} %bitcast.122), kind=kOutput, calls=%fused_computation.15 | convolution fusion | flops 25526784 | bytes 2295040 | tf_op jit(solution)/shard_map/dot_general | solution.py:394
  45.0 0.7 copy.93
  45.6 0.1 copy.95
  45.7 0.1 copy.96
  45.8 0.1 copy.97
  45.9 0.1 copy.98
  45.9 0.1 fusion.9
  46.1 0.1 reshape.232
  46.2 0.1 reshape.287
  46.3 0.1 reshape.229
  46.4 0.1 reshape.286
  46.5 0.1 pad.2.clone
  46.6 1.3 %scatter_custom_fusion = s32[65]{0:T(128)} fusion(s32[64]{0:T(128)S(1)} %fusion.32, s32[64]{0:T(128)S(1)} %iota.26, s32[]{:T(128)} %constant.13.clone.1), kind=kCustom, calls=%fused_computation.71 | custom fusion | bytes 264 | tf_op jit(solution)/shard_map/scatter | solution.py:348
  47.9 0.8 maximum_maximum_fusion.stats_ref
  48.6 49.7 %shard_map.114 = bf16[4,512]{1,0:T(4,128)(2,1)} custom-call(bf16[16,16,128]{2,1,0:T(8,128)(2,1)} %bitcast.124, f32[16,16,128]{2,1,0:T(8,128)} %maximum_maximum_fusion.stats_ref, bf16[1024,512]{1,0:T(8,128)(2,1)} %w_ref.1), custom_call_target="tpu_custom_call" | custom-call | flops 33554432 | bytes 1441792 | tf_op jit(solution)/shard_map/pallas_call | solution.py:220
  98.3 0.0 all-to-all-done
  98.4 5.7 %shard_map.115 = bf16[64,2,128,128]{3,2,1,0:T(8,128)(2,1)} custom-call(s32[64]{0:T(128)} %bitcast.136, bf16[64,2,128,128]{3,2,1,0:T(8,128)(2,1)} %bitcast.43.src_hbm), custom_call_target="tpu_custom_call" | custom-call | bytes 8388608 | tf_op jit(solution)/shard_map/pallas_call | solution.py:272
  104.1 0.6 copy.136
  (27 shorter events, 0.2 us)
Async XLA Ops:
  18.5 4.7 %copy-start = (bf16[16,20,128]{2,1,0:T(8,128)(2,1)S(1)}, bf16[16,20,128]{2,1,0:T(8,128)(2,1)}, u32[]{:S(2)}) copy-start(bf16[16,20,128]{2,1,0:T(8,128)(2,1)} %get-tuple-element.7) | copy-start | bytes 245764
  18.5 5.7 %copy-start.1 = (s32[8]{0:T(128)S(1)}, s32[8]{0:T(128)}, u32[]{:S(2)}) copy-start(s32[8]{0:T(128)} %lengths_ref.1) | copy-start | bytes 100
  18.5 79.8 %all-to-all-start = ((bf16[16,4,2,128,128]{4,3,2,1,0:T(8,128)(2,1)}), bf16[16,4,2,128,128]{4,3,2,1,0:T(8,128)(2,1)}, u32[]{:S(2)}, u32[]{:S(2)}) async-start(bf16[16,4,2,128,128]{4,3,2,1,0:T(8,128)(2,1)} %bitcast.123), calls=%async_computation | async-start | bytes 8388608 | tf_op jit(solution)/shard_map/all_to_all | solution.py:342
  24.8 4.8 %copy-start.4 = (s32[1,16,4]{1,2,0:T(4,128)S(1)}, s32[1,16,4]{1,2,0:T(4,128)}, u32[]{:S(2)}) copy-start(s32[1,16,4]{1,2,0:T(4,128)} %param.18) | copy-start | bytes 772
  24.8 5.2 %copy-start.3 = (s32[64]{0:T(128)S(1)}, s32[64]{0:T(128)}, u32[]{:S(2)}) copy-start(s32[64]{0:T(128)} %param.15) | copy-start | bytes 772
  24.8 5.2 %copy-start.5 = (s32[64]{0:T(128)S(1)}, s32[64]{0:T(128)}, u32[]{:S(2)}) copy-start(s32[64]{0:T(128)} %param.16) | copy-start | bytes 772
  98.3 5.7 %copy-start.2 = (bf16[4,512]{1,0:T(4,128)(2,1)S(1)}, bf16[4,512]{1,0:T(4,128)(2,1)}, u32[]{:S(2)}) copy-start(bf16[4,512]{1,0:T(4,128)(2,1)} %shard_map.114) | copy-start | bytes 12292

commit v10 on v8

--- a/solution.py
+++ b/solution.py
@@ -179,14 +179,15 @@
     sent_s = _send_all("seq", n, me, lambda p: stats_ref.at[p], land_s, sems.at[6], sems.at[7])
     _wait_all("seq", n, me, land_s, sems.at[6], sems.at[7])
     _wait_all("seq", n, me, land_p, sems.at[0], sems.at[1])
-    top = land_s[0, :, 0:1]
+    columns = [land_s[i].T for i in range(n)]
+    top = columns[0][:rows, 0:1]
     for i in range(1, n):
-        top = jnp.maximum(top, land_s[i, :, 0:1])
+        top = jnp.maximum(top, columns[i][:rows, 0:1])
     numerator = jnp.zeros((rows, HEAD), jnp.float32)
     denominator = jnp.zeros((rows, 1), jnp.float32)
     for i in range(n):
-        scale = jnp.exp(land_s[i, :, 0:1] - top)
-        denominator = denominator + land_s[i, :, 1:2] * scale
+        scale = jnp.exp(columns[i][:rows, 0:1] - top)
+        denominator = denominator + columns[i][rows : 2 * rows, 0:1] * scale
         numerator = numerator + land_p[i].astype(jnp.float32) * scale
     attended = (numerator / denominator).astype(mine.dtype)
     mine[...] = attended
@@ -435,14 +436,15 @@
         return lead.reshape(n_seq, requests * group_size * POS // n_seq, -1)
 
     chunk_rows = requests * flat_width // n_seq
-    stats = jnp.concatenate(
+    stats_row = jnp.concatenate(
         [
-            by_chunk(part_max),
-            by_chunk(part_sum),
-            jnp.zeros((n_seq, chunk_rows, HEAD - 2), jnp.float32),
+            by_chunk(part_max).reshape(n_seq, 1, chunk_rows),
+            by_chunk(part_sum).reshape(n_seq, 1, chunk_rows),
+            jnp.zeros((n_seq, 1, HEAD - 2 * chunk_rows), jnp.float32),
         ],
         axis=-1,
     )
+    stats = jnp.concatenate([stats_row, jnp.zeros((n_seq, 7, HEAD), jnp.float32)], axis=1)
     acc_chunks = by_chunk(part_acc).astype(jnp.bfloat16)
     source_of, acc_chunks, stats = lax.optimization_barrier((source_of, acc_chunks, stats))
     projected = attend_exchange(acc_chunks, stats, out_weight, n_head)

time: 105 us -> 104 us (level)
  transfers between devices with their start and end apart: 1 -> 1, of which waited for: 0 -> 0; matrix products, arithmetic and copies ran while one was open for 24% -> 24% of each run, Pallas kernels for 48% -> 47%
where the time goes in v10:
time: 104 us; the launch traced here: 103 us
  Pallas kernels  71.9 us (69%)
  local copies, waits for them, and re-layouts  12.3 us (12%)
  matrix products  7.13 us (7%)
  other arithmetic  6.28 us (6%)
  starting transfers between devices  4.55 us (4%)
    pallas_call x1, Pallas kernels, attend_exchange(): pl.pallas_call(functools.partial(_attend_kernel, n, m, rows), out_shape=j...  49 us
    pallas_call x1, Pallas kernels, qkv_exchange(): pl.pallas_call(functools.partial(_qkv_kernel, n, kv_cache.shape[0]), out_...  17.8 us
    unnamed x15, local copies, waits for them, and re-layouts  5.55 us
    pallas_call x1, Pallas kernels, pick_blocks(): pl.pallas_call(functools.partial(_pick_kernel, limit), out_shape=jax.Shap...  5.08 us
    gather x1, other arithmetic, body(): token_valid = (token_pos < lengths[slot_clip][:, None]) & live_slot[:, None]  4.94 us
    all_to_all x1, starting transfers between devices, body(): lax.all_to_all(outgoing, 'seq', split_axis=0, concat_axis=0, tiled=True)  4.55 us
    dot_general x1, matrix products, body(): jnp.einsum('sptgd,sbtd->stgpb', gathered, cache_view[:, 0], preferred_ele...  2.91 us
    dot_general x1, matrix products, body(): jnp.einsum('stgpb,sbtd->stgpd', weights.astype(jnp.bfloat16), cache_view[...  2.26 us
  transfers between devices with their start and end apart: 1, of which 0 were waited for; matrix products, arithmetic and copies ran while one was open for 24% of the time, Pallas kernels for 47%

profile of v10, /device:TPU:1, one launch (start us, length us, event | category | flops | bytes accessed | tf_op | source)
XLA Modules:
  0.0 103.2 jit_solution(166181154008511090)
XLA Ops:
  0.6 17.8 %shard_map.113 = (bf16[16,20,128]{2,1,0:T(8,128)(2,1)}, bf16[64,2,128,128]{3,2,1,0:T(8,128)(2,1)}) custom-call(bf16[32,512]{1,0:T(8,128)(2,1)} %x_hbm.1, bf16[512,1280]{1,0:T(8,128)(2,1)} %w_hbm.1, f32[1,128]{1,0:T(1,128)} %constant.11.clone.freq_ref, s32[8]{0:T(128)} %lengths_ref.1, s32[1,4,16]{2,1,0:T(4,128)} %bitcast.139, bf16[64,2,128,128]{3,2,1,0:T(8,128)(2,1)} %kv_hbm.1), custom_call_target="tpu_custom_call" | custom-call | flops 41943040 | bytes 9699328 | tf_op jit(solution)/shard_map/pallas_call | solution.py:134
  18.5 4.5 %all-to-all-start = ((bf16[16,4,2,128,128]{4,3,2,1,0:T(8,128)(2,1)}), bf16[16,4,2,128,128]{4,3,2,1,0:T(8,128)(2,1)}, u32[]{:S(2)}, u32[]{:S(2)}) async-start(bf16[16,4,2,128,128]{4,3,2,1,0:T(8,128)(2,1)} %bitcast.125), calls=%async_computation | async-start | bytes 8388608 | tf_op jit(solution)/shard_map/all_to_all | solution.py:353
  23.1 0.0 copy-start.1
  23.1 0.0 copy-start.3
  23.1 4.8 %copy.132 = bf16[64,2,128,128]{3,2,0,1:T(8,128)(2,1)} copy(bf16[64,2,128,128]{3,2,1,0:T(8,128)(2,1)} %kv_hbm.1) | data formatting | bytes 8388608 | tf_op args[3]
  28.0 0.1 copy.76
  28.0 0.1 reshape.210
  28.2 0.4 fusion.38
  28.7 0.1 fusion.18
  28.8 0.3 convolution_select_fusion
  29.1 0.1 copy.90
  29.2 0.1 copy.85
  29.3 0.1 copy.86
  29.3 0.7 fusion.37
  30.0 4.9 %compare_select_fusion.2 = (s32[64]{0:T(128)S(1)}, s32[64]{0:T(128)S(1)}, s32[64]{0:T(128)S(1)}) fusion(s32[]{:T(128)} %bitcast.2, s32[]{:T(128)} %bitcast.3, s32[]{:T(128)} %bitcast.4, s32[]{:T(128)} %bitcast.5, s32[]{:T(128)} %bitcast.6, s32[]{:T(128)} %bitcast.7, s32[]{:T(128)} %bitcast.8, s32[]{:T(128)} %bitcast.9, s32[64]{0:T(128)S(1)} %copy-done.3, ...), kind=kLoop, calls=%fused_computation.61 | loop fusion | flops 1216 | bytes 1312 | tf_op jit(solution)/shard_map/gather | solution.py:368
  35.0 0.7 gather_fusion
  35.7 0.1 fusion.25
  35.8 2.9 %fusion.39 = (f32[64,8,4]{1,2,0:T(4,128)S(1)}, f32[64,1,8,4,128]{4,2,3,0,1:T(8,128)S(1)}) fusion(bf16[64,4,8,128]{3,2,1,0:T(8,128)(2,1)S(1)} %gather_fusion, bf16[64,2,128,1,128]{4,2,0,3,1:T(8,128)(2,1)} %bitcast.122, pred[64,128]{1,0:T(8,128)(4,1)S(1)} %fusion.25), kind=kOutput, calls=%fused_computation.78 | convolution fusion | flops 67893248 | bytes 3686400 | tf_op jit(solution)/shard_map/sptgd,sbtd->stgpb/dot_general | solution.py:372
  38.7 0.1 copy.79
  38.8 0.1 copy.81
  38.9 0.1 select_reduce_fusion
  39.0 0.1 copy.80
  39.1 0.1 copy.92
  39.2 0.1 copy.87
  39.2 0.8 fusion.14
  40.0 2.3 %fusion = f32[64,8,4,128]{3,2,1,0:T(4,128)S(1)} fusion(bf16[64,2,128,1,128]{4,2,0,3,1:T(8,128)(2,1)} %bitcast.123, bf16[64,8,4,128]{3,1,2,0:T(8,128)(2,1)S(1)} %get-tuple-element.13), kind=kOutput, calls=%fused_computation.5 | convolution fusion | flops 67108864 | bytes 3670016 | tf_op jit(solution)/shard_map/stgpb,sbtd->stgpd/dot_general | solution.py:383
  42.3 0.4 reshape.217
  42.7 0.6 gather_fusion.1
  43.3 0.1 bitcast_multiply_fusion.1
  43.4 0.3 mul.74
  43.7 1.1 %fusion.7 = bf16[8,32,128]{2,0,1:T(8,128)(2,1)S(1)} fusion(f32[8,32,128]{2,0,1:T(8,128)S(1)} %bitcast_multiply_fusion.1, f32[8,32]{0,1:T(8,128)S(1)} %copy.87, s32[64]{0:T(128)S(1)} %copy-done.3, f32[64,4096]{1,0:T(8,128)S(1)} %reshape.217, f32[8,8,32,128]{3,2,1,0:T(8,128)S(1)} %bitcast.124), kind=kOutput, calls=%fused_computation.15 | convolution fusion | flops 25526784 | bytes 2295040 | tf_op jit(solution)/shard_map/dot_general | solution.py:405
  44.9 0.7 copy.93
  45.5 0.1 copy.95
  45.6 0.1 copy.96
  45.7 0.1 copy.97
  45.8 0.1 copy.98
  45.8 0.1 fusion.9
  46.0 0.1 reshape.225
  46.1 0.1 reshape_reshape.7
  46.2 0.1 reshape.223
  46.3 0.1 reshape_reshape.6
  46.4 0.1 pad.3.clone
  46.4 0.1 maximum_maximum_fusion
  46.5 0.6 concatenate.7.stats_ref
  47.2 1.3 %scatter_custom_fusion = s32[65]{0:T(128)} fusion(s32[64]{0:T(128)S(1)} %fusion.32, s32[64]{0:T(128)S(1)} %iota.26, s32[]{:T(128)} %constant.13.clone.1), kind=kCustom, calls=%fused_computation.71 | custom fusion | bytes 264 | tf_op jit(solution)/shard_map/scatter | solution.py:359
  48.4 49.0 %shard_map.114 = bf16[4,512]{1,0:T(4,128)(2,1)} custom-call(bf16[16,16,128]{2,1,0:T(8,128)(2,1)} %bitcast.126, f32[16,8,128]{2,1,0:T(8,128)} %concatenate.7.stats_ref, bf16[1024,512]{1,0:T(8,128)(2,1)} %w_ref.1), custom_call_target="tpu_custom_call" | custom-call | flops 33554432 | bytes 1310720 | tf_op jit(solution)/shard_map/pallas_call | solution.py:221
  97.5 5.1 %shard_map.115 = bf16[64,2,128,128]{3,2,1,0:T(8,128)(2,1)} custom-call(s32[64]{0:T(128)} %bitcast.140, bf16[64,2,128,128]{3,2,1,0:T(8,128)(2,1)} %bitcast.45.src_hbm), custom_call_target="tpu_custom_call" | custom-call | bytes 8388608 | tf_op jit(solution)/shard_map/pallas_call | solution.py:283
  102.6 0.6 copy.136
  (28 shorter events, 0.2 us)
Async XLA Ops:
  18.5 79.0 %all-to-all-start = ((bf16[16,4,2,128,128]{4,3,2,1,0:T(8,128)(2,1)}), bf16[16,4,2,128,128]{4,3,2,1,0:T(8,128)(2,1)}, u32[]{:S(2)}, u32[]{:S(2)}) async-start(bf16[16,4,2,128,128]{4,3,2,1,0:T(8,128)(2,1)} %bitcast.125), calls=%async_computation | async-start | bytes 8388608 | tf_op jit(solution)/shard_map/all_to_all | solution.py:353
  23.1 4.9 %copy-start.4 = (s32[1,16,4]{1,2,0:T(4,128)S(1)}, s32[1,16,4]{1,2,0:T(4,128)}, u32[]{:S(2)}) copy-start(s32[1,16,4]{1,2,0:T(4,128)} %param.18) | copy-start | bytes 772
  23.1 5.1 %copy-start = (bf16[16,20,128]{2,1,0:T(8,128)(2,1)S(1)}, bf16[16,20,128]{2,1,0:T(8,128)(2,1)}, u32[]{:S(2)}) copy-start(bf16[16,20,128]{2,1,0:T(8,128)(2,1)} %get-tuple-element.7) | copy-start | bytes 245764
  23.1 6.3 %copy-start.1 = (s32[8]{0:T(128)S(1)}, s32[8]{0:T(128)}, u32[]{:S(2)}) copy-start(s32[8]{0:T(128)} %lengths_ref.1) | copy-start | bytes 100
  23.1 6.9 %copy-start.3 = (s32[64]{0:T(128)S(1)}, s32[64]{0:T(128)}, u32[]{:S(2)}) copy-start(s32[64]{0:T(128)} %param.15) | copy-start | bytes 772
  23.1 6.9 %copy-start.5 = (s32[64]{0:T(128)S(1)}, s32[64]{0:T(128)}, u32[]{:S(2)}) copy-start(s32[64]{0:T(128)} %param.16) | copy-start | bytes 772
  97.5 5.1 %copy-start.2 = (bf16[4,512]{1,0:T(4,128)(2,1)S(1)}, bf16[4,512]{1,0:T(4,128)(2,1)}, u32[]{:S(2)}) copy-start(bf16[4,512]{1,0:T(4,128)(2,1)} %shard_map.114) | copy-start | bytes 12292

commit v11 on v10

--- a/solution.py
+++ b/solution.py
@@ -200,9 +200,11 @@
         lhs = land_a[2 * g : 2 * g + 2].reshape(2 * rows, HEAD)
         term = jnp.dot(lhs, w_ref[g * HEAD : (g + 1) * HEAD, :], preferred_element_type=jnp.float32)
         projected = term if projected is None else projected + term
-    per = part_c.shape[1]
+    per = projected.shape[0] // m
+    pieces = projected.shape[1] // HEAD
     for j in range(m):
-        part_c[j] = projected[j * per : (j + 1) * per]
+        for q in range(pieces):
+            part_c[j, q * per : (q + 1) * per, :] = projected[j * per : (j + 1) * per, q * HEAD : (q + 1) * HEAD]
     land_c[me_h] = part_c[me_h]
     sent_c = _send_all("head", m, me_h, lambda p: part_c.at[p], land_c, sems.at[4], sems.at[5])
     _wait_all("head", m, me_h, land_c, sems.at[4], sems.at[5])
@@ -211,7 +213,8 @@
         total = total + land_c[j]
     for copy in sent_p + sent_s + sent_a + sent_c:
         copy.wait_send()
-    out_ref[...] = total.astype(out_ref.dtype)
+    for q in range(pieces):
+        out_ref[:, q * HEAD : (q + 1) * HEAD] = total[q * per : (q + 1) * per].astype(out_ref.dtype)
 
 
 def attend_exchange(acc, stats, out_weight, m):
@@ -228,8 +231,8 @@
             pltpu.VMEM(stats.shape, jnp.float32),
             pltpu.VMEM((rows, HEAD), jnp.bfloat16),
             pltpu.VMEM((n, rows, HEAD), jnp.bfloat16),
-            pltpu.VMEM((m, per, width), jnp.float32),
-            pltpu.VMEM((m, per, width), jnp.float32),
+            pltpu.VMEM((m, per * width // HEAD, HEAD), jnp.float32),
+            pltpu.VMEM((m, per * width // HEAD, HEAD), jnp.float32),
             pltpu.SemaphoreType.DMA((8, max(n, m))),
         ],
         compiler_params=pltpu.CompilerParams(collective_id=1, has_side_effects=True),

time: 104 us -> 104 us (level)
  no operation moved by 1% of the time
where the time goes in v11:
time: 104 us; the launch traced here: 103 us
  Pallas kernels  71.9 us (69%)
  local copies, waits for them, and re-layouts  12.3 us (12%)
  matrix products  7.13 us (7%)
  other arithmetic  6.28 us (6%)
  starting transfers between devices  4.55 us (4%)
    pallas_call x1, Pallas kernels, attend_exchange(): pl.pallas_call(functools.partial(_attend_kernel, n, m, rows), out_shape=j...  49 us
    pallas_call x1, Pallas kernels, qkv_exchange(): pl.pallas_call(functools.partial(_qkv_kernel, n, kv_cache.shape[0]), out_...  17.8 us
    unnamed x15, local copies, waits for them, and re-layouts  5.55 us
    pallas_call x1, Pallas kernels, pick_blocks(): pl.pallas_call(functools.partial(_pick_kernel, limit), out_shape=jax.Shap...  5.08 us
    gather x1, other arithmetic, body(): token_valid = (token_pos < lengths[slot_clip][:, None]) & live_slot[:, None]  4.94 us
    all_to_all x1, starting transfers between devices, body(): lax.all_to_all(outgoing, 'seq', split_axis=0, concat_axis=0, tiled=True)  4.55 us
    dot_general x1, matrix products, body(): jnp.einsum('sptgd,sbtd->stgpb', gathered, cache_view[:, 0], preferred_ele...  2.91 us
    dot_general x1, matrix products, body(): jnp.einsum('stgpb,sbtd->stgpd', weights.astype(jnp.bfloat16), cache_view[...  2.26 us
  transfers between devices with their start and end apart: 1, of which 0 were waited for; matrix products, arithmetic and copies ran while one was open for 24% of the time, Pallas kernels for 47%

profile of v11, /device:TPU:1, one launch (start us, length us, event | category | flops | bytes accessed | tf_op | source)
XLA Modules:
  0.0 103.2 jit_solution(2765274203106089890)
XLA Ops:
  0.6 17.8 %shard_map.113 = (bf16[16,20,128]{2,1,0:T(8,128)(2,1)}, bf16[64,2,128,128]{3,2,1,0:T(8,128)(2,1)}) custom-call(bf16[32,512]{1,0:T(8,128)(2,1)} %x_hbm.1, bf16[512,1280]{1,0:T(8,128)(2,1)} %w_hbm.1, f32[1,128]{1,0:T(1,128)} %constant.11.clone.freq_ref, s32[8]{0:T(128)} %lengths_ref.1, s32[1,4,16]{2,1,0:T(4,128)} %bitcast.139, bf16[64,2,128,128]{3,2,1,0:T(8,128)(2,1)} %kv_hbm.1), custom_call_target="tpu_custom_call" | custom-call | flops 41943040 | bytes 9699328 | tf_op jit(solution)/shard_map/pallas_call | solution.py:134
  18.5 4.5 %all-to-all-start = ((bf16[16,4,2,128,128]{4,3,2,1,0:T(8,128)(2,1)}), bf16[16,4,2,128,128]{4,3,2,1,0:T(8,128)(2,1)}, u32[]{:S(2)}, u32[]{:S(2)}) async-start(bf16[16,4,2,128,128]{4,3,2,1,0:T(8,128)(2,1)} %bitcast.125), calls=%async_computation | async-start | bytes 8388608 | tf_op jit(solution)/shard_map/all_to_all | solution.py:356
  23.1 0.0 copy-start.1
  23.1 0.0 copy-start.3
  23.1 4.8 %copy.132 = bf16[64,2,128,128]{3,2,0,1:T(8,128)(2,1)} copy(bf16[64,2,128,128]{3,2,1,0:T(8,128)(2,1)} %kv_hbm.1) | data formatting | bytes 8388608 | tf_op args[3]
  28.0 0.1 copy.76
  28.0 0.1 reshape.210
  28.2 0.4 fusion.38
  28.7 0.1 fusion.18
  28.8 0.3 convolution_select_fusion
  29.1 0.1 copy.90
  29.2 0.1 copy.85
  29.3 0.1 copy.86
  29.3 0.7 fusion.37
  30.0 4.9 %compare_select_fusion.2 = (s32[64]{0:T(128)S(1)}, s32[64]{0:T(128)S(1)}, s32[64]{0:T(128)S(1)}) fusion(s32[]{:T(128)} %bitcast.2, s32[]{:T(128)} %bitcast.3, s32[]{:T(128)} %bitcast.4, s32[]{:T(128)} %bitcast.5, s32[]{:T(128)} %bitcast.6, s32[]{:T(128)} %bitcast.7, s32[]{:T(128)} %bitcast.8, s32[]{:T(128)} %bitcast.9, s32[64]{0:T(128)S(1)} %copy-done.3, ...), kind=kLoop, calls=%fused_computation.61 | loop fusion | flops 1216 | bytes 1312 | tf_op jit(solution)/shard_map/gather | solution.py:371
  35.0 0.7 gather_fusion
  35.7 0.1 fusion.25
  35.8 2.9 %fusion.39 = (f32[64,8,4]{1,2,0:T(4,128)S(1)}, f32[64,1,8,4,128]{4,2,3,0,1:T(8,128)S(1)}) fusion(bf16[64,4,8,128]{3,2,1,0:T(8,128)(2,1)S(1)} %gather_fusion, bf16[64,2,128,1,128]{4,2,0,3,1:T(8,128)(2,1)} %bitcast.122, pred[64,128]{1,0:T(8,128)(4,1)S(1)} %fusion.25), kind=kOutput, calls=%fused_computation.78 | convolution fusion | flops 67893248 | bytes 3686400 | tf_op jit(solution)/shard_map/sptgd,sbtd->stgpb/dot_general | solution.py:375
  38.7 0.1 copy.79
  38.8 0.1 copy.81
  38.9 0.1 select_reduce_fusion
  39.0 0.1 copy.80
  39.1 0.1 copy.92
  39.2 0.1 copy.87
  39.2 0.8 fusion.14
  40.0 2.3 %fusion = f32[64,8,4,128]{3,2,1,0:T(4,128)S(1)} fusion(bf16[64,2,128,1,128]{4,2,0,3,1:T(8,128)(2,1)} %bitcast.123, bf16[64,8,4,128]{3,1,2,0:T(8,128)(2,1)S(1)} %get-tuple-element.13), kind=kOutput, calls=%fused_computation.5 | convolution fusion | flops 67108864 | bytes 3670016 | tf_op jit(solution)/shard_map/stgpb,sbtd->stgpd/dot_general | solution.py:386
  42.3 0.4 reshape.217
  42.7 0.6 gather_fusion.1
  43.3 0.1 bitcast_multiply_fusion.1
  43.4 0.3 mul.74
  43.7 1.1 %fusion.7 = bf16[8,32,128]{2,0,1:T(8,128)(2,1)S(1)} fusion(f32[8,32,128]{2,0,1:T(8,128)S(1)} %bitcast_multiply_fusion.1, f32[8,32]{0,1:T(8,128)S(1)} %copy.87, s32[64]{0:T(128)S(1)} %copy-done.3, f32[64,4096]{1,0:T(8,128)S(1)} %reshape.217, f32[8,8,32,128]{3,2,1,0:T(8,128)S(1)} %bitcast.124), kind=kOutput, calls=%fused_computation.15 | convolution fusion | flops 25526784 | bytes 2295040 | tf_op jit(solution)/shard_map/dot_general | solution.py:408
  44.9 0.7 copy.93
  45.5 0.1 copy.95
  45.6 0.1 copy.96
  45.7 0.1 copy.97
  45.8 0.1 copy.98
  45.8 0.1 fusion.9
  46.0 0.1 reshape.225
  46.1 0.1 reshape_reshape.7
  46.2 0.1 reshape.223
  46.3 0.1 reshape_reshape.6
  46.4 0.1 pad.3.clone
  46.4 0.1 maximum_maximum_fusion
  46.5 0.6 concatenate.7.stats_ref
  47.2 1.3 %scatter_custom_fusion = s32[65]{0:T(128)} fusion(s32[64]{0:T(128)S(1)} %fusion.32, s32[64]{0:T(128)S(1)} %iota.26, s32[]{:T(128)} %constant.13.clone.1), kind=kCustom, calls=%fused_computation.71 | custom fusion | bytes 264 | tf_op jit(solution)/shard_map/scatter | solution.py:362
  48.4 49.0 %shard_map.114 = bf16[4,512]{1,0:T(4,128)(2,1)} custom-call(bf16[16,16,128]{2,1,0:T(8,128)(2,1)} %bitcast.126, f32[16,8,128]{2,1,0:T(8,128)} %concatenate.7.stats_ref, bf16[1024,512]{1,0:T(8,128)(2,1)} %w_ref.1), custom_call_target="tpu_custom_call" | custom-call | flops 33554432 | bytes 1310720 | tf_op jit(solution)/shard_map/pallas_call | solution.py:224
  97.5 5.1 %shard_map.115 = bf16[64,2,128,128]{3,2,1,0:T(8,128)(2,1)} custom-call(s32[64]{0:T(128)} %bitcast.140, bf16[64,2,128,128]{3,2,1,0:T(8,128)(2,1)} %bitcast.45.src_hbm), custom_call_target="tpu_custom_call" | custom-call | bytes 8388608 | tf_op jit(solution)/shard_map/pallas_call | solution.py:286
  102.6 0.6 copy.136
  (28 shorter events, 0.2 us)
Async XLA Ops:
  18.5 79.0 %all-to-all-start = ((bf16[16,4,2,128,128]{4,3,2,1,0:T(8,128)(2,1)}), bf16[16,4,2,128,128]{4,3,2,1,0:T(8,128)(2,1)}, u32[]{:S(2)}, u32[]{:S(2)}) async-start(bf16[16,4,2,128,128]{4,3,2,1,0:T(8,128)(2,1)} %bitcast.125), calls=%async_computation | async-start | bytes 8388608 | tf_op jit(solution)/shard_map/all_to_all | solution.py:356
  23.1 4.9 %copy-start.4 = (s32[1,16,4]{1,2,0:T(4,128)S(1)}, s32[1,16,4]{1,2,0:T(4,128)}, u32[]{:S(2)}) copy-start(s32[1,16,4]{1,2,0:T(4,128)} %param.18) | copy-start | bytes 772
  23.1 5.1 %copy-start = (bf16[16,20,128]{2,1,0:T(8,128)(2,1)S(1)}, bf16[16,20,128]{2,1,0:T(8,128)(2,1)}, u32[]{:S(2)}) copy-start(bf16[16,20,128]{2,1,0:T(8,128)(2,1)} %get-tuple-element.7) | copy-start | bytes 245764
  23.1 6.3 %copy-start.1 = (s32[8]{0:T(128)S(1)}, s32[8]{0:T(128)}, u32[]{:S(2)}) copy-start(s32[8]{0:T(128)} %lengths_ref.1) | copy-start | bytes 100
  23.1 6.9 %copy-start.3 = (s32[64]{0:T(128)S(1)}, s32[64]{0:T(128)}, u32[]{:S(2)}) copy-start(s32[64]{0:T(128)} %param.15) | copy-start | bytes 772
  23.1 6.9 %copy-start.5 = (s32[64]{0:T(128)S(1)}, s32[64]{0:T(128)}, u32[]{:S(2)}) copy-start(s32[64]{0:T(128)} %param.16) | copy-start | bytes 772
  97.5 5.1 %copy-start.2 = (bf16[4,512]{1,0:T(4,128)(2,1)S(1)}, bf16[4,512]{1,0:T(4,128)(2,1)}, u32[]{:S(2)}) copy-start(bf16[4,512]{1,0:T(4,128)(2,1)} %shard_map.114) | copy-start | bytes 12292

commit v12 on v10

--- a/solution.py
+++ b/solution.py
@@ -164,11 +164,13 @@
 
 
 def _attend_kernel(
-    n, m, rows, acc_ref, stats_ref, w_ref, out_ref, land_p, land_s, mine, land_a, part_c, land_c,
-    sems,
+    n, m, rows, limit, acc_ref, stats_ref, w_ref, place_ref, got_hbm, out_ref, moved_hbm,
+    land_p, land_s, mine, land_a, part_c, land_c, sems, got_vmem, moved_vmem, local_sems,
 ):
     me = lax.axis_index("seq")
     me_h = lax.axis_index("head")
+    got_in = pltpu.make_async_copy(got_hbm, got_vmem, local_sems.at[0])
+    got_in.start()
     land_p[me] = acc_ref[me]
     land_s[me] = stats_ref[me]
     _barrier(
@@ -177,6 +179,17 @@
     )
     sent_p = _send_all("seq", n, me, lambda p: acc_ref.at[p], land_p, sems.at[0], sems.at[1])
     sent_s = _send_all("seq", n, me, lambda p: stats_ref.at[p], land_s, sems.at[6], sems.at[7])
+    got_in.wait()
+
+    def place(k, carry):
+        src = place_ref[k]
+        block = got_vmem[jnp.minimum(src, limit - 1)]
+        moved_vmem[k] = jnp.where(src < limit, block, jnp.zeros_like(block))
+        return carry
+
+    lax.fori_loop(0, moved_vmem.shape[0], place, 0)
+    moved_out = pltpu.make_async_copy(moved_vmem, moved_hbm, local_sems.at[1])
+    moved_out.start()
     _wait_all("seq", n, me, land_s, sems.at[6], sems.at[7])
     _wait_all("seq", n, me, land_p, sems.at[0], sems.at[1])
     columns = [land_s[i].T for i in range(n)]
@@ -212,17 +225,23 @@
     for copy in sent_p + sent_s + sent_a + sent_c:
         copy.wait_send()
     out_ref[...] = total.astype(out_ref.dtype)
-
-
-def attend_exchange(acc, stats, out_weight, m):
+    moved_out.wait()
+
+
+def attend_exchange(acc, stats, out_weight, m, place, got):
     n, rows, _ = acc.shape
     width = out_weight.shape[1]
     per = 2 * rows // m
+    moved = (place.shape[0],) + got.shape[1:]
     return pl.pallas_call(
-        functools.partial(_attend_kernel, n, m, rows),
-        out_shape=jax.ShapeDtypeStruct((per, width), jnp.bfloat16),
-        in_specs=[pl.BlockSpec(memory_space=pltpu.VMEM)] * 3,
-        out_specs=pl.BlockSpec(memory_space=pltpu.VMEM),
+        functools.partial(_attend_kernel, n, m, rows, got.shape[0]),
+        out_shape=(
+            jax.ShapeDtypeStruct((per, width), jnp.bfloat16),
+            jax.ShapeDtypeStruct(moved, got.dtype),
+        ),
+        in_specs=[pl.BlockSpec(memory_space=pltpu.VMEM)] * 3
+        + [pl.BlockSpec(memory_space=pltpu.SMEM), pl.BlockSpec(memory_space=pl.ANY)],
+        out_specs=(pl.BlockSpec(memory_space=pltpu.VMEM), pl.BlockSpec(memory_space=pl.ANY)),
         scratch_shapes=[
             pltpu.VMEM(acc.shape, acc.dtype),
             pltpu.VMEM(stats.shape, jnp.float32),
@@ -231,14 +250,17 @@
             pltpu.VMEM((m, per, width), jnp.float32),
             pltpu.VMEM((m, per, width), jnp.float32),
             pltpu.SemaphoreType.DMA((8, max(n, m))),
+            pltpu.VMEM(got.shape, got.dtype),
+            pltpu.VMEM(moved, got.dtype),
+            pltpu.SemaphoreType.DMA((2,)),
         ],
         compiler_params=pltpu.CompilerParams(collective_id=1, has_side_effects=True),
         cost_estimate=pl.CostEstimate(
             flops=2 * 2 * rows * out_weight.shape[0] * width,
-            bytes_accessed=acc.size * 4 + stats.size * 8 + out_weight.size * 2,
+            bytes_accessed=acc.size * 4 + stats.size * 8 + out_weight.size * 2 + 2 * got.size * 2,
             transcendentals=n * rows * HEAD,
         ),
-    )(acc, stats, out_weight)
+    )(acc, stats, out_weight, place, got)
 
 
 def _pick_kernel(limit, index_ref, src_hbm, out_hbm, buf, sems, out_sem):
@@ -447,8 +469,7 @@
     stats = jnp.concatenate([stats_row, jnp.zeros((n_seq, 7, HEAD), jnp.float32)], axis=1)
     acc_chunks = by_chunk(part_acc).astype(jnp.bfloat16)
     source_of, acc_chunks, stats = lax.optimization_barrier((source_of, acc_chunks, stats))
-    projected = attend_exchange(acc_chunks, stats, out_weight, n_head)
-    moved_cache = pick_blocks(source_of, incoming, arrivals)
+    projected, moved_cache = attend_exchange(acc_chunks, stats, out_weight, n_head, source_of, incoming)
     return (projected, moved_cache)
 
 

time: 104 us -> 112 us (1.077)
  waiting for transfers between devices: 0.01 us -> 32 us
  Pallas kernels: 71.9 us -> 43 us
  local copies, waits for them, and re-layouts: 12.3 us -> 17.8 us
    all_to_all x1, waiting for transfers between devices: 0.01 us -> 32 us  [body(): lax.all_to_all(outgoing, 'seq', split_axis=0, concat_axis=0, tiled=True)]
    pallas_call x2 -> x1, Pallas kernels: 54.1 us -> 25.2 us  [attend_exchange(): pl.pallas_call(functools.partial(_attend_kernel, n, m, rows, got.shape[0]...]
    unnamed x15 -> x14, local copies, waits for them, and re-layouts: 5.55 us -> 11 us
  transfers between devices with their start and end apart: 1 -> 1, of which waited for: 0 -> 1; matrix products, arithmetic and copies ran while one was open for 24% -> 22% of each run, Pallas kernels for 47% -> 0%
where the time goes in v12:
time: 112 us
  Pallas kernels  43 us (38%)
  waiting for transfers between devices  32 us (29%)
  local copies, waits for them, and re-layouts  17.8 us (16%)
  matrix products  7.13 us (6%)
  other arithmetic  6.28 us (6%)
  starting transfers between devices  4.55 us (4%)
    all_to_all x1, waiting for transfers between devices, body(): lax.all_to_all(outgoing, 'seq', split_axis=0, concat_axis=0, tiled=True)  32 us
    pallas_call x1, Pallas kernels, attend_exchange(): pl.pallas_call(functools.partial(_attend_kernel, n, m, rows, got.shape[0]...  25.2 us
    pallas_call x1, Pallas kernels, qkv_exchange(): pl.pallas_call(functools.partial(_qkv_kernel, n, kv_cache.shape[0]), out_...  17.8 us
    unnamed x14, local copies, waits for them, and re-layouts  11 us
    gather x1, other arithmetic, body(): token_valid = (token_pos < lengths[slot_clip][:, None]) & live_slot[:, None]  4.94 us
    all_to_all x1, starting transfers between devices, body(): lax.all_to_all(outgoing, 'seq', split_axis=0, concat_axis=0, tiled=True)  4.55 us
    dot_general x1, matrix products, body(): jnp.einsum('sptgd,sbtd->stgpb', gathered, cache_view[:, 0], preferred_ele...  2.91 us
    dot_general x1, matrix products, body(): jnp.einsum('stgpb,sbtd->stgpd', weights.astype(jnp.bfloat16), cache_view[...  2.26 us
  transfers between devices with their start and end apart: 1, of which 1 were waited for; matrix products, arithmetic and copies ran while one was open for 22% of the time, Pallas kernels for 0%

profile of v12, /device:TPU:1, one launch (start us, length us, event | category | flops | bytes accessed | tf_op | source)
XLA Modules:
  0.0 111.7 jit_solution(15541708415138275305)
XLA Ops:
  0.6 17.8 %shard_map.113 = (bf16[16,20,128]{2,1,0:T(8,128)(2,1)}, bf16[64,2,128,128]{3,2,1,0:T(8,128)(2,1)}) custom-call(bf16[32,512]{1,0:T(8,128)(2,1)} %x_hbm.1, bf16[512,1280]{1,0:T(8,128)(2,1)} %w_hbm.1, f32[1,128]{1,0:T(1,128)} %constant.11.clone.freq_ref, s32[8]{0:T(128)} %lengths_ref.1, s32[1,4,16]{2,1,0:T(4,128)} %bitcast.139, bf16[64,2,128,128]{3,2,1,0:T(8,128)(2,1)} %kv_hbm.1), custom_call_target="tpu_custom_call" | custom-call | flops 41943040 | bytes 9699328 | tf_op jit(solution)/shard_map/pallas_call | solution.py:134
  18.5 4.5 %all-to-all-start = ((bf16[16,4,2,128,128]{4,3,2,1,0:T(8,128)(2,1)}), bf16[16,4,2,128,128]{4,3,2,1,0:T(8,128)(2,1)}, u32[]{:S(2)}, u32[]{:S(2)}) async-start(bf16[16,4,2,128,128]{4,3,2,1,0:T(8,128)(2,1)} %bitcast.125), calls=%async_computation | async-start | bytes 8388608 | tf_op jit(solution)/shard_map/all_to_all | solution.py:375
  23.1 0.0 copy-start.1
  23.1 4.8 %copy.132 = bf16[64,2,128,128]{3,2,0,1:T(8,128)(2,1)} copy(bf16[64,2,128,128]{3,2,1,0:T(8,128)(2,1)} %kv_hbm.1) | data formatting | bytes 8388608 | tf_op args[3]
  28.0 0.1 copy.76
  28.0 0.1 reshape.210
  28.2 0.4 fusion.38
  28.7 0.1 fusion.18
  28.8 0.3 convolution_select_fusion
  29.1 0.1 copy.90
  29.2 0.1 copy.85
  29.3 0.1 copy.86
  29.3 0.7 fusion.37
  30.0 4.9 %compare_select_fusion.2 = (s32[64]{0:T(128)S(1)}, s32[64]{0:T(128)S(1)}, s32[64]{0:T(128)S(1)}) fusion(s32[]{:T(128)} %bitcast.2, s32[]{:T(128)} %bitcast.3, s32[]{:T(128)} %bitcast.4, s32[]{:T(128)} %bitcast.5, s32[]{:T(128)} %bitcast.6, s32[]{:T(128)} %bitcast.7, s32[]{:T(128)} %bitcast.8, s32[]{:T(128)} %bitcast.9, s32[64]{0:T(128)S(1)} %copy-done.2, ...), kind=kLoop, calls=%fused_computation.61 | loop fusion | flops 1216 | bytes 1312 | tf_op jit(solution)/shard_map/gather | solution.py:390
  35.0 0.7 gather_fusion
  35.7 0.1 fusion.25
  35.8 2.9 %fusion.39 = (f32[64,8,4]{1,2,0:T(4,128)S(1)}, f32[64,1,8,4,128]{4,2,3,0,1:T(8,128)S(1)}) fusion(bf16[64,4,8,128]{3,2,1,0:T(8,128)(2,1)S(1)} %gather_fusion, bf16[64,2,128,1,128]{4,2,0,3,1:T(8,128)(2,1)} %bitcast.122, pred[64,128]{1,0:T(8,128)(4,1)S(1)} %fusion.25), kind=kOutput, calls=%fused_computation.78 | convolution fusion | flops 67893248 | bytes 3686400 | tf_op jit(solution)/shard_map/sptgd,sbtd->stgpb/dot_general | solution.py:394
  38.7 0.1 copy.79
  38.8 0.1 copy.81
  38.9 0.1 select_reduce_fusion
  39.0 0.1 copy.80
  39.1 0.1 copy.92
  39.2 0.1 copy.87
  39.2 0.8 fusion.14
  40.0 2.3 %fusion = f32[64,8,4,128]{3,2,1,0:T(4,128)S(1)} fusion(bf16[64,2,128,1,128]{4,2,0,3,1:T(8,128)(2,1)} %bitcast.123, bf16[64,8,4,128]{3,1,2,0:T(8,128)(2,1)S(1)} %get-tuple-element.13), kind=kOutput, calls=%fused_computation.5 | convolution fusion | flops 67108864 | bytes 3670016 | tf_op jit(solution)/shard_map/stgpb,sbtd->stgpd/dot_general | solution.py:405
  42.3 0.4 reshape.217
  42.7 0.6 gather_fusion.1
  43.3 0.1 bitcast_multiply_fusion.1
  43.4 0.3 mul.74
  43.7 1.1 fusion.7
  44.9 0.7 copy.93
  45.5 0.1 copy.95
  45.6 0.1 copy.96
  45.7 0.1 copy.97
  45.8 0.1 copy.98
  45.8 0.1 fusion.9
  46.0 0.1 reshape.225
  46.1 0.1 reshape_reshape.7
  46.2 0.1 reshape.223
  46.3 0.1 reshape_reshape.6
  46.4 0.1 pad.3.clone
  46.4 0.1 maximum_maximum_fusion
  46.5 0.6 concatenate.7.stats_ref
  47.2 1.3 %scatter_custom_fusion = s32[65]{0:T(128)} fusion(s32[64]{0:T(128)S(1)} %fusion.32, s32[64]{0:T(128)S(1)} %iota.26, s32[]{:T(128)} %constant.13.clone.1), kind=kCustom, calls=%fused_computation.71 | custom fusion | bytes 264 | tf_op jit(solution)/shard_map/scatter | solution.py:381
  48.4 32.0 %all-to-all-done = bf16[16,4,2,128,128]{4,3,2,1,0:T(8,128)(2,1)} async-done(((bf16[16,4,2,128,128]{4,3,2,1,0:T(8,128)(2,1)}), bf16[16,4,2,128,128]{4,3,2,1,0:T(8,128)(2,1)}, u32[]{:S(2)}, u32[]{:S(2)}) %all-to-all-start) | async-done | bytes 4194336 | tf_op jit(solution)/shard_map/all_to_all | solution.py:375
  80.5 25.2 %shard_map.114 = (bf16[4,512]{1,0:T(4,128)(2,1)}, bf16[64,2,128,128]{3,2,1,0:T(8,128)(2,1)}) custom-call(bf16[16,16,128]{2,1,0:T(8,128)(2,1)} %bitcast.126, f32[16,8,128]{2,1,0:T(8,128)} %concatenate.7.stats_ref, bf16[1024,512]{1,0:T(8,128)(2,1)} %w_ref.1, s32[64]{0:T(128)} %bitcast.140, bf16[64,2,128,128]{3,2,1,0:T(8,128)(2,1)} %bitcast.45.got_hbm), custom_call_target="tpu_custom_call" | custom-call | flops 33554432 | bytes 9699328 | tf_op jit(solution)/shard_map/pallas_call | solution.py:236
  105.7 1.3 %copy.137 = bf16[4,512]{1,0:T(4,128)(2,1)} copy(bf16[4,512]{1,0:T(4,128)(2,1)} %get-tuple-element.38) | data formatting | bytes 8192
  107.0 4.8 %copy.138 = bf16[64,2,128,128]{3,2,1,0:T(8,128)(2,1)} copy(bf16[64,2,128,128]{3,2,1,0:T(8,128)(2,1)} %get-tuple-element.39) | data formatting | bytes 8388608
  (26 shorter events, 0.2 us)
Async XLA Ops:
  18.5 62.0 %all-to-all-start = ((bf16[16,4,2,128,128]{4,3,2,1,0:T(8,128)(2,1)}), bf16[16,4,2,128,128]{4,3,2,1,0:T(8,128)(2,1)}, u32[]{:S(2)}, u32[]{:S(2)}) async-start(bf16[16,4,2,128,128]{4,3,2,1,0:T(8,128)(2,1)} %bitcast.125), calls=%async_computation | async-start | bytes 8388608 | tf_op jit(solution)/shard_map/all_to_all | solution.py:375
  23.1 4.9 %copy-start.3 = (s32[1,16,4]{1,2,0:T(4,128)S(1)}, s32[1,16,4]{1,2,0:T(4,128)}, u32[]{:S(2)}) copy-start(s32[1,16,4]{1,2,0:T(4,128)} %param.18) | copy-start | bytes 772
  23.1 5.1 %copy-start = (bf16[16,20,128]{2,1,0:T(8,128)(2,1)S(1)}, bf16[16,20,128]{2,1,0:T(8,128)(2,1)}, u32[]{:S(2)}) copy-start(bf16[16,20,128]{2,1,0:T(8,128)(2,1)} %get-tuple-element.7) | copy-start | bytes 245764
  23.1 6.3 %copy-start.1 = (s32[8]{0:T(128)S(1)}, s32[8]{0:T(128)}, u32[]{:S(2)}) copy-start(s32[8]{0:T(128)} %lengths_ref.1) | copy-start | bytes 100
  23.1 6.9 %copy-start.2 = (s32[64]{0:T(128)S(1)}, s32[64]{0:T(128)}, u32[]{:S(2)}) copy-start(s32[64]{0:T(128)} %param.15) | copy-start | bytes 772
  23.1 6.9 %copy-start.4 = (s32[64]{0:T(128)S(1)}, s32[64]{0:T(128)}, u32[]{:S(2)}) copy-start(s32[64]{0:T(128)} %param.16) | copy-start | bytes 772

commit v13 on v10

--- a/solution.py
+++ b/solution.py
@@ -89,16 +89,6 @@
     land_a[me] = part_ref[me]
     pl.semaphore_wait(barrier, n - 1)
     sent_a = _send_all("seq", n, me, lambda p: part_ref.at[p], land_a, sems.at[0], sems.at[1])
-    kv_in.wait()
-
-    def pick(j, carry):
-        per = pick_ref.shape[1]
-        sent_vmem[j] = kv_vmem[jnp.minimum(pick_ref[0, j % per, j // per], limit - 1)]
-        return carry
-
-    lax.fori_loop(0, sent_vmem.shape[0], pick, 0)
-    kv_out = pltpu.make_async_copy(sent_vmem, sent_hbm, local_sems.at[1])
-    kv_out.start()
     _wait_all("seq", n, me, land_a, sems.at[0], sems.at[1])
     total = land_a[0]
     for i in range(1, n):
@@ -119,6 +109,16 @@
     mine[...] = rotated
     land_b[me] = rotated
     sent_b = _send_all("seq", n, me, lambda p: mine, land_b, sems.at[2], sems.at[3])
+    kv_in.wait()
+
+    def pick(j, carry):
+        per = pick_ref.shape[1]
+        sent_vmem[j] = kv_vmem[jnp.minimum(pick_ref[0, j % per, j // per], limit - 1)]
+        return carry
+
+    lax.fori_loop(0, sent_vmem.shape[0], pick, 0)
+    kv_out = pltpu.make_async_copy(sent_vmem, sent_hbm, local_sems.at[1])
+    kv_out.start()
     _wait_all("seq", n, me, land_b, sems.at[2], sems.at[3])
     for copy in sent_a + sent_b:
         copy.wait_send()

time: 104 us -> 104 us (level)
  no operation moved by 1% of the time
where the time goes in v13:
time: 104 us; the launch traced here: 103 us
  Pallas kernels  72 us (69%)
  local copies, waits for them, and re-layouts  12.3 us (12%)
  matrix products  7.13 us (7%)
  other arithmetic  6.28 us (6%)
  starting transfers between devices  4.55 us (4%)
    pallas_call x1, Pallas kernels, attend_exchange(): pl.pallas_call(functools.partial(_attend_kernel, n, m, rows), out_shape=j...  49 us
    pallas_call x1, Pallas kernels, qkv_exchange(): pl.pallas_call(functools.partial(_qkv_kernel, n, kv_cache.shape[0]), out_...  17.8 us
    unnamed x15, local copies, waits for them, and re-layouts  5.55 us
    pallas_call x1, Pallas kernels, pick_blocks(): pl.pallas_call(functools.partial(_pick_kernel, limit), out_shape=jax.Shap...  5.14 us
    gather x1, other arithmetic, body(): token_valid = (token_pos < lengths[slot_clip][:, None]) & live_slot[:, None]  4.94 us
    all_to_all x1, starting transfers between devices, body(): lax.all_to_all(outgoing, 'seq', split_axis=0, concat_axis=0, tiled=True)  4.55 us
    dot_general x1, matrix products, body(): jnp.einsum('sptgd,sbtd->stgpb', gathered, cache_view[:, 0], preferred_ele...  2.91 us
    dot_general x1, matrix products, body(): jnp.einsum('stgpb,sbtd->stgpd', weights.astype(jnp.bfloat16), cache_view[...  2.26 us
  transfers between devices with their start and end apart: 1, of which 0 were waited for; matrix products, arithmetic and copies ran while one was open for 24% of the time, Pallas kernels for 47%

profile of v13, /device:TPU:1, one launch (start us, length us, event | category | flops | bytes accessed | tf_op | source)
XLA Modules:
  0.0 103.2 jit_solution(12073150300294249085)
XLA Ops:
  0.6 17.8 %shard_map.113 = (bf16[16,20,128]{2,1,0:T(8,128)(2,1)}, bf16[64,2,128,128]{3,2,1,0:T(8,128)(2,1)}) custom-call(bf16[32,512]{1,0:T(8,128)(2,1)} %x_hbm.1, bf16[512,1280]{1,0:T(8,128)(2,1)} %w_hbm.1, f32[1,128]{1,0:T(1,128)} %constant.11.clone.freq_ref, s32[8]{0:T(128)} %lengths_ref.1, s32[1,4,16]{2,1,0:T(4,128)} %bitcast.139, bf16[64,2,128,128]{3,2,1,0:T(8,128)(2,1)} %kv_hbm.1), custom_call_target="tpu_custom_call" | custom-call | flops 41943040 | bytes 9699328 | tf_op jit(solution)/shard_map/pallas_call | solution.py:134
  18.5 4.5 %all-to-all-start = ((bf16[16,4,2,128,128]{4,3,2,1,0:T(8,128)(2,1)}), bf16[16,4,2,128,128]{4,3,2,1,0:T(8,128)(2,1)}, u32[]{:S(2)}, u32[]{:S(2)}) async-start(bf16[16,4,2,128,128]{4,3,2,1,0:T(8,128)(2,1)} %bitcast.125), calls=%async_computation | async-start | bytes 8388608 | tf_op jit(solution)/shard_map/all_to_all | solution.py:353
  23.1 0.0 copy-start.4
  23.1 0.0 copy-start.1
  23.1 4.8 %copy.132 = bf16[64,2,128,128]{3,2,0,1:T(8,128)(2,1)} copy(bf16[64,2,128,128]{3,2,1,0:T(8,128)(2,1)} %kv_hbm.1) | data formatting | bytes 8388608 | tf_op args[3]
  28.0 0.1 copy.76
  28.0 0.1 reshape.210
  28.2 0.4 fusion.38
  28.7 0.1 fusion.18
  28.8 0.3 convolution_select_fusion
  29.1 0.1 copy.90
  29.2 0.1 copy.85
  29.3 0.1 copy.86
  29.3 0.7 fusion.37
  30.0 4.9 %compare_select_fusion.2 = (s32[64]{0:T(128)S(1)}, s32[64]{0:T(128)S(1)}, s32[64]{0:T(128)S(1)}) fusion(s32[]{:T(128)} %bitcast.2, s32[]{:T(128)} %bitcast.3, s32[]{:T(128)} %bitcast.4, s32[]{:T(128)} %bitcast.5, s32[]{:T(128)} %bitcast.6, s32[]{:T(128)} %bitcast.7, s32[]{:T(128)} %bitcast.8, s32[]{:T(128)} %bitcast.9, s32[64]{0:T(128)S(1)} %copy-done.3, ...), kind=kLoop, calls=%fused_computation.61 | loop fusion | flops 1216 | bytes 1312 | tf_op jit(solution)/shard_map/gather | solution.py:368
  35.0 0.7 gather_fusion
  35.7 0.1 fusion.25
  35.8 2.9 %fusion.39 = (f32[64,8,4]{1,2,0:T(4,128)S(1)}, f32[64,1,8,4,128]{4,2,3,0,1:T(8,128)S(1)}) fusion(bf16[64,4,8,128]{3,2,1,0:T(8,128)(2,1)S(1)} %gather_fusion, bf16[64,2,128,1,128]{4,2,0,3,1:T(8,128)(2,1)} %bitcast.122, pred[64,128]{1,0:T(8,128)(4,1)S(1)} %fusion.25), kind=kOutput, calls=%fused_computation.78 | convolution fusion | flops 67893248 | bytes 3686400 | tf_op jit(solution)/shard_map/sptgd,sbtd->stgpb/dot_general | solution.py:372
  38.7 0.1 copy.79
  38.8 0.1 copy.81
  38.9 0.1 select_reduce_fusion
  39.0 0.1 copy.80
  39.1 0.1 copy.92
  39.2 0.1 copy.87
  39.2 0.8 fusion.14
  40.0 2.3 %fusion = f32[64,8,4,128]{3,2,1,0:T(4,128)S(1)} fusion(bf16[64,2,128,1,128]{4,2,0,3,1:T(8,128)(2,1)} %bitcast.123, bf16[64,8,4,128]{3,1,2,0:T(8,128)(2,1)S(1)} %get-tuple-element.13), kind=kOutput, calls=%fused_computation.5 | convolution fusion | flops 67108864 | bytes 3670016 | tf_op jit(solution)/shard_map/stgpb,sbtd->stgpd/dot_general | solution.py:383
  42.3 0.4 reshape.217
  42.7 0.6 gather_fusion.1
  43.3 0.1 bitcast_multiply_fusion.1
  43.4 0.3 mul.74
  43.7 1.1 %fusion.7 = bf16[8,32,128]{2,0,1:T(8,128)(2,1)S(1)} fusion(f32[8,32,128]{2,0,1:T(8,128)S(1)} %bitcast_multiply_fusion.1, f32[8,32]{0,1:T(8,128)S(1)} %copy.87, s32[64]{0:T(128)S(1)} %copy-done.3, f32[64,4096]{1,0:T(8,128)S(1)} %reshape.217, f32[8,8,32,128]{3,2,1,0:T(8,128)S(1)} %bitcast.124), kind=kOutput, calls=%fused_computation.15 | convolution fusion | flops 25526784 | bytes 2295040 | tf_op jit(solution)/shard_map/dot_general | solution.py:405
  44.9 0.7 copy.93
  45.5 0.1 copy.95
  45.6 0.1 copy.96
  45.7 0.1 copy.97
  45.8 0.1 copy.98
  45.8 0.1 fusion.9
  46.0 0.1 reshape.225
  46.1 0.1 reshape_reshape.7
  46.2 0.1 reshape.223
  46.3 0.1 reshape_reshape.6
  46.4 0.1 pad.3.clone
  46.4 0.1 maximum_maximum_fusion
  46.5 0.6 concatenate.7.stats_ref
  47.2 1.3 %scatter_custom_fusion = s32[65]{0:T(128)} fusion(s32[64]{0:T(128)S(1)} %fusion.32, s32[64]{0:T(128)S(1)} %iota.26, s32[]{:T(128)} %constant.13.clone.1), kind=kCustom, calls=%fused_computation.71 | custom fusion | bytes 264 | tf_op jit(solution)/shard_map/scatter | solution.py:359
  48.4 49.0 %shard_map.114 = bf16[4,512]{1,0:T(4,128)(2,1)} custom-call(bf16[16,16,128]{2,1,0:T(8,128)(2,1)} %bitcast.126, f32[16,8,128]{2,1,0:T(8,128)} %concatenate.7.stats_ref, bf16[1024,512]{1,0:T(8,128)(2,1)} %w_ref.1), custom_call_target="tpu_custom_call" | custom-call | flops 33554432 | bytes 1310720 | tf_op jit(solution)/shard_map/pallas_call | solution.py:221
  97.5 5.1 %shard_map.115 = bf16[64,2,128,128]{3,2,1,0:T(8,128)(2,1)} custom-call(s32[64]{0:T(128)} %bitcast.140, bf16[64,2,128,128]{3,2,1,0:T(8,128)(2,1)} %bitcast.45.src_hbm), custom_call_target="tpu_custom_call" | custom-call | bytes 8388608 | tf_op jit(solution)/shard_map/pallas_call | solution.py:283
  102.6 0.6 copy.136
  (28 shorter events, 0.2 us)
Async XLA Ops:
  18.5 79.0 %all-to-all-start = ((bf16[16,4,2,128,128]{4,3,2,1,0:T(8,128)(2,1)}), bf16[16,4,2,128,128]{4,3,2,1,0:T(8,128)(2,1)}, u32[]{:S(2)}, u32[]{:S(2)}) async-start(bf16[16,4,2,128,128]{4,3,2,1,0:T(8,128)(2,1)} %bitcast.125), calls=%async_computation | async-start | bytes 8388608 | tf_op jit(solution)/shard_map/all_to_all | solution.py:353
  23.1 4.9 %copy-start.4 = (s32[1,16,4]{1,2,0:T(4,128)S(1)}, s32[1,16,4]{1,2,0:T(4,128)}, u32[]{:S(2)}) copy-start(s32[1,16,4]{1,2,0:T(4,128)} %param.18) | copy-start | bytes 772
  23.1 5.1 %copy-start = (bf16[16,20,128]{2,1,0:T(8,128)(2,1)S(1)}, bf16[16,20,128]{2,1,0:T(8,128)(2,1)}, u32[]{:S(2)}) copy-start(bf16[16,20,128]{2,1,0:T(8,128)(2,1)} %get-tuple-element.7) | copy-start | bytes 245764
  23.1 6.3 %copy-start.1 = (s32[8]{0:T(128)S(1)}, s32[8]{0:T(128)}, u32[]{:S(2)}) copy-start(s32[8]{0:T(128)} %lengths_ref.1) | copy-start | bytes 100
  23.1 6.9 %copy-start.3 = (s32[64]{0:T(128)S(1)}, s32[64]{0:T(128)}, u32[]{:S(2)}) copy-start(s32[64]{0:T(128)} %param.15) | copy-start | bytes 772
  23.1 6.9 %copy-start.5 = (s32[64]{0:T(128)S(1)}, s32[64]{0:T(128)}, u32[]{:S(2)}) copy-start(s32[64]{0:T(128)} %param.16) | copy-start | bytes 772
  97.5 5.2 %copy-start.2 = (bf16[4,512]{1,0:T(4,128)(2,1)S(1)}, bf16[4,512]{1,0:T(4,128)(2,1)}, u32[]{:S(2)}) copy-start(bf16[4,512]{1,0:T(4,128)(2,1)} %shard_map.114) | copy-start | bytes 12292

commit v14 on v13

--- a/solution.py
+++ b/solution.py
@@ -192,8 +192,55 @@
     attended = (numerator / denominator).astype(mine.dtype)
     mine[...] = attended
     land_a[me] = attended
-    sent_a = _send_all("seq", n, me, lambda p: mine, land_a, sems.at[2], sems.at[3])
-    _wait_all("seq", n, me, land_a, sems.at[2], sems.at[3])
+    ring = 4
+    z, y = me // ring, me % ring
+    sent_a = []
+    for i in range(1, ring):
+        peer = z * ring + lax.rem(y + i, ring)
+        copy = pltpu.make_async_remote_copy(
+            src_ref=mine,
+            dst_ref=land_a.at[me],
+            send_sem=sems.at[2, peer],
+            recv_sem=sems.at[3, me],
+            device_id={"seq": peer},
+            device_id_type=MESH,
+        )
+        copy.start()
+        sent_a.append(copy)
+    for i in range(1, ring):
+        src = z * ring + lax.rem(y + ring - i, ring)
+        pltpu.make_async_remote_copy(
+            src_ref=mine,
+            dst_ref=land_a.at[src],
+            send_sem=sems.at[2, src],
+            recv_sem=sems.at[3, src],
+            device_id={"seq": src},
+            device_id_type=MESH,
+        ).wait_recv()
+    block = pl.ds(z * ring, ring)
+    for i in range(1, n // ring):
+        peer = lax.rem(z + i, n // ring) * ring + y
+        copy = pltpu.make_async_remote_copy(
+            src_ref=land_a.at[block],
+            dst_ref=land_a.at[block],
+            send_sem=sems.at[8, peer],
+            recv_sem=sems.at[9, me],
+            device_id={"seq": peer},
+            device_id_type=MESH,
+        )
+        copy.start()
+        sent_a.append(copy)
+    for i in range(1, n // ring):
+        zs = lax.rem(z + n // ring - i, n // ring)
+        src = zs * ring + y
+        pltpu.make_async_remote_copy(
+            src_ref=land_a.at[pl.ds(zs * ring, ring)],
+            dst_ref=land_a.at[pl.ds(zs * ring, ring)],
+            send_sem=sems.at[8, src],
+            recv_sem=sems.at[9, src],
+            device_id={"seq": src},
+            device_id_type=MESH,
+        ).wait_recv()
     heads = n // 2
     projected = None
     for g in range(heads):
@@ -230,7 +277,7 @@
             pltpu.VMEM((n, rows, HEAD), jnp.bfloat16),
             pltpu.VMEM((m, per, width), jnp.float32),
             pltpu.VMEM((m, per, width), jnp.float32),
-            pltpu.SemaphoreType.DMA((8, max(n, m))),
+            pltpu.SemaphoreType.DMA((10, max(n, m))),
         ],
         compiler_params=pltpu.CompilerParams(collective_id=1, has_side_effects=True),
         cost_estimate=pl.CostEstimate(

time: 104 us -> 106 us (1.019)
  Pallas kernels: 72 us -> 74.2 us
    pallas_call x1, Pallas kernels: 49 us -> 51.2 us  [attend_exchange(): pl.pallas_call(functools.partial(_attend_kernel, n, m, rows), out_shape=j...]
  transfers between devices with their start and end apart: 1 -> 1, of which waited for: 0 -> 0; matrix products, arithmetic and copies ran while one was open for 24% -> 24% of each run, Pallas kernels for 47% -> 49%
where the time goes in v14:
time: 106 us; the launch traced here: 105 us
  Pallas kernels  74.2 us (70%)
  local copies, waits for them, and re-layouts  12.3 us (12%)
  matrix products  7.13 us (7%)
  other arithmetic  6.28 us (6%)
  starting transfers between devices  4.55 us (4%)
    pallas_call x1, Pallas kernels, attend_exchange(): pl.pallas_call(functools.partial(_attend_kernel, n, m, rows), out_shape=j...  51.2 us
    pallas_call x1, Pallas kernels, qkv_exchange(): pl.pallas_call(functools.partial(_qkv_kernel, n, kv_cache.shape[0]), out_...  17.8 us
    unnamed x15, local copies, waits for them, and re-layouts  5.55 us
    pallas_call x1, Pallas kernels, pick_blocks(): pl.pallas_call(functools.partial(_pick_kernel, limit), out_shape=jax.Shap...  5.15 us
    gather x1, other arithmetic, body(): token_valid = (token_pos < lengths[slot_clip][:, None]) & live_slot[:, None]  4.94 us
    all_to_all x1, starting transfers between devices, body(): lax.all_to_all(outgoing, 'seq', split_axis=0, concat_axis=0, tiled=True)  4.55 us
    dot_general x1, matrix products, body(): jnp.einsum('sptgd,sbtd->stgpb', gathered, cache_view[:, 0], preferred_ele...  2.91 us
    dot_general x1, matrix products, body(): jnp.einsum('stgpb,sbtd->stgpd', weights.astype(jnp.bfloat16), cache_view[...  2.26 us
  transfers between devices with their start and end apart: 1, of which 0 were waited for; matrix products, arithmetic and copies ran while one was open for 24% of the time, Pallas kernels for 49%

profile of v14, /device:TPU:1, one launch (start us, length us, event | category | flops | bytes accessed | tf_op | source)
XLA Modules:
  0.0 105.4 jit_solution(2511236295803586795)
XLA Ops:
  0.6 17.8 %shard_map.113 = (bf16[16,20,128]{2,1,0:T(8,128)(2,1)}, bf16[64,2,128,128]{3,2,1,0:T(8,128)(2,1)}) custom-call(bf16[32,512]{1,0:T(8,128)(2,1)} %x_hbm.1, bf16[512,1280]{1,0:T(8,128)(2,1)} %w_hbm.1, f32[1,128]{1,0:T(1,128)} %constant.11.clone.freq_ref, s32[8]{0:T(128)} %lengths_ref.1, s32[1,4,16]{2,1,0:T(4,128)} %bitcast.139, bf16[64,2,128,128]{3,2,1,0:T(8,128)(2,1)} %kv_hbm.1), custom_call_target="tpu_custom_call" | custom-call | flops 41943040 | bytes 9699328 | tf_op jit(solution)/shard_map/pallas_call | solution.py:134
  18.5 4.5 %all-to-all-start = ((bf16[16,4,2,128,128]{4,3,2,1,0:T(8,128)(2,1)}), bf16[16,4,2,128,128]{4,3,2,1,0:T(8,128)(2,1)}, u32[]{:S(2)}, u32[]{:S(2)}) async-start(bf16[16,4,2,128,128]{4,3,2,1,0:T(8,128)(2,1)} %bitcast.125), calls=%async_computation | async-start | bytes 8388608 | tf_op jit(solution)/shard_map/all_to_all | solution.py:400
  23.1 0.0 copy-start.1
  23.1 0.0 copy-start.3
  23.1 4.8 %copy.132 = bf16[64,2,128,128]{3,2,0,1:T(8,128)(2,1)} copy(bf16[64,2,128,128]{3,2,1,0:T(8,128)(2,1)} %kv_hbm.1) | data formatting | bytes 8388608 | tf_op args[3]
  28.0 0.1 copy.76
  28.0 0.1 reshape.210
  28.2 0.4 fusion.38
  28.7 0.1 fusion.18
  28.8 0.3 convolution_select_fusion
  29.1 0.1 copy.90
  29.2 0.1 copy.85
  29.3 0.1 copy.86
  29.3 0.7 fusion.37
  30.0 4.9 %compare_select_fusion.2 = (s32[64]{0:T(128)S(1)}, s32[64]{0:T(128)S(1)}, s32[64]{0:T(128)S(1)}) fusion(s32[]{:T(128)} %bitcast.2, s32[]{:T(128)} %bitcast.3, s32[]{:T(128)} %bitcast.4, s32[]{:T(128)} %bitcast.5, s32[]{:T(128)} %bitcast.6, s32[]{:T(128)} %bitcast.7, s32[]{:T(128)} %bitcast.8, s32[]{:T(128)} %bitcast.9, s32[64]{0:T(128)S(1)} %copy-done.3, ...), kind=kLoop, calls=%fused_computation.61 | loop fusion | flops 1216 | bytes 1312 | tf_op jit(solution)/shard_map/gather | solution.py:415
  35.0 0.7 gather_fusion
  35.7 0.1 fusion.25
  35.8 2.9 %fusion.39 = (f32[64,8,4]{1,2,0:T(4,128)S(1)}, f32[64,1,8,4,128]{4,2,3,0,1:T(8,128)S(1)}) fusion(bf16[64,4,8,128]{3,2,1,0:T(8,128)(2,1)S(1)} %gather_fusion, bf16[64,2,128,1,128]{4,2,0,3,1:T(8,128)(2,1)} %bitcast.122, pred[64,128]{1,0:T(8,128)(4,1)S(1)} %fusion.25), kind=kOutput, calls=%fused_computation.78 | convolution fusion | flops 67893248 | bytes 3686400 | tf_op jit(solution)/shard_map/sptgd,sbtd->stgpb/dot_general | solution.py:419
  38.7 0.1 copy.79
  38.8 0.1 copy.81
  38.9 0.1 select_reduce_fusion
  39.0 0.1 copy.80
  39.1 0.1 copy.92
  39.2 0.1 copy.87
  39.2 0.8 fusion.14
  40.0 2.3 %fusion = f32[64,8,4,128]{3,2,1,0:T(4,128)S(1)} fusion(bf16[64,2,128,1,128]{4,2,0,3,1:T(8,128)(2,1)} %bitcast.123, bf16[64,8,4,128]{3,1,2,0:T(8,128)(2,1)S(1)} %get-tuple-element.13), kind=kOutput, calls=%fused_computation.5 | convolution fusion | flops 67108864 | bytes 3670016 | tf_op jit(solution)/shard_map/stgpb,sbtd->stgpd/dot_general | solution.py:430
  42.3 0.4 reshape.217
  42.7 0.6 gather_fusion.1
  43.3 0.1 bitcast_multiply_fusion.1
  43.4 0.3 mul.74
  43.7 1.1 %fusion.7 = bf16[8,32,128]{2,0,1:T(8,128)(2,1)S(1)} fusion(f32[8,32,128]{2,0,1:T(8,128)S(1)} %bitcast_multiply_fusion.1, f32[8,32]{0,1:T(8,128)S(1)} %copy.87, s32[64]{0:T(128)S(1)} %copy-done.3, f32[64,4096]{1,0:T(8,128)S(1)} %reshape.217, f32[8,8,32,128]{3,2,1,0:T(8,128)S(1)} %bitcast.124), kind=kOutput, calls=%fused_computation.15 | convolution fusion | flops 25526784 | bytes 2295040 | tf_op jit(solution)/shard_map/dot_general | solution.py:452
  44.9 0.7 copy.93
  45.5 0.1 copy.95
  45.6 0.1 copy.96
  45.7 0.1 copy.97
  45.8 0.1 copy.98
  45.8 0.1 fusion.9
  46.0 0.1 reshape.225
  46.1 0.1 reshape_reshape.7
  46.2 0.1 reshape.223
  46.3 0.1 reshape_reshape.6
  46.4 0.1 pad.3.clone
  46.4 0.1 maximum_maximum_fusion
  46.5 0.6 concatenate.7.stats_ref
  47.2 1.3 %scatter_custom_fusion = s32[65]{0:T(128)} fusion(s32[64]{0:T(128)S(1)} %fusion.32, s32[64]{0:T(128)S(1)} %iota.26, s32[]{:T(128)} %constant.13.clone.1), kind=kCustom, calls=%fused_computation.71 | custom fusion | bytes 264 | tf_op jit(solution)/shard_map/scatter | solution.py:406
  48.4 51.2 %shard_map.114 = bf16[4,512]{1,0:T(4,128)(2,1)} custom-call(bf16[16,16,128]{2,1,0:T(8,128)(2,1)} %bitcast.126, f32[16,8,128]{2,1,0:T(8,128)} %concatenate.7.stats_ref, bf16[1024,512]{1,0:T(8,128)(2,1)} %w_ref.1), custom_call_target="tpu_custom_call" | custom-call | flops 33554432 | bytes 1310720 | tf_op jit(solution)/shard_map/pallas_call | solution.py:268
  99.7 5.1 %shard_map.115 = bf16[64,2,128,128]{3,2,1,0:T(8,128)(2,1)} custom-call(s32[64]{0:T(128)} %bitcast.140, bf16[64,2,128,128]{3,2,1,0:T(8,128)(2,1)} %bitcast.45.src_hbm), custom_call_target="tpu_custom_call" | custom-call | bytes 8388608 | tf_op jit(solution)/shard_map/pallas_call | solution.py:330
  104.8 0.6 copy.136
  (28 shorter events, 0.2 us)
Async XLA Ops:
  18.5 81.2 %all-to-all-start = ((bf16[16,4,2,128,128]{4,3,2,1,0:T(8,128)(2,1)}), bf16[16,4,2,128,128]{4,3,2,1,0:T(8,128)(2,1)}, u32[]{:S(2)}, u32[]{:S(2)}) async-start(bf16[16,4,2,128,128]{4,3,2,1,0:T(8,128)(2,1)} %bitcast.125), calls=%async_computation | async-start | bytes 8388608 | tf_op jit(solution)/shard_map/all_to_all | solution.py:400
  23.1 4.9 %copy-start.4 = (s32[1,16,4]{1,2,0:T(4,128)S(1)}, s32[1,16,4]{1,2,0:T(4,128)}, u32[]{:S(2)}) copy-start(s32[1,16,4]{1,2,0:T(4,128)} %param.18) | copy-start | bytes 772
  23.1 5.1 %copy-start = (bf16[16,20,128]{2,1,0:T(8,128)(2,1)S(1)}, bf16[16,20,128]{2,1,0:T(8,128)(2,1)}, u32[]{:S(2)}) copy-start(bf16[16,20,128]{2,1,0:T(8,128)(2,1)} %get-tuple-element.7) | copy-start | bytes 245764
  23.1 6.3 %copy-start.1 = (s32[8]{0:T(128)S(1)}, s32[8]{0:T(128)}, u32[]{:S(2)}) copy-start(s32[8]{0:T(128)} %lengths_ref.1) | copy-start | bytes 100
  23.1 6.9 %copy-start.3 = (s32[64]{0:T(128)S(1)}, s32[64]{0:T(128)}, u32[]{:S(2)}) copy-start(s32[64]{0:T(128)} %param.15) | copy-start | bytes 772
  23.1 6.9 %copy-start.5 = (s32[64]{0:T(128)S(1)}, s32[64]{0:T(128)}, u32[]{:S(2)}) copy-start(s32[64]{0:T(128)} %param.16) | copy-start | bytes 772
  99.7 5.2 %copy-start.2 = (bf16[4,512]{1,0:T(4,128)(2,1)S(1)}, bf16[4,512]{1,0:T(4,128)(2,1)}, u32[]{:S(2)}) copy-start(bf16[4,512]{1,0:T(4,128)(2,1)} %shard_map.114) | copy-start | bytes 12292

commit v15 on v13

--- a/solution.py
+++ b/solution.py
@@ -69,8 +69,6 @@
     ]
     for load in loads:
         load.start()
-    kv_in = pltpu.make_async_copy(kv_hbm, kv_vmem, local_sems.at[0])
-    kv_in.start()
     barrier = pltpu.get_barrier_semaphore()
     for i in range(1, n):
         pl.semaphore_signal(
@@ -78,6 +76,8 @@
         )
     for load in loads:
         load.wait()
+    kv_in = pltpu.make_async_copy(kv_hbm, kv_vmem, local_sems.at[0])
+    kv_in.start()
     product = jnp.dot(x_vmem[...], w_vmem[...], preferred_element_type=jnp.float32)
     groups = product.shape[1] // HEAD
     per = part_ref.shape[1] // groups

time: 104 us -> 104 us (level)
  no operation moved by 1% of the time
where the time goes in v15:
time: 104 us; the launch traced here: 103 us
  Pallas kernels  72.1 us (69%)
  local copies, waits for them, and re-layouts  12.3 us (12%)
  matrix products  7.13 us (7%)
  other arithmetic  6.28 us (6%)
  starting transfers between devices  4.55 us (4%)
    pallas_call x1, Pallas kernels, attend_exchange(): pl.pallas_call(functools.partial(_attend_kernel, n, m, rows), out_shape=j...  49 us
    pallas_call x1, Pallas kernels, qkv_exchange(): pl.pallas_call(functools.partial(_qkv_kernel, n, kv_cache.shape[0]), out_...  17.8 us
    unnamed x15, local copies, waits for them, and re-layouts  5.55 us
    pallas_call x1, Pallas kernels, pick_blocks(): pl.pallas_call(functools.partial(_pick_kernel, limit), out_shape=jax.Shap...  5.21 us
    gather x1, other arithmetic, body(): token_valid = (token_pos < lengths[slot_clip][:, None]) & live_slot[:, None]  4.94 us
    all_to_all x1, starting transfers between devices, body(): lax.all_to_all(outgoing, 'seq', split_axis=0, concat_axis=0, tiled=True)  4.55 us
    dot_general x1, matrix products, body(): jnp.einsum('sptgd,sbtd->stgpb', gathered, cache_view[:, 0], preferred_ele...  2.91 us
    dot_general x1, matrix products, body(): jnp.einsum('stgpb,sbtd->stgpd', weights.astype(jnp.bfloat16), cache_view[...  2.26 us
  transfers between devices with their start and end apart: 1, of which 0 were waited for; matrix products, arithmetic and copies ran while one was open for 24% of the time, Pallas kernels for 47%

profile of v15, /device:TPU:1, one launch (start us, length us, event | category | flops | bytes accessed | tf_op | source)
XLA Modules:
  0.0 103.3 jit_solution(16647331360066617824)
XLA Ops:
  0.6 17.8 %shard_map.113 = (bf16[16,20,128]{2,1,0:T(8,128)(2,1)}, bf16[64,2,128,128]{3,2,1,0:T(8,128)(2,1)}) custom-call(bf16[32,512]{1,0:T(8,128)(2,1)} %x_hbm.1, bf16[512,1280]{1,0:T(8,128)(2,1)} %w_hbm.1, f32[1,128]{1,0:T(1,128)} %constant.11.clone.freq_ref, s32[8]{0:T(128)} %lengths_ref.1, s32[1,4,16]{2,1,0:T(4,128)} %bitcast.139, bf16[64,2,128,128]{3,2,1,0:T(8,128)(2,1)} %kv_hbm.1), custom_call_target="tpu_custom_call" | custom-call | flops 41943040 | bytes 9699328 | tf_op jit(solution)/shard_map/pallas_call | solution.py:134
  18.5 4.5 %all-to-all-start = ((bf16[16,4,2,128,128]{4,3,2,1,0:T(8,128)(2,1)}), bf16[16,4,2,128,128]{4,3,2,1,0:T(8,128)(2,1)}, u32[]{:S(2)}, u32[]{:S(2)}) async-start(bf16[16,4,2,128,128]{4,3,2,1,0:T(8,128)(2,1)} %bitcast.125), calls=%async_computation | async-start | bytes 8388608 | tf_op jit(solution)/shard_map/all_to_all | solution.py:353
  23.1 0.0 copy-start.1
  23.1 0.0 copy-start.3
  23.1 4.8 %copy.132 = bf16[64,2,128,128]{3,2,0,1:T(8,128)(2,1)} copy(bf16[64,2,128,128]{3,2,1,0:T(8,128)(2,1)} %kv_hbm.1) | data formatting | bytes 8388608 | tf_op args[3]
  28.0 0.1 copy.76
  28.0 0.1 reshape.210
  28.2 0.4 fusion.38
  28.7 0.1 fusion.18
  28.8 0.3 convolution_select_fusion
  29.1 0.1 copy.90
  29.2 0.1 copy.85
  29.3 0.1 copy.86
  29.3 0.7 fusion.37
  30.0 4.9 %compare_select_fusion.2 = (s32[64]{0:T(128)S(1)}, s32[64]{0:T(128)S(1)}, s32[64]{0:T(128)S(1)}) fusion(s32[]{:T(128)} %bitcast.2, s32[]{:T(128)} %bitcast.3, s32[]{:T(128)} %bitcast.4, s32[]{:T(128)} %bitcast.5, s32[]{:T(128)} %bitcast.6, s32[]{:T(128)} %bitcast.7, s32[]{:T(128)} %bitcast.8, s32[]{:T(128)} %bitcast.9, s32[64]{0:T(128)S(1)} %copy-done.3, ...), kind=kLoop, calls=%fused_computation.61 | loop fusion | flops 1216 | bytes 1312 | tf_op jit(solution)/shard_map/gather | solution.py:368
  35.0 0.7 gather_fusion
  35.7 0.1 fusion.25
  35.8 2.9 %fusion.39 = (f32[64,8,4]{1,2,0:T(4,128)S(1)}, f32[64,1,8,4,128]{4,2,3,0,1:T(8,128)S(1)}) fusion(bf16[64,4,8,128]{3,2,1,0:T(8,128)(2,1)S(1)} %gather_fusion, bf16[64,2,128,1,128]{4,2,0,3,1:T(8,128)(2,1)} %bitcast.122, pred[64,128]{1,0:T(8,128)(4,1)S(1)} %fusion.25), kind=kOutput, calls=%fused_computation.78 | convolution fusion | flops 67893248 | bytes 3686400 | tf_op jit(solution)/shard_map/sptgd,sbtd->stgpb/dot_general | solution.py:372
  38.7 0.1 copy.79
  38.8 0.1 copy.81
  38.9 0.1 select_reduce_fusion
  39.0 0.1 copy.80
  39.1 0.1 copy.92
  39.2 0.1 copy.87
  39.2 0.8 fusion.14
  40.0 2.3 %fusion = f32[64,8,4,128]{3,2,1,0:T(4,128)S(1)} fusion(bf16[64,2,128,1,128]{4,2,0,3,1:T(8,128)(2,1)} %bitcast.123, bf16[64,8,4,128]{3,1,2,0:T(8,128)(2,1)S(1)} %get-tuple-element.13), kind=kOutput, calls=%fused_computation.5 | convolution fusion | flops 67108864 | bytes 3670016 | tf_op jit(solution)/shard_map/stgpb,sbtd->stgpd/dot_general | solution.py:383
  42.3 0.4 reshape.217
  42.7 0.6 gather_fusion.1
  43.3 0.1 bitcast_multiply_fusion.1
  43.4 0.3 mul.74
  43.7 1.1 %fusion.7 = bf16[8,32,128]{2,0,1:T(8,128)(2,1)S(1)} fusion(f32[8,32,128]{2,0,1:T(8,128)S(1)} %bitcast_multiply_fusion.1, f32[8,32]{0,1:T(8,128)S(1)} %copy.87, s32[64]{0:T(128)S(1)} %copy-done.3, f32[64,4096]{1,0:T(8,128)S(1)} %reshape.217, f32[8,8,32,128]{3,2,1,0:T(8,128)S(1)} %bitcast.124), kind=kOutput, calls=%fused_computation.15 | convolution fusion | flops 25526784 | bytes 2295040 | tf_op jit(solution)/shard_map/dot_general | solution.py:405
  44.9 0.7 copy.93
  45.5 0.1 copy.95
  45.6 0.1 copy.96
  45.7 0.1 copy.97
  45.8 0.1 copy.98
  45.8 0.1 fusion.9
  46.0 0.1 reshape.225
  46.1 0.1 reshape_reshape.7
  46.2 0.1 reshape.223
  46.3 0.1 reshape_reshape.6
  46.4 0.1 pad.3.clone
  46.4 0.1 maximum_maximum_fusion
  46.5 0.6 concatenate.7.stats_ref
  47.2 1.3 %scatter_custom_fusion = s32[65]{0:T(128)} fusion(s32[64]{0:T(128)S(1)} %fusion.32, s32[64]{0:T(128)S(1)} %iota.26, s32[]{:T(128)} %constant.13.clone.1), kind=kCustom, calls=%fused_computation.71 | custom fusion | bytes 264 | tf_op jit(solution)/shard_map/scatter | solution.py:359
  48.4 49.0 %shard_map.114 = bf16[4,512]{1,0:T(4,128)(2,1)} custom-call(bf16[16,16,128]{2,1,0:T(8,128)(2,1)} %bitcast.126, f32[16,8,128]{2,1,0:T(8,128)} %concatenate.7.stats_ref, bf16[1024,512]{1,0:T(8,128)(2,1)} %w_ref.1), custom_call_target="tpu_custom_call" | custom-call | flops 33554432 | bytes 1310720 | tf_op jit(solution)/shard_map/pallas_call | solution.py:221
  97.5 5.2 %shard_map.115 = bf16[64,2,128,128]{3,2,1,0:T(8,128)(2,1)} custom-call(s32[64]{0:T(128)} %bitcast.140, bf16[64,2,128,128]{3,2,1,0:T(8,128)(2,1)} %bitcast.45.src_hbm), custom_call_target="tpu_custom_call" | custom-call | bytes 8388608 | tf_op jit(solution)/shard_map/pallas_call | solution.py:283
  102.7 0.6 copy.136
  (28 shorter events, 0.2 us)
Async XLA Ops:
  18.5 79.0 %all-to-all-start = ((bf16[16,4,2,128,128]{4,3,2,1,0:T(8,128)(2,1)}), bf16[16,4,2,128,128]{4,3,2,1,0:T(8,128)(2,1)}, u32[]{:S(2)}, u32[]{:S(2)}) async-start(bf16[16,4,2,128,128]{4,3,2,1,0:T(8,128)(2,1)} %bitcast.125), calls=%async_computation | async-start | bytes 8388608 | tf_op jit(solution)/shard_map/all_to_all | solution.py:353
  23.1 4.9 %copy-start.4 = (s32[1,16,4]{1,2,0:T(4,128)S(1)}, s32[1,16,4]{1,2,0:T(4,128)}, u32[]{:S(2)}) copy-start(s32[1,16,4]{1,2,0:T(4,128)} %param.18) | copy-start | bytes 772
  23.1 5.1 %copy-start = (bf16[16,20,128]{2,1,0:T(8,128)(2,1)S(1)}, bf16[16,20,128]{2,1,0:T(8,128)(2,1)}, u32[]{:S(2)}) copy-start(bf16[16,20,128]{2,1,0:T(8,128)(2,1)} %get-tuple-element.7) | copy-start | bytes 245764
  23.1 6.3 %copy-start.1 = (s32[8]{0:T(128)S(1)}, s32[8]{0:T(128)}, u32[]{:S(2)}) copy-start(s32[8]{0:T(128)} %lengths_ref.1) | copy-start | bytes 100
  23.1 6.9 %copy-start.3 = (s32[64]{0:T(128)S(1)}, s32[64]{0:T(128)}, u32[]{:S(2)}) copy-start(s32[64]{0:T(128)} %param.15) | copy-start | bytes 772
  23.1 6.9 %copy-start.5 = (s32[64]{0:T(128)S(1)}, s32[64]{0:T(128)}, u32[]{:S(2)}) copy-start(s32[64]{0:T(128)} %param.16) | copy-start | bytes 772
  97.5 5.2 %copy-start.2 = (bf16[4,512]{1,0:T(4,128)(2,1)S(1)}, bf16[4,512]{1,0:T(4,128)(2,1)}, u32[]{:S(2)}) copy-start(bf16[4,512]{1,0:T(4,128)(2,1)} %shard_map.114) | copy-start | bytes 12292
